TPU v7x, 32 devices: a whole 2x2x4 slice. The times are simulated.
32 devices in a mesh: seq: 8 (over z, x), batch: 4 (over y, core).
Axes of the slice: x: 2, y: 2, z: 4, core: 2. Of those that a mesh axis runs over, the one named last changes fastest.
Arguments:
- inputs: float32 [4, 1024, 768], P('batch', 'seq'), may hold values from -6 to 6
- norm_gain: float32 [768], replicated, may hold values from 0.5 to 1.5
- input_projection_weight: float32 [768, 3072], replicated, may hold values from -0.21875 to 0.21875
- conv_weight: float32 [4, 1536], replicated, may hold values from -3 to 3
- conv_bias: float32 [1536], replicated, may hold values from -3 to 3
- x_proj: float32 [1536, 80], replicated, may hold values from -0.15625 to 0.15625
- step_proj: float32 [48, 1536], replicated, may hold values from -0.875 to 0.875
- step_bias: float32 [1536], replicated, may hold values from -3 to -1
- decay_code: int32 [1536], replicated, may hold values from 0 to 9
- decay_log: float32 [1536, 16], replicated, may hold values from -5 to -1.5
- skip_gain: float32 [1536], replicated, may hold values from 0.5 to 1.5
- output_projection_weight: float32 [1536, 768], replicated, may hold values from -0.15625 to 0.15625
- cotangent: float32 [4, 1024, 768], P('batch', 'seq'), may hold values from -6 to 6
Outputs:
- block_out: float32 [4, 1024, 768], P('batch', 'seq')
- input_grad: float32 [4, 1024, 768], P('batch', 'seq')
- norm_gain_grad: float32 [768], replicated
- in_proj_grad: float32 [768, 3072], replicated
- conv_weight_grad: float32 [4, 1536], replicated
- conv_bias_grad: float32 [1536], replicated
- x_proj_grad: float32 [1536, 80], replicated
- step_proj_grad: float32 [48, 1536], replicated
- step_bias_grad: float32 [1536], replicated
- decay_log_grad: float32 [1536, 16], replicated
- skip_gain_grad: float32 [1536], replicated
- out_proj_grad: float32 [1536, 768], replicated
All inputs are finite; a program needn't handle non-finite values.
Results may differ from a plain program's by a relative error of at most 0.0003.
Values sent between devices are 32-bit elements; how exact they have to be, the bound alone decides.
A program may use at most 128 MiB of HBM per device.

v0:
```python
from functools import partial

import jax
import jax.numpy as jnp
from jax import lax
from jax.sharding import PartitionSpec as P

QB = 32


MATMUL_ACCURACY = lax.Precision.HIGHEST
EPSILON = 1e-05


def shifted(x, axis, by):
    length = lax.axis_size(axis)
    pairs = [(i, i + by) for i in range(length) if 0 <= i + by < length]
    return lax.ppermute(x, axis, pairs)


def prefix(value, axis, join, neutral, backward):
    count, mine = (lax.axis_size(axis), lax.axis_index(axis))
    pieces = jax.tree.map(lambda part: lax.all_gather(part, axis), value)
    if backward:
        pieces = jax.tree.map(lambda part: part[::-1], pieces)
        mine = count - 1 - mine
    subtotal = jax.tree.map(
        lambda part, zero: jnp.full_like(part, 0) + jnp.asarray(zero, part.dtype), value, neutral
    )

    def turn(position, subtotal):
        longer = join(subtotal, jax.tree.map(lambda part: part[position], pieces))
        return jax.tree.map(lambda new, old: jnp.where(position < mine, new, old), longer, subtotal)

    return lax.fori_loop(0, count - 1, turn, subtotal)


def matmul(left, right):
    return jnp.dot(left, right, precision=MATMUL_ACCURACY, preferred_element_type=jnp.float32)


def silu_grad(value):
    sigma = jax.nn.sigmoid(value)
    return sigma * (1.0 + value * (1.0 - sigma))


def pair_combine(first, second):
    return (first[0] * second[0], first[1] * second[0] + second[1])


def block_states(factor, source, start):
    cumulative_decay_factor, cum_source = lax.associative_scan(
        pair_combine, (factor, source), axis=0
    )
    return cum_source + cumulative_decay_factor * start[None]


def join_carry(negative_decay_rate, earlier, later):
    return (
        earlier[0] + later[0],
        earlier[1] * jnp.exp(negative_decay_rate[None] * later[0][:, None, :]) + later[1],
    )


def adjoint(factor, values, carry):
    alpha = jnp.concatenate([factor[1:], jnp.ones_like(factor[:1])], axis=0)
    return block_states(alpha[::-1], values[::-1], carry)[::-1]


def shards(
    inputs,
    norm_gain,
    input_projection_weight,
    conv_weight,
    conv_bias,
    x_proj,
    step_proj,
    step_bias,
    decay_code,
    decay_log,
    skip_gain,
    output_projection_weight,
    cotangent,
):
    seqs, group, width = inputs.shape
    inner = input_projection_weight.shape[1] // 2
    rank = step_proj.shape[0]
    states = decay_log.shape[1]
    taps = conv_weight.shape[0]
    blocks = group // QB
    rows = seqs * group

    def to_blocks(value):
        cols = value.shape[-1]
        return jnp.swapaxes(value.reshape(seqs, group, cols), 0, 1).reshape(blocks, QB, seqs, cols)

    def from_blocks(value):
        cols = value.shape[-1]
        return jnp.swapaxes(value.reshape(group, seqs, cols), 0, 1).reshape(rows, cols)

    def unpack(packed_blk):
        step_blk = packed_blk[..., :inner]
        mixed_blk = packed_blk[..., inner : 2 * inner]
        b_blk = packed_blk[..., 2 * inner : 2 * inner + states]
        c_blk = packed_blk[..., 2 * inner + states :]
        return (step_blk, mixed_blk, b_blk, c_blk)

    flat_in = inputs.reshape(rows, width)
    rms = lax.rsqrt(jnp.mean(flat_in * flat_in, axis=1, keepdims=True) + EPSILON)
    normalized_input = flat_in * rms * norm_gain
    mixer_and_gate = matmul(normalized_input, input_projection_weight)
    hidden_x = mixer_and_gate[:, :inner].reshape(seqs, group, inner)
    gate_z = mixer_and_gate[:, inner:]
    rim = shifted(hidden_x[:, group - taps + 1 :], "seq", 1)
    padded = jnp.concatenate([rim, hidden_x], axis=1)
    conv = conv_bias + conv_weight[0] * padded[:, 0:group]
    for k in range(1, taps):
        conv = conv + conv_weight[k] * padded[:, k : k + group]
    conv = conv.reshape(rows, inner)
    mixed = jax.nn.silu(conv)
    proj = matmul(mixed, x_proj)
    low_rank = proj[:, :rank]
    pre = matmul(low_rank, step_proj) + step_bias - 0.5 * decay_code.astype(jnp.float32)
    step = jax.nn.softplus(pre)
    negative_decay_rate = -jnp.exp(decay_log).T
    packed_blocks = to_blocks(jnp.concatenate([step, mixed, proj[:, rank:]], axis=1))
    zero_state = jnp.zeros((seqs, states, inner), jnp.float32)
    zero_sum = jnp.zeros((seqs, inner), jnp.float32)

    def terms(step_blk, mixed_blk, b_blk):
        factor = jnp.exp(step_blk[:, :, None, :] * negative_decay_rate)
        source = (step_blk * mixed_blk)[:, :, None, :] * b_blk[:, :, :, None]
        return (factor, source)

    def local_block(state, packed_blk):
        step_blk, mixed_blk, b_blk, c_blk = unpack(packed_blk)
        factor, source = terms(step_blk, mixed_blk, b_blk)
        held = block_states(factor, source, state)
        output = jnp.sum(held * c_blk[:, :, :, None], axis=2)
        return (held[-1], (output, state))

    end_state, (local_out, local_starts) = lax.scan(local_block, zero_state, packed_blocks)
    group_sum = jnp.sum(step.reshape(seqs, group, inner), axis=1)
    combine = partial(join_carry, negative_decay_rate)
    identity = (jnp.zeros_like(group_sum), zero_state)
    start_state = prefix((group_sum, end_state), "seq", combine, identity, False)[1]

    def shift_in(total, data):
        packed_blk, out_blk = data
        step_blk, mixed_blk, b_blk, c_blk = unpack(packed_blk)
        inside = total[None] + jnp.cumsum(step_blk, axis=0)
        decay = jnp.exp(inside[:, :, None, :] * negative_decay_rate)
        output = out_blk + jnp.sum(decay * start_state[None] * c_blk[:, :, :, None], axis=2)
        begin = jnp.exp(total[:, None, :] * negative_decay_rate) * start_state
        return (inside[-1], (output, begin))

    _, (scanned, begins) = lax.scan(shift_in, zero_sum, (packed_blocks, local_out))
    starts = local_starts + begins
    result = from_blocks(scanned) + skip_gain * mixed
    gate_act = jax.nn.silu(gate_z)
    gate_applied_output = result * gate_act
    block_out = (flat_in + matmul(gate_applied_output, output_projection_weight)).reshape(
        seqs, group, width
    )
    flat_cot = cotangent.reshape(rows, width)
    d_gated = matmul(flat_cot, output_projection_weight.T)
    out_grad = matmul(gate_applied_output.T, flat_cot)
    d_result = d_gated * gate_act
    d_gate = d_gated * result * silu_grad(gate_z)
    skip_grad = jnp.sum(d_result * mixed, axis=0)
    dres_blocks = to_blocks(d_result)

    def collect_back(acc, data):
        total, lam_in = acc
        packed_blk, dres_blk = data
        step_blk, mixed_blk, b_blk, c_blk = unpack(packed_blk)
        inside = total[None] + jnp.cumsum(step_blk, axis=0)
        decay = jnp.exp(inside[:, :, None, :] * negative_decay_rate)
        lam_in = lam_in + jnp.sum(decay * c_blk[:, :, :, None] * dres_blk[:, :, None, :], axis=0)
        return ((inside[-1], lam_in), None)

    (_, later_in), _ = lax.scan(collect_back, (zero_sum, zero_state), (packed_blocks, dres_blocks))
    after_state = prefix((group_sum, later_in), "seq", combine, identity, True)[1]

    def full_back(carry, data):
        lam_next, rate_acc = carry
        packed_blk, dres_blk, start = data
        step_blk, mixed_blk, b_blk, c_blk = unpack(packed_blk)
        factor, source = terms(step_blk, mixed_blk, b_blk)
        held = block_states(factor, source, start)
        prior = jnp.concatenate([start[None], held[:-1]], axis=0)
        lam = adjoint(factor, c_blk[:, :, :, None] * dres_blk[:, :, None, :], lam_next)
        c_grad = jnp.sum(held * dres_blk[:, :, None, :], axis=3)
        decayed = lam * prior * factor
        lam_b = jnp.sum(lam * b_blk[:, :, :, None], axis=2)
        step_grad = jnp.sum(decayed * negative_decay_rate, axis=2) + mixed_blk * lam_b
        rate_acc = rate_acc + jnp.sum(decayed * step_blk[:, :, None, :], axis=(0, 1))
        mixed_scan = step_blk * lam_b
        b_grad = jnp.sum(lam * (step_blk * mixed_blk)[:, :, None, :], axis=3)
        joined = jnp.concatenate([step_grad, mixed_scan, b_grad, c_grad], axis=-1)
        return ((factor[0] * lam[0], rate_acc), joined)

    rate_zero = jnp.zeros((states, inner), jnp.float32)
    (_, rate_sum), back_blocks = lax.scan(
        full_back, (after_state, rate_zero), (packed_blocks, dres_blocks, starts), reverse=True
    )
    back_rows = from_blocks(back_blocks)
    step_grad = back_rows[:, :inner]
    mixed_scan = back_rows[:, inner : 2 * inner]
    b_grad = back_rows[:, 2 * inner : 2 * inner + states]
    c_grad = back_rows[:, 2 * inner + states :]
    decay_grad = (rate_sum * negative_decay_rate).T
    pre_grad = step_grad * jax.nn.sigmoid(pre)
    bias_grad = jnp.sum(pre_grad, axis=0)
    step_proj_grad = matmul(low_rank.T, pre_grad)
    proj_grad = jnp.concatenate([matmul(pre_grad, step_proj.T), b_grad, c_grad], axis=1)
    x_proj_grad = matmul(mixed.T, proj_grad)
    mixed_grad = mixed_scan + d_result * skip_gain + matmul(proj_grad, x_proj.T)
    conv_grad = (mixed_grad * silu_grad(conv)).reshape(seqs, group, inner)
    tap_grads = jnp.stack(
        [jnp.sum(conv_grad * padded[:, k : k + group], axis=(0, 1)) for k in range(taps)]
    )
    conv_bias_grad = jnp.sum(conv_grad, axis=(0, 1))
    spread = jnp.zeros((seqs, group + taps - 1, inner), jnp.float32)
    for k in range(taps):
        spread = spread.at[:, k : k + group].add(conv_weight[k] * conv_grad)
    back_rim = shifted(spread[:, : taps - 1], "seq", -1)
    x_grad = spread[:, taps - 1 :].at[:, group - taps + 1 :].add(back_rim)
    both_grad = jnp.concatenate([x_grad.reshape(rows, inner), d_gate], axis=1)
    in_grad = matmul(normalized_input.T, both_grad)
    normed_grad = matmul(both_grad, input_projection_weight.T)
    gain_grad = jnp.sum(normed_grad * flat_in * rms, axis=0)
    weighted = normed_grad * norm_gain
    input_grad = (
        rms * weighted
        - rms * rms * rms * flat_in * jnp.mean(weighted * flat_in, axis=1, keepdims=True)
        + flat_cot
    )
    input_grad = input_grad.reshape(seqs, group, width)
    summed_all = lax.psum(
        (
            gain_grad,
            in_grad,
            tap_grads,
            conv_bias_grad,
            x_proj_grad,
            step_proj_grad,
            bias_grad,
            decay_grad,
            skip_grad,
            out_grad,
        ),
        ("seq", "batch"),
    )
    summed = summed_all[:8]
    skip_sum = summed_all[8]
    out_sum = summed_all[9]
    return (
        block_out,
        input_grad,
        summed[0],
        summed[1],
        summed[2],
        summed[3],
        summed[4],
        summed[5],
        summed[6],
        summed[7],
        skip_sum,
        out_sum,
    )


def solution(mesh):
    return jax.shard_map(
        shards,
        mesh=mesh,
        in_specs=(
            P("batch", "seq", None),
            P(),
            P(),
            P(),
            P(),
            P(),
            P(),
            P(),
            P(),
            P(),
            P(),
            P(),
            P("batch", "seq", None),
        ),
        out_specs=(
            P("batch", "seq", None),
            P("batch", "seq", None),
            P(),
            P(),
            P(),
            P(),
            P(),
            P(),
            P(),
            P(),
            P(),
            P(),
        ),
        check_vma=False,
    )
```

profile of v0, /device:TPU:1, one launch (start us, length us, event | category | flops | bytes accessed | tf_op | source)
XLA Modules:
  0.0 2101.0 jit_solution(8007326374587562995)
XLA Ops:
  9.0 7.8 fusion.71
  22.0 10.2 multiply_reduce_fusion.8
  36.4 26.5 %all-gather.3 = f32[8,1,1536]{2,1,0:T(1,128)S(1)} all-gather(f32[1,1,1536]{2,1,0:T(1,128)S(1)} %reshape.758), channel_id=2, replica_groups=mesh['seq'=8,'batch'=4] {'seq'}, dimensions={0}, use_global_device_ids=true | all-gather | bytes 55296 | tf_op jit(solution)/shard_map/all_gather | solution.py:23
  66.8 414.5 %while.93 = (s32[]{:T(128)}, f32[1,16,1536]{2,1,0:T(8,128)}, f32[4,32,1,1536]{3,2,1,0:T(1,128)}, f32[4,1,16,1536]{3,2,1,0:T(8,128)}, f32[4,32,1,3104]{3,2,1,0:T(...) while((s32[]{:T(128)}, f32[1,16,1536]{2,1,0:T(8,128)}, f32[4,32,1,1536]{3,2,1,0:T(1,128)}, ...), condition=%wide.region_3.4_spmd, body=%wide.region_1.3_spmd.sunk | while | flops 14721026 | bytes 223114064 | solution.py:142
  126.7 10.9 pad.889
  144.4 10.9 pad.890
  230.3 10.9 pad.889
  248.0 10.9 pad.890
  333.9 10.9 pad.889
  351.7 10.9 pad.890
  437.5 10.9 pad.889
  455.3 10.9 pad.890
  481.3 10.9 while.96
  492.2 26.8 %all-gather.2 = f32[8,16,1536]{2,1,0:T(8,128)S(1)} all-gather(f32[1,16,1536]{2,1,0:T(8,128)} %get-tuple-element.564), channel_id=4, replica_groups=mesh['seq'=8,'batch'=4] {'seq'}, dimensions={0}, use_global_device_ids=true | all-gather | bytes 884736 | tf_op jit(solution)/shard_map/all_gather | solution.py:23
  519.9 11.9 while.97
  531.9 28.0 %all-gather.1 = f32[8,16,1536]{2,1,0:T(8,128)} all-gather(f32[1,16,1536]{2,1,0:T(8,128)} %get-tuple-element.561), channel_id=3, replica_groups=mesh['seq'=8,'batch'=4] {'seq'}, dimensions={0}, use_global_device_ids=true | all-gather | bytes 884736 | tf_op jit(solution)/shard_map/all_gather | solution.py:23
  559.8 11.9 while.95
  571.8 12.4 while.94
  587.3 883.2 %while.98 = (s32[]{:T(128)}, f32[1,16,1536]{2,1,0:T(8,128)S(1)}, f32[16,1536]{1,0:T(8,128)}, f32[4,32,1,3104]{3,1,2,0:T(8,128)}, f32[4,32,1,3104]{3,2,1,0:T(1,12...) while((s32[]{:T(128)}, f32[1,16,1536]{2,1,0:T(8,128)S(1)}, ...), condition=%wide.region_23.24_spmd.clone, body=%wide.region_17.23_spmd.clone.sunk | while | flops 36273152 | bytes 493608896 | solution.py:204
  655.5 10.9 pad.945
  673.3 10.9 pad.946
  684.3 7.0 pad.944
  758.6 10.9 pad.961
  776.4 11.1 pad.962
  787.5 6.8 pad.960
  876.2 10.9 pad.945
  894.0 10.9 pad.946
  904.9 7.0 pad.944
  979.3 10.9 pad.961
  997.1 11.1 pad.962
  1008.1 6.8 pad.960
  1096.8 10.9 pad.945
  1114.6 10.9 pad.946
  1125.6 7.0 pad.944
  1199.9 10.9 pad.961
  1217.7 11.1 pad.962
  1228.8 6.8 pad.960
  1317.5 10.9 pad.945
  1335.3 10.9 pad.946
  1346.2 7.0 pad.944
  1420.6 10.9 pad.961
  1438.4 11.1 pad.962
  1495.2 7.3 fusion.58
  1506.6 11.3 fusion.44
  1524.2 12.0 fusion.69
  1536.3 62.5 %all-reduce.63 = (f32[768]{0:T(1024)}, f32[4,1536]{1,0:T(4,128)}, f32[1536]{0:T(1024)}, f32[1536]{0:T(1024)}, f32[1536]{0:T(1024)}) all-reduce(f32[768]{0:T(1024)S(1)} %get-tuple-element.805, f32[4,1536]{1,0:T(4,128)S(1)} %pad_maximum_fusion.31, ...), channel_id=1, replica_groups=mesh['seq'=8,'batch'=4] {'seq','batch'}, use_global_device_ids=true, to_apply=%region_26.27 | all-reduce | flops 11520 | bytes 92160 | tf_op jit(solution)/shard_map/psum | solution.py:240
  1599.6 481.2 %all-reduce.67.cloned.1.call-done = (f32[768,3072]{1,0:T(8,128)}, f32[1536,80]{0,1:T(8,128)}, f32[48,1536]{1,0:T(8,128)}, f32[1536,16]{0,1:T(8,128)}, f32[1536,768]{1,0:T(8,128)}) async-done(((f32[768,3072]{1,0:T(8,128)}, f32[1536,80]{0,1:T(8,128)}, f32[48,1536]{1,0:T(8,128)}, f32[1536,16]{0,1:T(8,128)}, f32[1536,768]{1,0:T(8,128)}), (f32[768,3072]{1,0:T(8,128)}, f32[1536,80]{0,1:T(8,128)}, ...) | async-done | bytes 15040528 | tf_op jit(solution)/shard_map/psum | solution.py:240
  2080.9 8.8 copy.196
  (1593 shorter events, 1087.0 us)
Async XLA Ops:
  7.2 25.1 %copy-start = (f32[1536,80]{0,1:T(8,128)S(1)}, f32[1536,80]{0,1:T(8,128)}, u32[]{:S(2)}) copy-start(f32[1536,80]{0,1:T(8,128)} %param.40) | copy-start | bytes 1474564
  7.2 2073.7 %all-reduce.67.cloned.1.call-start = ((), (), s32[]{:S(2)}) async-start(), calls=%async_computation | async-start | bytes 30081024 | tf_op jit(solution)/shard_map/psum | solution.py:240
  9.0 7.8 copy-start.125
  16.8 15.4 copy-start.60
  16.9 5.0 collective-permute-start
  21.2 11.0 copy-start.114
  21.2 11.0 copy-start.116
  21.2 11.0 copy-start.118
  21.2 11.0 copy-start.120
  22.0 10.3 copy-start.122
  22.0 11.3 copy-start.132
  32.2 31.3 %copy-start.63 = (f32[128,1536]{1,0:T(8,128)}, f32[128,1536]{1,0:T(8,128)S(1)}, u32[]{:S(2)}) copy-start(f32[128,1536]{1,0:T(8,128)S(1)} %get-tuple-element.907) | copy-start | bytes 2359300
  144.4 10.9 copy-start.29
  162.2 8.2 copy-start.52
  248.0 10.9 copy-start.29
  265.8 8.3 copy-start.52
  351.7 10.9 copy-start.29
  369.5 8.2 copy-start.52
  455.3 10.9 copy-start.29
  473.1 8.2 copy-start.52
  492.2 27.7 %copy-start.69 = (f32[1,16,1536]{2,1,0:T(8,128)S(1)}, f32[1,16,1536]{2,1,0:T(8,128)}, u32[]{:S(2)}) copy-start(f32[1,16,1536]{2,1,0:T(8,128)} %custom-call.2) | copy-start | bytes 294916
  519.9 39.9 %copy-start.87 = (f32[1,16,1536]{2,1,0:T(8,128)S(1)}, f32[1,16,1536]{2,1,0:T(8,128)}, u32[]{:S(2)}) copy-start(f32[1,16,1536]{2,1,0:T(8,128)} %custom-call) | copy-start | bytes 294916
  587.4 7.7 copy-start.36
  673.3 10.9 copy-start.31
  776.4 11.1 copy-start.30
  808.1 7.7 copy-start.36
  894.0 10.9 copy-start.31
  904.9 7.0 copy-start.71
  997.1 11.1 copy-start.30
  1028.7 7.7 copy-start.36
  1114.6 10.9 copy-start.31
  1217.7 11.1 copy-start.30
  1249.4 7.7 copy-start.36
  1335.3 10.9 copy-start.31
  1438.4 11.1 copy-start.30
  1487.7 7.5 copy-start.101
  1493.9 11.1 collective-permute-start.1
  1495.2 7.4 copy-start.90
  1495.2 7.4 copy-start.99
  1495.2 7.4 copy-start.115
  1495.2 7.4 copy-start.123
  1524.2 12.1 copy-start.129
  1524.2 74.6 %copy-start.102 = (f32[1,128,768]{2,1,0:T(8,128)S(1)}, f32[1,128,768]{2,1,0:T(8,128)}, u32[]{:S(2)}) copy-start(f32[1,128,768]{2,1,0:T(8,128)} %param.47) | copy-start | bytes 1179652
  1524.2 74.6 %copy-start.130 = (f32[128]{0:T(128)S(1)}, f32[128]{0:T(128)}, u32[]{:S(2)}) copy-start(f32[128]{0:T(128)} %get-tuple-element.1005) | copy-start | bytes 1540
  2080.9 10.9 slice-start.1
  2080.9 8.8 copy-start.105
  2080.9 9.5 copy-start.108
  2080.9 10.9 slice-start.2
  (340 other events, 877.7 us)
Sparse Core Ops, SparseCore 0:
  1518.0 562.7 all-reduce.66
where the time goes:
time: 2130 us; the launch traced here: 2100 us
  local copies, waits for them, and re-layouts  1010 us (47%)
  waiting for transfers between devices  482 us (23%)
  other arithmetic  379 us (18%)
  blocking collectives  144 us (7%)
  matrix products  65.3 us (3%)
    pad x192, local copies, waits for them, and re-layouts, block_states(): lax.associative_scan(pair_combine, (factor, source), axis=0)  811 us
    psum x1, waiting for transfers between devices, shards(): lax.psum((gain_grad, in_grad, tap_grads, conv_bias_grad, x_proj_grad, ste...  481 us
    add x96, other arithmetic, pair_combine(): return (first[0] * second[0], first[1] * second[0] + second[1])  105 us
    add x96, other arithmetic, block_states(): lax.associative_scan(pair_combine, (factor, source), axis=0)  87.8 us
    all_gather x3, blocking collectives, prefix(): pieces = jax.tree.map(lambda part: lax.all_gather(part, axis), value)  81.3 us
    dot_general x12, matrix products, matmul(): jnp.dot(left, right, precision=MATMUL_ACCURACY, preferred_element_type=jn...  65.3 us
    psum x1, blocking collectives, shards(): lax.psum((gain_grad, in_grad, tap_grads, conv_bias_grad, x_proj_grad, ste...  62.5 us
    slice x84, local copies, waits for them, and re-layouts, block_states(): lax.associative_scan(pair_combine, (factor, source), axis=0)  54.1 us
  transfers between devices with their start and end apart: 3, of which 2 were waited for; matrix products, arithmetic and copies ran while one was open for 1% of the time, Pallas kernels for 0%

commit v1 on v0

v1 whole, which is shorter than its diff:
```python
import functools

import jax
import jax.numpy as jnp
from jax import lax
from jax.experimental import pallas as pl
from jax.experimental.pallas import tpu as pltpu
from jax.sharding import PartitionSpec as P

f32 = jnp.float32
MESH = pl.DeviceIdType.MESH
EPSILON = 1e-05
LOG2E=1.4426950408889634
LN2=0.6931471805599453

def wide(tile, reps):
    return jnp.concatenate([tile]*reps, axis=1) if reps>1 else tile
def rows(block, j, n):
    return jnp.broadcast_to(block[j:j+1], (n, block.shape[1]))

def pass_ac(step_ref, u_ref, d_ref, bb_ref, cc_ref, a2_ref, end_ref, lam_ref, dec_ref, lanes, LB):
    n=a2_ref.shape[0]; reps=LB//128
    a2=a2_ref[:, lanes]
    def chunk(i, carry):
        h,dec,acc=carry
        r=pl.multiple_of(i*8,8)
        s8=step_ref[pl.ds(r,8), lanes]; u8=u_ref[pl.ds(r,8), lanes]; d8=d_ref[pl.ds(r,8), lanes]
        for j in range(8):
            b=wide(bb_ref[r+j],reps); c=wide(cc_ref[r+j],reps)
            a=jnp.exp2(rows(s8,j,n)*a2)
            h=a*h+rows(u8,j,n)*b
            dec=dec*a
            acc=acc+dec*(rows(d8,j,n)*c)
        return h,dec,acc
    z=jnp.zeros((n,LB),f32)
    h,dec,acc=lax.fori_loop(0, step_ref.shape[0]//8, chunk, (z, z+1.0, z))
    end_ref[:, lanes]=h; lam_ref[:, lanes]=acc; dec_ref[:, lanes]=dec

def pass_b(step_ref,u_ref,bb_ref,cc_ref,d_ref,a2_ref,start_ref,y_ref,h_ref,cg_ref,lanes,LB,first):
    n=a2_ref.shape[0]; reps=LB//128
    a2=a2_ref[:, lanes]
    def chunk(i, h):
        r=pl.multiple_of(i*8,8)
        s8=step_ref[pl.ds(r,8), lanes]; u8=u_ref[pl.ds(r,8), lanes]; d8=d_ref[pl.ds(r,8), lanes]
        ys=[]
        for j in range(8):
            b=wide(bb_ref[r+j],reps); c=wide(cc_ref[r+j],reps)
            h_ref[r+j]=h
            a=jnp.exp2(rows(s8,j,n)*a2)
            h=a*h+rows(u8,j,n)*b
            ys.append(jnp.sum(c*h,axis=0,keepdims=True))
            w=rows(d8,j,n)*h
            p=sum(w[:,k*128:(k+1)*128] for k in range(reps))
            cg_ref[r+j]=p if first else cg_ref[r+j]+p
        y_ref[pl.ds(r,8), lanes]=jnp.concatenate(ys,axis=0)
        return h
    lax.fori_loop(0, step_ref.shape[0]//8, chunk, start_ref[:, lanes])

def pass_d(step_ref,u_ref,m_ref,bb_ref,cc_ref,d_ref,a2_ref,after_ref,h_ref,sg_ref,ms_ref,bg_ref,rate_ref,lanes,LB,first):
    n=a2_ref.shape[0]; reps=LB//128; T=step_ref.shape[0]
    a2=a2_ref[:, lanes]
    def chunk(i, carry):
        q,rate=carry
        r=pl.multiple_of(T-8-i*8,8)
        s8=step_ref[pl.ds(r,8), lanes]; u8=u_ref[pl.ds(r,8), lanes]; d8=d_ref[pl.ds(r,8), lanes]
        sg=[None]*8; lb=[None]*8
        for j in reversed(range(8)):
            b=wide(bb_ref[r+j],reps); c=wide(cc_ref[r+j],reps)
            st=rows(s8,j,n)
            a=jnp.exp2(st*a2)
            lam=rows(d8,j,n)*c+q
            q=a*lam
            dec=q*h_ref[r+j]
            lb[j]=jnp.sum(lam*b,axis=0,keepdims=True)
            sg[j]=jnp.sum(dec*a2,axis=0,keepdims=True)
            rate=rate+dec*st
            w=lam*rows(u8,j,n)
            p=sum(w[:,k*128:(k+1)*128] for k in range(reps))
            bg_ref[r+j]=p if first else bg_ref[r+j]+p
        lb8=jnp.concatenate(lb,axis=0); sg8=jnp.concatenate(sg,axis=0)
        sg_ref[pl.ds(r,8), lanes]=LN2*sg8+m_ref[pl.ds(r,8), lanes]*lb8
        ms_ref[pl.ds(r,8), lanes]=s8*lb8
        return q,rate
    q,rate=lax.fori_loop(0, T//8, chunk, (after_ref[:, lanes], jnp.zeros((n,LB),f32)))
    rate_ref[:, lanes]=rate

def bits_of(size): return size.bit_length()-1

def stage_plan(sizes, kind):
    s=[("seq",k) for k in range(bits_of(sizes["seq"]))]
    b=[("batch",k) for k in range(bits_of(sizes["batch"]))]
    core,y=b[0],b[1]; x=s[0]; z=s[1:]
    if kind=="xy": order=[(core,core),(x,y),(y,x)]+[(q,q) for q in z]
    else: order=[(core,core),(z[0],z[0]),(x,y),(y,x)]+[(q,q) for q in z[1:]]
    return order+[(q,q) for q in b[2:]]

class Place:
    def __init__(self):
        self.at={"seq":lax.axis_index("seq"),"batch":lax.axis_index("batch")}
        self.odd=self.at["batch"]%2
    def bit(self, d): return (self.at[d[0]]//(1<<d[1]))%2
    def stage(self, pair):
        to=dict(self.at); first,second=pair
        if first==second:
            v=self.bit(first); to[first[0]]=to[first[0]]+(1-2*v)*(1<<first[1])
        else:
            va,vb=self.bit(first),self.bit(second)
            to[first[0]]=to[first[0]]+(1-self.odd)*(1-2*va)*(1<<first[1])
            to[second[0]]=to[second[0]]+self.odd*(1-2*vb)*(1<<second[1])
            v=(1-self.odd)*va+self.odd*vb
        return (to["seq"],to["batch"]),v

def halvings(rows, stages):
    out=[]
    for _ in range(stages):
        ok=rows%16==0; out.append(ok); rows=rows//2 if ok else rows
    return out

class Chunk:
    def __init__(self, place, plan, acc, out, cols, recv, ss, rs):
        self.acc,self.out,self.cols,self.recv,self.ss,self.rs=acc,out,cols,recv,ss,rs
        rows=acc.shape[0]
        self.half=halvings(rows,len(plan)); self.K=len(plan)
        self.info=[place.stage(p) for p in plan]
        off=0; self.regs=[]; base=0
        for k in range(self.K):
            v=self.info[k][1]
            if self.half[k]:
                rows//=2
                keep=off+v*rows; send=off+(1-v)*rows
                self.regs.append((keep,send,rows,base)); off=keep
            else: self.regs.append((off,off,rows,base))
            base+=rows
        self.final=(off,rows)
        self.steps=[("r",k) for k in range(self.K)]+[("g",k) for k in reversed(range(self.K)) if self.half[k]]
        self.open=None; self.sends=[]; self.at=0
    def region(self, ref, off, rows): return ref.at[pl.ds(pl.multiple_of(off,8),rows), self.cols]
    def advance(self):
        if self.open is not None: self.finish()
        if self.at==self.K:
            off,rows=self.final
            self.move(rows, lambda r: self.put(self.out, off+r, self.acc[pl.ds(pl.multiple_of(off+r,8),8), self.cols]))
        if self.at<len(self.steps):
            kind,k=self.steps[self.at]
            keep,send,rows,base=self.regs[k]
            if kind=="r":
                src=self.region(self.acc,send,rows); dst=self.recv.at[pl.ds(base,rows)]
            else:
                src=dst=self.region(self.out,keep,rows)
            i=self.at
            cp=pltpu.make_async_remote_copy(src_ref=src,dst_ref=dst,send_sem=self.ss.at[i],recv_sem=self.rs.at[i],device_id=self.info[k][0],device_id_type=MESH)
            cp.start(); self.open=(cp,kind,k)
        self.at+=1
    def put(self, ref, off, v): ref[pl.ds(pl.multiple_of(off,8),8), self.cols]=v
    def move(self, rows, f):
        def body(i,_):
            f(i*8); return 0
        lax.fori_loop(0, rows//8, body, 0)
    def finish(self):
        cp,kind,k=self.open; self.open=None
        keep,send,rows,base=self.regs[k]
        cp.wait_recv()
        if kind=="r" and not self.half[k]: cp.wait_send()
        else: self.sends.append(cp)
        if kind=="r":
            def add(r):
                o=keep+r
                self.put(self.acc,o,self.acc[pl.ds(pl.multiple_of(o,8),8),self.cols]+self.recv[pl.ds(base+r,8)])
            self.move(rows, add)
    def done(self): return self.at>len(self.steps)
    def drain(self):
        for cp in self.sends: cp.wait_send()

def greet(place, plans):
    pairs=sorted({q for p in plans for q in p})
    bar=pltpu.get_barrier_semaphore()
    seen=sorted({d for p in pairs for d in p})
    for d in seen:
        to,_=place.stage((d,d))
        pl.semaphore_signal(bar,inc=1,device_id=to,device_id_type=MESH)
    pl.semaphore_wait(bar,len(seen))

def recv_rows(rows, stages):
    tot=0
    for ok in halvings(rows,stages):
        rows=rows//2 if ok else rows
        tot+=rows
    return tot

def ar_kernel(chunks, plans, n, order, *refs):
    ins,outs,refs=refs[:n],refs[n:2*n],refs[2*n:]
    recvs,ss,rs=refs[:len(chunks)],refs[-2],refs[-1]
    place=Place()
    greet(place, plans.values())
    cs=[Chunk(place,plans[kind],ins[o],outs[o],slice(c0,c0+w),recvs[i],ss.at[i],rs.at[i]) for i,(o,c0,w,kind) in enumerate(chunks)]
    t=0
    while not all(c.done() for c in cs):
        for i,c in enumerate(cs):
            if t>=i and not c.done(): c.advance()
        t+=1
    for c in cs: c.drain()

def all_reduce(sizes, arrays, chunks):
    plans={k:stage_plan(sizes,k) for k in {c[3] for c in chunks}}
    K=len(next(iter(plans.values())))
    V=pl.BlockSpec(memory_space=pltpu.VMEM)
    scratch=[pltpu.VMEM((recv_rows(arrays[o].shape[0],K),w),f32) for o,c0,w,kind in chunks]
    scratch+=[pltpu.SemaphoreType.DMA((len(chunks),2*K))]*2
    return pl.pallas_call(functools.partial(ar_kernel,chunks,plans,len(arrays),None),
        in_specs=[V]*len(arrays),out_specs=[V]*len(arrays),out_shape=[jax.ShapeDtypeStruct(a.shape,f32) for a in arrays],
        scratch_shapes=scratch,compiler_params=pltpu.CompilerParams(collective_id=1,has_side_effects=True,vmem_limit_bytes=62<<20))(*arrays)

VMEM = pl.BlockSpec(memory_space=pltpu.VMEM)


def local_call(kernel, outs, args, scratch=()):
    return pl.pallas_call(
        kernel,
        in_specs=[VMEM] * len(args),
        out_specs=[VMEM] * len(outs),
        out_shape=[jax.ShapeDtypeStruct(o, f32) for o in outs],
        scratch_shapes=list(scratch),
        compiler_params=pltpu.CompilerParams(vmem_limit_bytes=56 << 20),
    )(*args)


def lane_blocks(inner, width):
    return [slice(k, k + width) for k in range(0, inner, width)]


def ends_kernel(width, step, u, d, bb, cc, a2, end, lam, dec):
    for lanes in lane_blocks(a2.shape[1], width):
        pass_ac(step, u, d, bb, cc, a2, end, lam, dec, lanes, width)


def scans_kernel(width, step, u, m, d, bb, cc, a2, start, after, y, cg, sg, ms, bg, rate, h):
    for k, lanes in enumerate(lane_blocks(a2.shape[1], width)):
        pass_b(step, u, bb, cc, d, a2, start, y, h, cg, lanes, width, k == 0)
        pass_d(step, u, m, bb, cc, d, a2, after, h, sg, ms, bg, rate, lanes, width, k == 0)


def exchange_kernel(count, x_ref, o_ref, got, back, s1, r1, s2, r2):
    s, b = lax.axis_index("seq"), lax.axis_index("batch")
    across = count // 2
    width = x_ref.shape[2] // across
    bar = pltpu.get_barrier_semaphore()
    peers = [lax.rem(s + i, count) for i in range(1, count)]
    for p in peers:
        pl.semaphore_signal(bar, inc=1, device_id=(p, b), device_id_type=MESH)
    pl.semaphore_wait(bar, count - 1)

    def part(ref, p):
        return ref.at[:, pl.ds(pl.multiple_of(p // across * 8, 8), 8), pl.ds(pl.multiple_of(p % across * width, 128), width)]

    def copies(src, dst, ss, rs):
        out = []
        for i, p in enumerate(peers):
            out.append(pltpu.make_async_remote_copy(
                src_ref=src(p), dst_ref=dst, send_sem=ss.at[i], recv_sem=rs.at[i],
                device_id=(p, b), device_id_type=MESH))
            out[-1].start()
        return out

    first = copies(lambda p: part(x_ref, p), got.at[s], s1, r1)
    got[s] = part(x_ref, s)[...]
    for c in first:
        c.wait_recv()
    zero = jnp.zeros((8, width), f32)
    value = zero
    for q in range(count):
        back[q, 0] = value
        value = got[q, 0] + got[q, 2] * value
    value = zero
    for q in reversed(range(count)):
        back[q, 1] = value
        value = got[q, 1] + got[q, 2] * value
    second = copies(lambda p: back.at[p], part(o_ref, s), s2, r2)
    part(o_ref, s)[...] = back[s]
    for c in second:
        c.wait_recv()
    for c in first + second:
        c.wait_send()


def exchange(count, end, lam, dec):
    n, inner = end.shape
    if count % 2 or n != 16 or inner % (count // 2 * 128):
        return exchange_gathered(end, lam, dec)
    width = inner // (count // 2)
    sems = [pltpu.SemaphoreType.DMA((count - 1,))] * 4
    out = pl.pallas_call(
        functools.partial(exchange_kernel, count),
        in_specs=[VMEM], out_specs=VMEM,
        out_shape=jax.ShapeDtypeStruct((2, n, inner), f32),
        scratch_shapes=[pltpu.VMEM((count, 3, 8, width), f32), pltpu.VMEM((count, 2, 8, width), f32)] + sems,
        compiler_params=pltpu.CompilerParams(collective_id=2, has_side_effects=True),
    )(jnp.stack([end, lam, dec]))
    return out[0], out[1]


def exchange_gathered(end, lam, dec):
    ends, lams, decs = lax.all_gather((end, lam, dec), "seq")
    count, mine = lax.axis_size("seq"), lax.axis_index("seq")

    def ahead(q, value):
        return jnp.where(q < mine, ends[q] + decs[q] * value, value)

    def behind(i, value):
        q = count - 1 - i
        return jnp.where(q > mine, lams[q] + decs[q] * value, value)

    zero = jnp.zeros_like(end)
    return lax.fori_loop(0, count, ahead, zero), lax.fori_loop(0, count, behind, zero)


def shifted(x, axis, by):
    length = lax.axis_size(axis)
    return lax.ppermute(x, axis, [(i, i + by) for i in range(length) if 0 <= i + by < length])


def matmul(left, right, dims=((1,), (0,))):
    return lax.dot_general(left, right, (dims, ((), ())), precision=lax.Precision.HIGH, preferred_element_type=f32)


def silu_grad(value):
    sigma = jax.nn.sigmoid(value)
    return sigma * (1.0 + value * (1.0 - sigma))


def shards(sizes, inputs, norm_gain, w_in, conv_weight, conv_bias, x_proj, step_proj, step_bias, decay_code, decay_log,
           skip_gain, w_out, cotangent):
    seqs, group, width = inputs.shape
    assert seqs == 1
    inner = w_in.shape[1] // 2
    rank, states, taps = step_proj.shape[0], decay_log.shape[1], conv_weight.shape[0]
    x, g = inputs[0], cotangent[0]
    rms = lax.rsqrt(jnp.mean(x * x, axis=1, keepdims=True) + EPSILON)
    normed = x * rms * norm_gain
    both = matmul(normed, w_in)
    hidden, gate = both[:, :inner], both[:, inner:]
    padded = jnp.concatenate([shifted(hidden[group - taps + 1:], "seq", 1), hidden], axis=0)
    conv = conv_bias + sum(conv_weight[k] * padded[k:k + group] for k in range(taps))
    mixed = jax.nn.silu(conv)
    proj = matmul(mixed, x_proj)
    low_rank = proj[:, :rank]
    pre = matmul(low_rank, step_proj) + step_bias - 0.5 * decay_code.astype(f32)
    step = jax.nn.softplus(pre)
    rate = -jnp.exp(decay_log).T
    a2 = rate * LOG2E
    d_gated = matmul(g, w_out, ((1,), (1,)))
    gate_act = jax.nn.silu(gate)
    d_result = d_gated * gate_act
    spread = [jnp.broadcast_to(proj[:, k:k + states, None], (group, states, 128)) for k in (rank, rank + states)]
    u = step * mixed
    end, lam, dec = local_call(functools.partial(ends_kernel, 512), [(states, inner)] * 3, (step, u, d_result, *spread, a2))
    start, after = exchange(sizes["seq"], end, lam, dec)
    token, part, state = (group, inner), (group, states, 128), (states, inner)
    y, cg, step_grad, mixed_scan, bg, rate_sum = local_call(
        functools.partial(scans_kernel, 512), [token, part, token, token, part, state],
        (step, u, mixed, d_result, *spread, a2, start, after), [pltpu.VMEM((group, states, 512), f32)])
    result = y + skip_gain * mixed
    gated = result * gate_act
    block_out = x + matmul(gated, w_out)
    out_grad = matmul(gated, g, ((0,), (0,)))
    d_gate = d_gated * result * silu_grad(gate)
    skip_grad = jnp.sum(d_result * mixed, axis=0)
    pre_grad = step_grad * jax.nn.sigmoid(pre)
    bias_grad = jnp.sum(pre_grad, axis=0)
    step_proj_grad = matmul(low_rank, pre_grad, ((0,), (0,)))
    proj_grad = jnp.concatenate([matmul(pre_grad, step_proj, ((1,), (1,))), jnp.sum(bg, axis=2), jnp.sum(cg, axis=2)], axis=1)
    x_proj_grad_t = matmul(proj_grad, mixed, ((0,), (0,)))
    mixed_grad = mixed_scan + d_result * skip_gain + matmul(proj_grad, x_proj, ((1,), (1,)))
    conv_grad = mixed_grad * silu_grad(conv)
    tap_grads = [jnp.sum(conv_grad * padded[k:k + group], axis=0) for k in range(taps)]
    conv_bias_grad = jnp.sum(conv_grad, axis=0)
    behind = jnp.concatenate([conv_grad, shifted(conv_grad[:taps - 1], "seq", -1)], axis=0)
    x_grad = sum(conv_weight[k] * behind[taps - 1 - k:taps - 1 - k + group] for k in range(taps))
    both_grad = jnp.concatenate([x_grad, d_gate], axis=1)
    in_grad = matmul(normed, both_grad, ((0,), (0,)))
    normed_grad = matmul(both_grad, w_in, ((1,), (1,)))
    gain_grad = jnp.sum(normed_grad * x * rms, axis=0)
    weighted = normed_grad * norm_gain
    input_grad = rms * weighted - rms * rms * rms * x * jnp.mean(weighted * x, axis=1, keepdims=True) + g
    rows = jnp.stack(tap_grads + [conv_bias_grad, bias_grad, skip_grad, jnp.pad(gain_grad, (0, inner - width))])
    small = jnp.concatenate([x_proj_grad_t, step_proj_grad, rate_sum * rate, rows], axis=0)
    cells = small.size
    small = jnp.pad(small.reshape(-1), (0, 256 * 1024 - cells)).reshape(256, 1024)
    chunks = [(0, k, 768, "xy") for k in range(0, 2 * inner, 768)] + [(1, 0, width, "xy"), (2, 0, 1024, "xy")]
    in_sum, out_sum, small = all_reduce(sizes, [in_grad, out_grad, small], chunks)
    small = small.reshape(-1)[:cells].reshape(-1, inner)
    at = [0]

    def take(count):
        at[0] += count
        return small[at[0] - count:at[0]]

    x_proj_sum, step_proj_sum, decay_sum, taps_sum = take(x_proj.shape[1]).T, take(rank), take(states).T, take(taps)
    conv_bias_sum, bias_sum, skip_sum, gain_sum = (take(1)[0] for _ in range(4))
    return (block_out[None], input_grad[None], gain_sum[:width], in_sum, taps_sum, conv_bias_sum, x_proj_sum, step_proj_sum,
            bias_sum, decay_sum, skip_sum, out_sum)


def solution(mesh):
    tokens = P("batch", "seq", None)
    return jax.shard_map(
        functools.partial(shards, dict(mesh.shape)),
        mesh=mesh,
        in_specs=(tokens,) + (P(),) * 11 + (tokens,),
        out_specs=(tokens, tokens) + (P(),) * 10,
        check_vma=False,
    )
```

time: 2130 us -> 306 us (0.14); the launches traced: 2100 us -> 305 us
  local copies, waits for them, and re-layouts: 1010 us -> 31.3 us
  waiting for transfers between devices: 482 us -> 2.65 us
  other arithmetic: 379 us -> 12.5 us
  Pallas kernels: 0 us -> 213 us
  blocking collectives: 144 us -> 0 us
  matrix products: 65.3 us -> 39.3 us
    pad x192 -> x2, local copies, waits for them, and re-layouts: 811 us -> 0.07 us  [the longest x1 0.07 us: shards(): jnp.pad(small.reshape(-1), (0, 256 * 1024 - cells)).reshape(256, 1024)]
    psum x1 -> x0, waiting for transfers between devices: 481 us -> none  [shards(): lax.psum((gain_grad, in_grad, tap_grads, conv_bias_grad, x_proj_grad, ste...]
    add x215 -> x1, other arithmetic: 223 us -> 0.35 us  [shards(): sum((conv_weight[k] * behind[taps - 1 - k:taps - 1 - k + group] for k in...]
    pallas_call x0 -> x4, Pallas kernels: none -> 213 us  [the longest x1 171 us: all_reduce(): pl.pallas_call(functools.partial(ar_kernel, chunks, plans, len(arrays), N...]
    all_gather x3 -> x0, blocking collectives: 81.3 us -> none  [prefix(): pieces = jax.tree.map(lambda part: lax.all_gather(part, axis), value)]
    reduce_sum x23 -> x4, other arithmetic: 70.5 us -> 6.13 us  [the longest x1 1.71 us: shards(): conv_bias_grad = jnp.sum(conv_grad, axis=0)]
    psum x1 -> x0, blocking collectives: 62.5 us -> none  [shards(): lax.psum((gain_grad, in_grad, tap_grads, conv_bias_grad, x_proj_grad, ste...]
    while x669 -> x0, local copies, waits for them, and re-layouts: 50.7 us -> none
  transfers between devices with their start and end apart: 3 -> 2, of which waited for: 2 -> 2; matrix products, arithmetic and copies ran while one was open for 1% -> 0% of each run, Pallas kernels for 0% -> 0%
where the time goes in v1:
time: 306 us; the launch traced here: 305 us
  Pallas kernels  213 us (70%)
  matrix products  39.3 us (13%)
  local copies, waits for them, and re-layouts  31.3 us (10%)
  other arithmetic  12.5 us (4%)
  starting transfers between devices  5.44 us (2%)
    pallas_call x1, Pallas kernels, all_reduce(): pl.pallas_call(functools.partial(ar_kernel, chunks, plans, len(arrays), N...  171 us
    dot_general x12, matrix products, matmul(): lax.dot_general(left, right, (dims, ((), ())), precision=lax.Precision.HI...  39.3 us
    pallas_call x2, Pallas kernels, local_call(): pl.pallas_call(kernel, in_specs=[VMEM] * len(args), out_specs=[VMEM] * le...  25.7 us
    pallas_call x1, Pallas kernels, exchange(): pl.pallas_call(functools.partial(exchange_kernel, count), in_specs=[VMEM]...  16.1 us
    unnamed x74, local copies, waits for them, and re-layouts  12.9 us
    slice x9, local copies, waits for them, and re-layouts, take(): return small[at[0] - count:at[0]]  8.3 us
  transfers between devices with their start and end apart: 2, of which 2 were waited for; matrix products, arithmetic and copies ran while one was open for 0% of the time, Pallas kernels for 0%

profile of v1, /device:TPU:1, one launch (start us, length us, event | category | flops | bytes accessed | tf_op | source)
XLA Modules:
  0.0 305.5 jit_solution(17576378501430675174)
XLA Ops:
  0.7 1.3 fusion.22
  1.9 0.5 multiply_multiply_fusion.1
  2.5 0.5 copy-done.22
  3.0 6.6 %fusion.30 = f32[128,3072]{1,0:T(8,128)S(1)} fusion(f32[768,3072]{1,0:T(8,128)} %param.15, f32[1,128,768]{2,1,0:T(8,128)} %param.13, f32[768]{0:T(1024)} %param.14, f32[128]{0:T(128)S(1)} %get-tuple-element.70), kind=kOutput, calls=%fused_computation.61 | convolution fusion | flops 1812135936 | bytes 11406848 | tf_op jit(solution)/shard_map/dot_general | solution.py:322
  9.6 3.9 %collective-permute-start = (f32[3,1536]{1,0:T(4,128)S(1)}, f32[3,1536]{1,0:T(4,128)S(1)}, u32[]{:S(2)}, u32[]{:S(2)}) collective-permute-start(f32[3,1536]{1,0:T(4,128)S(1)} %slice.147), channel_id=1, source_target_pairs={{0,4},{4,8},{8,12},{12,16},{16,20},{20,24},{24,28},{1,5},{5,9},{9,... | collective-permute-start | bytes 55304 | tf_op jit(solution)/shard_map/ppermute | solution.py:318
  13.6 0.7 bitcast_multiply_fusion.6.a2
  14.6 4.8 %multiply_reduce_fusion = (f32[1536]{0:T(1024)}, f32[128,1536]{1,0:T(8,128)}, f32[128,1536]{1,0:T(8,128)S(1)}, f32[128,1536]{1,0:T(8,128)}, f32[128,1536]{1,0:T(8,128)}) fusion(f32[128,3072]{1,0:T(8,128)S(1)} %fusion.30, f32[128,1536]{1,0:T(8,128)S(1)} %slice.148, f32[1536]{0:T(1024)S(1)} %get-tuple-element.51, f32[3,1536]{1,0:T(4,128)S(1)} %collective-permute-done, ...), kind=kOutput, calls=%fused_computation.30 | convolution fusion | flops 910293504 | bytes 9885696 | tf_op jit(solution)/shard_map/dot_general | solution.py:322
  19.4 0.5 fusion.55
  20.2 2.4 fusion.46
  22.6 1.3 broadcast_in_dim.8.bb
  23.9 1.3 broadcast_in_dim.9.cc
  25.2 7.0 %shard_map.220 = (f32[16,1536]{1,0:T(8,128)}, f32[16,1536]{1,0:T(8,128)}, f32[16,1536]{1,0:T(8,128)}) custom-call(f32[128,1536]{1,0:T(8,128)} %get-tuple-element.64.step, f32[128,1536]{1,0:T(8,128)} %get-tuple-element.63.u, f32[128,1536]{1,0:T(8,128)} %get-tuple-element.54.d, f32[128,16,128]{2,1,0:T(8,128)} %broadcast_in_dim.8.bb, ...), custom_call_target="tpu_custom_call" | custom-call | tf_op jit(solution)/shard_map/pallas_call | solution.py:217
  32.2 1.7 pad_maximum_fusion.5.x_ref
  34.0 16.1 %shard_map.221 = f32[2,16,1536]{2,1,0:T(8,128)} custom-call(f32[3,16,1536]{2,1,0:T(8,128)} %pad_maximum_fusion.5.x_ref), custom_call_target="tpu_custom_call" | custom-call | tf_op jit(solution)/shard_map/pallas_call | solution.py:291
  50.1 1.6 slice_bitcast_fusion
  51.7 18.7 %shard_map.222 = (f32[128,1536]{1,0:T(8,128)}, f32[128,16,128]{2,1,0:T(8,128)}, f32[128,1536]{1,0:T(8,128)}, f32[128,1536]{1,0:T(8,128)}, f32[128,16,128]{2,1,0:T(8,128)}, /*index=5*/f32[16,1536]{1,0:T(8,128)}) custom-call(f32[128,1536]{1,0:T(8,128)} %get-tuple-element.64.step, f32[128,1536]{1,0:T(8,128)} %get-tuple-element.63.u, f32[128,1536]{1,0:T(8,128)} %copy-done.2, ...), custom_call_target="tpu_custom_call" | custom-call | tf_op jit(solution)/shard_map/pallas_call | solution.py:217
  70.4 2.2 fusion.53
  72.6 0.9 copy-done.5
  73.5 0.5 fusion.56
  74.0 1.6 reduce_sum.109
  75.6 1.6 reduce_sum.110
  77.3 0.4 fusion.38
  77.7 2.5 fusion.1
  80.3 1.7 fusion.50
  82.0 4.7 %fusion.4 = f32[1,128,768]{2,1,0:T(8,128)} fusion(f32[1536,768]{1,0:T(8,128)} %param.24, f32[1,128,768]{2,1,0:T(8,128)S(1)} %copy-done.4, f32[128,1536]{1,0:T(8,128)S(1)} %get-tuple-element.62, f32[128,3072]{1,0:T(8,128)S(1)} %fusion.30), kind=kOutput, calls=%fused_computation.9 | convolution fusion | flops 907051008 | bytes 7077888 | tf_op jit(solution)/shard_map/dot_general | solution.py:322
  86.8 4.3 %fusion.17.refs_1_ = f32[1536,768]{1,0:T(8,128)} fusion(f32[1,128,768]{2,1,0:T(8,128)S(1)} %copy-done.10, f32[128,1536]{1,0:T(8,128)S(1)} %get-tuple-element.62, f32[128,3072]{1,0:T(8,128)S(1)} %fusion.30), kind=kOutput, calls=%fused_computation.43 | convolution fusion | flops 906952704 | bytes 6684672 | tf_op jit(solution)/shard_map/dot_general | solution.py:322
  91.1 1.5 collective-permute-start.1
  93.1 2.6 collective-permute-done.1
  95.6 0.4 fusion.9
  96.1 5.8 %fusion.28 = (f32[768]{0:T(1024)S(1)}, f32[128]{0:T(128)S(1)}, f32[128,768]{1,0:T(8,128)}) fusion(f32[1,128,768]{2,1,0:T(8,128)S(1)} %copy-done.4, f32[128]{0:T(128)S(1)} %copy-done.23, f32[768]{0:T(1024)S(1)} %copy-done.17, f32[768,3072]{1,0:T(8,128)S(1)} %bitcast.64, f32[128,1536]{1,0:T(8,128)S(1)} %get-tuple-element.61, f32[128,1536]{1,0:T(8,128)S(1)} %fusion.9), kind=kOutput, calls=%fused_computation.60 | convolution fusion | flops 1812921472 | bytes 11803648 | tf_op jit(solution)/shard_map/dot_general | solution.py:322
  101.9 6.4 %fusion.2.refs_0_ = f32[768,3072]{1,0:T(8,128)} fusion(f32[128,1536]{1,0:T(8,128)S(1)} %get-tuple-element.61, f32[128,1536]{1,0:T(8,128)S(1)} %fusion.9, f32[1,128,768]{2,1,0:T(8,128)S(1)} %copy-done.4, f32[768]{0:T(1024)S(1)} %copy-done.17, f32[128]{0:T(128)S(1)} %copy-done.23), kind=kOutput, calls=%fused_computation.6 | convolution fusion | flops 1812529152 | bytes 11406848 | tf_op jit(solution)/shard_map/dot_general | solution.py:322
  108.8 1.1 reshape.67.refs_2_
  109.9 171.2 %shard_map.223 = (f32[768,3072]{1,0:T(8,128)}, f32[1536,768]{1,0:T(8,128)}, f32[256,1024]{1,0:T(8,128)}) custom-call(f32[768,3072]{1,0:T(8,128)} %fusion.2.refs_0_, f32[1536,768]{1,0:T(8,128)} %fusion.17.refs_1_, f32[256,1024]{1,0:T(8,128)} %reshape.67.refs_2_), custom_call_target="tpu_custom_call" | custom-call | tf_op jit(solution)/shard_map/pallas_call | solution.py:209
  281.2 0.8 slice.136
  282.0 0.9 slice.144
  282.9 1.0 slice.141
  283.9 1.1 slice.139
  285.0 1.3 slice.133
  286.2 1.2 reshape.68
  287.4 1.3 slice_reduce_fusion.7
  288.7 1.6 slice_reduce_fusion
  290.3 0.6 slice.137
  290.9 0.7 slice.145
  291.6 0.8 slice.142
  292.4 0.9 slice.140
  293.3 0.9 fusion.21
  294.2 9.1 %copy.33 = f32[768,3072]{1,0:T(8,128)} copy(f32[768,3072]{1,0:T(8,128)} %get-tuple-element.89) | data formatting | bytes 18874368
  303.3 2.2 copy.34
  (99 shorter events, 1.6 us)
Async XLA Ops:
  0.6 18.8 %copy-start = (f32[1536,80]{0,1:T(8,128)S(1)}, f32[1536,80]{0,1:T(8,128)}, u32[]{:S(2)}) copy-start(f32[1536,80]{0,1:T(8,128)} %param.18) | copy-start | bytes 1474564
  0.7 13.9 %slice-start.3 = ((s8[4718592]{0:T(1024)(128)(4,1)}), s8[4194304]{0:T(1024)(128)(4,1)S(1)}, s32[]{:S(2)}) async-start(s8[4718592]{0:T(1024)(128)(4,1)} %bitcast.65), calls=%async_computation.3 | async-start | bytes 8388608
  2.5 0.5 copy-start.22
  3.0 10.6 %copy-start.26 = (s32[1536]{0:T(1024)S(1)}, s32[1536]{0:T(1024)}, u32[]{:S(2)}) copy-start(s32[1536]{0:T(1024)} %param.21) | copy-start | bytes 18436
  3.0 10.6 %copy-start.16 = (f32[1536,16]{0,1:T(8,128)S(1)}, f32[1536,16]{0,1:T(8,128)}, u32[]{:S(2)}) copy-start(f32[1536,16]{0,1:T(8,128)} %param.22) | copy-start | bytes 294916
  3.0 11.3 %copy-start.20 = (f32[4,1536]{1,0:T(4,128)S(1)}, f32[4,1536]{1,0:T(4,128)}, u32[]{:S(2)}) copy-start(f32[4,1536]{1,0:T(4,128)} %param.16) | copy-start | bytes 73732
  3.0 11.5 %slice-start.4 = ((s8[4718592]{0:T(1024)(128)(4,1)}), s8[524288]{0:T(1024)(128)(4,1)S(1)}, s32[]{:S(2)}) async-start(s8[4718592]{0:T(1024)(128)(4,1)} %bitcast.65), calls=%async_computation.4 | async-start | bytes 1048576
  3.0 11.5 %copy-start.9 = (f32[1,128,768]{2,1,0:T(8,128)S(1)}, f32[1,128,768]{2,1,0:T(8,128)}, u32[]{:S(2)}) copy-start(f32[1,128,768]{2,1,0:T(8,128)} %param.25) | copy-start | bytes 1179652
  3.0 11.5 %copy-start.28 = (f32[1536]{0:T(1024)S(1)}, f32[1536]{0:T(1024)}, u32[]{:S(2)}) copy-start(f32[1536]{0:T(1024)} %param.17) | copy-start | bytes 18436
  9.6 4.9 %collective-permute-start = (f32[3,1536]{1,0:T(4,128)S(1)}, f32[3,1536]{1,0:T(4,128)S(1)}, u32[]{:S(2)}, u32[]{:S(2)}) collective-permute-start(f32[3,1536]{1,0:T(4,128)S(1)} %slice.147), channel_id=1, source_target_pairs={{0,4},{4,8},{8,12},{12,16},{16,20},{20,24},{24,28},{1,5},{5,9},{9,... | collective-permute-start | bytes 55304 | tf_op jit(solution)/shard_map/ppermute | solution.py:318
  14.4 5.0 %copy-start.7 = (f32[128,1536]{1,0:T(8,128)}, f32[128,1536]{1,0:T(8,128)S(1)}, u32[]{:S(2)}) copy-start(f32[128,1536]{1,0:T(8,128)S(1)} %slice.148) | copy-start | bytes 2359300
  14.5 4.9 %copy-start.21 = (f32[3,1536]{1,0:T(4,128)}, f32[3,1536]{1,0:T(4,128)S(1)}, u32[]{:S(2)}) copy-start(f32[3,1536]{1,0:T(4,128)S(1)} %collective-permute-done) | copy-start | bytes 55300
  14.5 5.6 %copy-start.13 = (f32[48,1536]{1,0:T(8,128)S(1)}, f32[48,1536]{1,0:T(8,128)}, u32[]{:S(2)}) copy-start(f32[48,1536]{1,0:T(8,128)} %param.19) | copy-start | bytes 884740
  14.6 5.6 %copy-start.24 = (f32[1536]{0:T(1024)S(1)}, f32[1536]{0:T(1024)}, u32[]{:S(2)}) copy-start(f32[1536]{0:T(1024)} %param.20) | copy-start | bytes 18436
  19.4 12.8 %copy-start.2 = (f32[128,1536]{1,0:T(8,128)}, f32[128,1536]{1,0:T(8,128)S(1)}, u32[]{:S(2)}) copy-start(f32[128,1536]{1,0:T(8,128)S(1)} %get-tuple-element.55.m) | copy-start | bytes 2359300
  51.7 25.5 %copy-start.3 = (f32[128,1536]{1,0:T(8,128)S(1)}, f32[128,1536]{1,0:T(8,128)}, u32[]{:S(2)}) copy-start(f32[128,1536]{1,0:T(8,128)} %copy-done.2) | copy-start | bytes 2359300
  72.6 0.9 copy-start.5
  77.3 3.0 copy-start.8
  77.3 3.0 copy-start.14
  77.3 3.0 copy-start.15
  80.2 1.8 copy-start.4
  80.3 15.7 %slice-start = ((s8[9437184]{0:T(1024)(128)(4,1)}), s8[4194304]{0:T(1024)(128)(4,1)S(1)}, s32[]{:S(2)}) async-start(s8[9437184]{0:T(1024)(128)(4,1)} %bitcast.63), calls=%async_computation | async-start | bytes 8388608
  82.0 4.8 %copy-start.10 = (f32[1,128,768]{2,1,0:T(8,128)S(1)}, f32[1,128,768]{2,1,0:T(8,128)}, u32[]{:S(2)}) copy-start(f32[1,128,768]{2,1,0:T(8,128)} %param.25) | copy-start | bytes 1179652
  82.0 14.0 %slice-start.1 = ((s8[9437184]{0:T(1024)(128)(4,1)}), s8[4194304]{0:T(1024)(128)(4,1)S(1)}, s32[]{:S(2)}) async-start(s8[9437184]{0:T(1024)(128)(4,1)} %bitcast.63), calls=%async_computation.1 | async-start | bytes 8388608
  86.7 5.9 %copy-start.18 = (f32[16,1536]{1,0:T(8,128)S(1)}, f32[16,1536]{1,0:T(8,128)}, u32[]{:S(2)}) copy-start(f32[16,1536]{1,0:T(8,128)} %get-tuple-element.32) | copy-start | bytes 294916
  86.7 5.9 %copy-start.6 = (f32[128,1536]{1,0:T(8,128)S(1)}, f32[128,1536]{1,0:T(8,128)}, u32[]{:S(2)}) copy-start(f32[128,1536]{1,0:T(8,128)} %copy-done.5) | copy-start | bytes 2359300
  86.7 6.2 %copy-start.25 = (f32[1536]{0:T(1024)S(1)}, f32[1536]{0:T(1024)}, u32[]{:S(2)}) copy-start(f32[1536]{0:T(1024)} %get-tuple-element.53) | copy-start | bytes 18436
  86.8 6.2 %copy-start.19 = (f32[1536]{0:T(1024)S(1)}, f32[1536]{0:T(1024)}, u32[]{:S(2)}) copy-start(f32[1536]{0:T(1024)} %get-tuple-element.57) | copy-start | bytes 18436
  86.8 9.3 %slice-start.2 = ((s8[9437184]{0:T(1024)(128)(4,1)}), s8[1048576]{0:T(1024)(128)(4,1)S(1)}, s32[]{:S(2)}) async-start(s8[9437184]{0:T(1024)(128)(4,1)} %bitcast.63), calls=%async_computation.2 | async-start | bytes 2097152
  86.8 9.3 %copy-start.17 = (f32[768]{0:T(1024)S(1)}, f32[768]{0:T(1024)}, u32[]{:S(2)}) copy-start(f32[768]{0:T(1024)} %param.14) | copy-start | bytes 9220
  86.8 9.2 %copy-start.23 = (f32[128]{0:T(128)S(1)}, f32[128]{0:T(128)}, u32[]{:S(2)}) copy-start(f32[128]{0:T(128)} %copy-done.22) | copy-start | bytes 1540
  91.1 4.6 %collective-permute-start.1 = (f32[3,1536]{1,0:T(4,128)S(1)}, f32[3,1536]{1,0:T(4,128)S(1)}, u32[]{:S(2)}, u32[]{:S(2)}) collective-permute-start(f32[3,1536]{1,0:T(4,128)S(1)} %slice.157), channel_id=1, source_target_pairs={{4,0},{8,4},{12,8},{16,12},{20,16},{24,20},{28,24},{5,1},{9,5},{13... | collective-permute-start | bytes 55304 | tf_op jit(solution)/shard_map/ppermute | solution.py:318
  281.1 12.1 %copy-start.11 = (f32[1,128,768]{2,1,0:T(8,128)S(1)}, f32[1,128,768]{2,1,0:T(8,128)}, u32[]{:S(2)}) copy-start(f32[1,128,768]{2,1,0:T(8,128)} %param.25) | copy-start | bytes 1179652
  281.2 12.1 %copy-start.12 = (f32[128,768]{1,0:T(8,128)S(1)}, f32[128,768]{1,0:T(8,128)}, u32[]{:S(2)}) copy-start(f32[128,768]{1,0:T(8,128)} %get-tuple-element.73) | copy-start | bytes 1179652
  281.2 12.1 %copy-start.27 = (f32[128]{0:T(128)S(1)}, f32[128]{0:T(128)}, u32[]{:S(2)}) copy-start(f32[128]{0:T(128)} %get-tuple-element.69) | copy-start | bytes 1540
  293.3 10.0 %slice-start.5 = ((s8[4718592]{0:T(1024)(128)(4,1)}), s8[4194304]{0:T(1024)(128)(4,1)S(1)}, s32[]{:S(2)}) async-start(s8[4718592]{0:T(1024)(128)(4,1)} %bitcast.67), calls=%async_computation.5 | async-start | bytes 8388608
  294.2 9.1 %slice-start.6 = ((s8[4718592]{0:T(1024)(128)(4,1)}), s8[524288]{0:T(1024)(128)(4,1)S(1)}, s32[]{:S(2)}) async-start(s8[4718592]{0:T(1024)(128)(4,1)} %bitcast.67), calls=%async_computation.6 | async-start | bytes 1048576
  294.2 11.3 %copy-start.1 = (f32[1536,80]{0,1:T(8,128)S(1)}, f32[1536,80]{0,1:T(8,128)}, u32[]{:S(2)}) copy-start(f32[1536,80]{0,1:T(8,128)} %param.18) | copy-start | bytes 1474564

commit v2 on v1

--- a/solution.py
+++ b/solution.py
@@ -228,26 +228,86 @@
     return [slice(k, k + width) for k in range(0, inner, width)]
 
 
-def ends_kernel(width, step, u, d, bb, cc, a2, end, lam, dec):
-    for lanes in lane_blocks(a2.shape[1], width):
-        pass_ac(step, u, d, bb, cc, a2, end, lam, dec, lanes, width)
-
-
-def scans_kernel(width, step, u, m, d, bb, cc, a2, start, after, y, cg, sg, ms, bg, rate, h):
-    for k, lanes in enumerate(lane_blocks(a2.shape[1], width)):
-        pass_b(step, u, bb, cc, d, a2, start, y, h, cg, lanes, width, k == 0)
-        pass_d(step, u, m, bb, cc, d, a2, after, h, sg, ms, bg, rate, lanes, width, k == 0)
-
-
-def exchange_kernel(count, x_ref, o_ref, got, back, s1, r1, s2, r2):
+def scan_kernel(width, count, step, u, m, d, bb, cc, a2, y, cg, sg, ms, bg, rate, h, ends, edges, *carry):
+    meet(carry_peers(count), lax.axis_index("batch"), pltpu.get_barrier_semaphore())
+    blocks = lane_blocks(a2.shape[1], width)
+    for lanes in blocks:
+        pass_ac(step, u, d, bb, cc, a2, ends.at[0], ends.at[1], ends.at[2], lanes, width)
+    carry_exchange(count, ends, edges, *carry)
+    for k, lanes in enumerate(blocks):
+        pass_b(step, u, bb, cc, d, a2, edges.at[0], y, h, cg, lanes, width, k == 0)
+        pass_d(step, u, m, bb, cc, d, a2, edges.at[1], h, sg, ms, bg, rate, lanes, width, k == 0)
+
+
+def meet(seqs, b, bar):
+    for p in seqs:
+        pl.semaphore_signal(bar, inc=1, device_id=(p, b), device_id_type=MESH)
+    pl.semaphore_wait(bar, len(seqs))
+
+
+def carry_peers(count):
+    s = lax.axis_index("seq")
+    if tiled(count):
+        return [lax.rem(s + i, count) for i in range(1, count)]
+    return [s + (1 - 2 * (s // k % 2)) * k for k in powers(count)]
+
+
+def powers(count):
+    return [1 << k for k in range(count.bit_length() - 1)]
+
+
+def tiled(count):
+    return count in (2, 4, 6, 8, 12, 24)
+
+
+def carry_scratch(count, n, inner):
+    if tiled(count):
+        w = inner // (count // 2)
+        return [pltpu.VMEM((count, 3, 8, w), f32), pltpu.VMEM((count, 2, 8, w), f32)] + [pltpu.SemaphoreType.DMA((count - 1,))] * 4
+    k = len(powers(count))
+    return [pltpu.VMEM((k, 3, n, inner), f32), pltpu.VMEM((2, n, inner), f32)] + [pltpu.SemaphoreType.DMA((k,))] * 4
+
+
+def carry_exchange(count, ends, edges, got, back, s1, r1, s2, r2):
+    if tiled(count):
+        carry_tiles(count, ends, edges, got, back, s1, r1, s2, r2)
+    else:
+        carry_doubling(count, ends, edges, got, back, s1, r1)
+
+
+def carry_doubling(count, ends, edges, got, decays, ss, rs):
+    s, b = lax.axis_index("seq"), lax.axis_index("batch")
+    edges[...] = jnp.zeros_like(edges)
+    decays[...] = jnp.ones_like(decays)
+    for k, p in enumerate(carry_peers(count)):
+        copy = pltpu.make_async_remote_copy(
+            src_ref=ends, dst_ref=got.at[k], send_sem=ss.at[k], recv_sem=rs.at[k], device_id=(p, b), device_id_type=MESH)
+        copy.start()
+        copy.wait()
+        later = s // (1 << k) % 2
+
+        @pl.when(later == 1)
+        def _():
+            edges[0] += decays[0] * got[k, 0]
+            decays[0] *= got[k, 2]
+            ends[0] += ends[2] * got[k, 0]
+            ends[1] = got[k, 1] + got[k, 2] * ends[1]
+
+        @pl.when(later == 0)
+        def _():
+            edges[1] += decays[1] * got[k, 1]
+            decays[1] *= got[k, 2]
+            ends[1] += ends[2] * got[k, 1]
+            ends[0] = got[k, 0] + got[k, 2] * ends[0]
+
+        ends[2] *= got[k, 2]
+
+
+def carry_tiles(count, ends, edges, got, back, s1, r1, s2, r2):
     s, b = lax.axis_index("seq"), lax.axis_index("batch")
     across = count // 2
-    width = x_ref.shape[2] // across
-    bar = pltpu.get_barrier_semaphore()
-    peers = [lax.rem(s + i, count) for i in range(1, count)]
-    for p in peers:
-        pl.semaphore_signal(bar, inc=1, device_id=(p, b), device_id_type=MESH)
-    pl.semaphore_wait(bar, count - 1)
+    width = ends.shape[2] // across
+    peers = carry_peers(count)
 
     def part(ref, p):
         return ref.at[:, pl.ds(pl.multiple_of(p // across * 8, 8), 8), pl.ds(pl.multiple_of(p % across * width, 128), width)]
@@ -261,56 +321,37 @@
             out[-1].start()
         return out
 
-    first = copies(lambda p: part(x_ref, p), got.at[s], s1, r1)
-    got[s] = part(x_ref, s)[...]
+    first = copies(lambda p: part(ends, p), got.at[s], s1, r1)
+    got[s] = part(ends, s)[...]
     for c in first:
         c.wait_recv()
-    zero = jnp.zeros((8, width), f32)
-    value = zero
+    value = jnp.zeros((8, width), f32)
     for q in range(count):
         back[q, 0] = value
         value = got[q, 0] + got[q, 2] * value
-    value = zero
+    value = jnp.zeros((8, width), f32)
     for q in reversed(range(count)):
         back[q, 1] = value
         value = got[q, 1] + got[q, 2] * value
-    second = copies(lambda p: back.at[p], part(o_ref, s), s2, r2)
-    part(o_ref, s)[...] = back[s]
+    second = copies(lambda p: back.at[p], part(edges, s), s2, r2)
+    part(edges, s)[...] = back[s]
     for c in second:
         c.wait_recv()
     for c in first + second:
         c.wait_send()
 
 
-def exchange(count, end, lam, dec):
-    n, inner = end.shape
-    if count % 2 or n != 16 or inner % (count // 2 * 128):
-        return exchange_gathered(end, lam, dec)
-    width = inner // (count // 2)
-    sems = [pltpu.SemaphoreType.DMA((count - 1,))] * 4
-    out = pl.pallas_call(
-        functools.partial(exchange_kernel, count),
-        in_specs=[VMEM], out_specs=VMEM,
-        out_shape=jax.ShapeDtypeStruct((2, n, inner), f32),
-        scratch_shapes=[pltpu.VMEM((count, 3, 8, width), f32), pltpu.VMEM((count, 2, 8, width), f32)] + sems,
-        compiler_params=pltpu.CompilerParams(collective_id=2, has_side_effects=True),
-    )(jnp.stack([end, lam, dec]))
-    return out[0], out[1]
-
-
-def exchange_gathered(end, lam, dec):
-    ends, lams, decs = lax.all_gather((end, lam, dec), "seq")
-    count, mine = lax.axis_size("seq"), lax.axis_index("seq")
-
-    def ahead(q, value):
-        return jnp.where(q < mine, ends[q] + decs[q] * value, value)
-
-    def behind(i, value):
-        q = count - 1 - i
-        return jnp.where(q > mine, lams[q] + decs[q] * value, value)
-
-    zero = jnp.zeros_like(end)
-    return lax.fori_loop(0, count, ahead, zero), lax.fori_loop(0, count, behind, zero)
+def scans(count, step, u, mixed, d_result, bb, cc, a2):
+    group, inner = step.shape
+    n = a2.shape[0]
+    token, part, state = [jax.ShapeDtypeStruct(v, f32) for v in ((group, inner), (group, n, 128), (n, inner))]
+    return pl.pallas_call(
+        functools.partial(scan_kernel, 512, count),
+        in_specs=[VMEM] * 7, out_specs=[VMEM] * 6,
+        out_shape=[token, part, token, token, part, state],
+        scratch_shapes=[pltpu.VMEM((group, n, 512), f32), pltpu.VMEM((3, n, inner), f32), pltpu.VMEM((2, n, inner), f32), *carry_scratch(count, n, inner)],
+        compiler_params=pltpu.CompilerParams(collective_id=2, has_side_effects=True, vmem_limit_bytes=56 << 20),
+    )(step, u, mixed, d_result, bb, cc, a2)
 
 
 def shifted(x, axis, by):
@@ -352,12 +393,7 @@
     d_result = d_gated * gate_act
     spread = [jnp.broadcast_to(proj[:, k:k + states, None], (group, states, 128)) for k in (rank, rank + states)]
     u = step * mixed
-    end, lam, dec = local_call(functools.partial(ends_kernel, 512), [(states, inner)] * 3, (step, u, d_result, *spread, a2))
-    start, after = exchange(sizes["seq"], end, lam, dec)
-    token, part, state = (group, inner), (group, states, 128), (states, inner)
-    y, cg, step_grad, mixed_scan, bg, rate_sum = local_call(
-        functools.partial(scans_kernel, 512), [token, part, token, token, part, state],
-        (step, u, mixed, d_result, *spread, a2, start, after), [pltpu.VMEM((group, states, 512), f32)])
+    y, cg, step_grad, mixed_scan, bg, rate_sum = scans(sizes["seq"], step, u, mixed, d_result, *spread, a2)
     result = y + skip_gain * mixed
     gated = result * gate_act
     block_out = x + matmul(gated, w_out)

time: 306 us -> 297 us (0.971)
  Pallas kernels: 213 us -> 208 us
    pallas_call x3 -> x1, Pallas kernels: 41.8 us -> 37.1 us  [scans(): pl.pallas_call(functools.partial(scan_kernel, 512, count), in_specs=[VMEM...]
where the time goes in v2:
time: 297 us
  Pallas kernels  208 us (70%)
  matrix products  39.1 us (13%)
  local copies, waits for them, and re-layouts  29.6 us (10%)
  other arithmetic  10.6 us (4%)
  starting transfers between devices  5.44 us (2%)
    pallas_call x1, Pallas kernels, all_reduce(): pl.pallas_call(functools.partial(ar_kernel, chunks, plans, len(arrays), N...  171 us
    dot_general x12, matrix products, matmul(): lax.dot_general(left, right, (dims, ((), ())), precision=lax.Precision.HI...  39.1 us
    pallas_call x1, Pallas kernels, scans(): pl.pallas_call(functools.partial(scan_kernel, 512, count), in_specs=[VMEM...  37.1 us
    unnamed x74, local copies, waits for them, and re-layouts  12.9 us
    slice x9, local copies, waits for them, and re-layouts, take(): return small[at[0] - count:at[0]]  8.3 us
  transfers between devices with their start and end apart: 2, of which 2 were waited for; matrix products, arithmetic and copies ran while one was open for 0% of the time, Pallas kernels for 0%

profile of v2, /device:TPU:1, one launch (start us, length us, event | category | flops | bytes accessed | tf_op | source)
XLA Modules:
  0.0 296.9 jit_solution(3245111952193518598)
XLA Ops:
  0.7 1.3 fusion.22
  1.9 0.5 multiply_multiply_fusion.1
  2.5 0.5 copy-done.22
  3.0 6.6 %fusion.30 = f32[128,3072]{1,0:T(8,128)S(1)} fusion(f32[768,3072]{1,0:T(8,128)} %param.15, f32[1,128,768]{2,1,0:T(8,128)} %param.13, f32[768]{0:T(1024)} %param.14, f32[128]{0:T(128)S(1)} %get-tuple-element.62), kind=kOutput, calls=%fused_computation.61 | convolution fusion | flops 1812135936 | bytes 11406848 | tf_op jit(solution)/shard_map/dot_general | solution.py:363
  9.6 3.9 %collective-permute-start = (f32[3,1536]{1,0:T(4,128)S(1)}, f32[3,1536]{1,0:T(4,128)S(1)}, u32[]{:S(2)}, u32[]{:S(2)}) collective-permute-start(f32[3,1536]{1,0:T(4,128)S(1)} %slice.139), channel_id=1, source_target_pairs={{0,4},{4,8},{8,12},{12,16},{16,20},{20,24},{24,28},{1,5},{5,9},{9,... | collective-permute-start | bytes 55304 | tf_op jit(solution)/shard_map/ppermute | solution.py:359
  13.6 0.7 bitcast_multiply_fusion.6.a2
  14.6 4.8 %multiply_reduce_fusion = (f32[1536]{0:T(1024)}, f32[128,1536]{1,0:T(8,128)}, f32[128,1536]{1,0:T(8,128)S(1)}, f32[128,1536]{1,0:T(8,128)}, f32[128,1536]{1,0:T(8,128)}) fusion(f32[128,3072]{1,0:T(8,128)S(1)} %fusion.30, f32[128,1536]{1,0:T(8,128)S(1)} %slice.140, f32[1536]{0:T(1024)S(1)} %get-tuple-element.45, f32[3,1536]{1,0:T(4,128)S(1)} %collective-permute-done, ...), kind=kOutput, calls=%fused_computation.30 | convolution fusion | flops 910293504 | bytes 9885696 | tf_op jit(solution)/shard_map/dot_general | solution.py:363
  19.4 0.5 fusion.55
  20.0 0.1 copy.28
  20.1 0.1 copy.27
  20.2 2.2 fusion.46
  22.4 1.3 broadcast_in_dim.8.bb
  23.7 1.3 broadcast_in_dim.9.cc
  25.0 37.1 %shard_map.220 = (f32[128,1536]{1,0:T(8,128)}, f32[128,16,128]{2,1,0:T(8,128)}, f32[128,1536]{1,0:T(8,128)}, f32[128,1536]{1,0:T(8,128)}, f32[128,16,128]{2,1,0:T(8,128)}, /*index=5*/f32[16,1536]{1,0:T(8,128)}) custom-call(f32[128,1536]{1,0:T(8,128)} %get-tuple-element.58.step, f32[128,1536]{1,0:T(8,128)} %get-tuple-element.57.u, f32[128,1536]{1,0:T(8,128)} %copy-done.2, ...), custom_call_target="tpu_custom_call" | custom-call | tf_op jit(solution)/shard_map/pallas_call | solution.py:348
  62.1 2.0 fusion.53
  64.1 0.9 copy-done.5
  65.0 0.5 fusion.56
  65.5 1.6 reduce_sum.109
  67.2 1.6 reduce_sum.110
  68.9 0.4 fusion.38
  69.2 2.5 fusion.1
  71.8 1.7 fusion.50
  73.6 4.7 %fusion.4 = f32[1,128,768]{2,1,0:T(8,128)} fusion(f32[1536,768]{1,0:T(8,128)} %param.24, f32[1,128,768]{2,1,0:T(8,128)S(1)} %copy-done.4, f32[128,1536]{1,0:T(8,128)S(1)} %get-tuple-element.56, f32[128,3072]{1,0:T(8,128)S(1)} %fusion.30), kind=kOutput, calls=%fused_computation.9 | convolution fusion | flops 907051008 | bytes 7077888 | tf_op jit(solution)/shard_map/dot_general | solution.py:363
  78.4 4.3 %fusion.17.refs_1_ = f32[1536,768]{1,0:T(8,128)} fusion(f32[1,128,768]{2,1,0:T(8,128)S(1)} %copy-done.10, f32[128,1536]{1,0:T(8,128)S(1)} %get-tuple-element.56, f32[128,3072]{1,0:T(8,128)S(1)} %fusion.30), kind=kOutput, calls=%fused_computation.43 | convolution fusion | flops 906952704 | bytes 6684672 | tf_op jit(solution)/shard_map/dot_general | solution.py:363
  82.6 1.5 collective-permute-start.1
  84.2 0.3 fusion.39
  84.6 2.6 collective-permute-done.1
  87.2 0.4 fusion.9
  87.6 5.8 %fusion.28 = (f32[768]{0:T(1024)S(1)}, f32[128]{0:T(128)S(1)}, f32[128,768]{1,0:T(8,128)}) fusion(f32[1,128,768]{2,1,0:T(8,128)S(1)} %copy-done.4, f32[128]{0:T(128)S(1)} %copy-done.23, f32[768]{0:T(1024)S(1)} %copy-done.17, f32[768,3072]{1,0:T(8,128)S(1)} %bitcast.57, f32[128,1536]{1,0:T(8,128)S(1)} %get-tuple-element.55, f32[128,1536]{1,0:T(8,128)S(1)} %fusion.9), kind=kOutput, calls=%fused_computation.60 | convolution fusion | flops 1812921472 | bytes 11803648 | tf_op jit(solution)/shard_map/dot_general | solution.py:363
  93.4 6.4 %fusion.2.refs_0_ = f32[768,3072]{1,0:T(8,128)} fusion(f32[128,1536]{1,0:T(8,128)S(1)} %get-tuple-element.55, f32[128,1536]{1,0:T(8,128)S(1)} %fusion.9, f32[1,128,768]{2,1,0:T(8,128)S(1)} %copy-done.4, f32[768]{0:T(1024)S(1)} %copy-done.17, f32[128]{0:T(128)S(1)} %copy-done.23), kind=kOutput, calls=%fused_computation.6 | convolution fusion | flops 1812529152 | bytes 11406848 | tf_op jit(solution)/shard_map/dot_general | solution.py:363
  99.9 0.3 concatenate.19
  100.3 1.1 reshape.67.refs_2_
  101.5 171.1 %shard_map.221 = (f32[768,3072]{1,0:T(8,128)}, f32[1536,768]{1,0:T(8,128)}, f32[256,1024]{1,0:T(8,128)}) custom-call(f32[768,3072]{1,0:T(8,128)} %fusion.2.refs_0_, f32[1536,768]{1,0:T(8,128)} %fusion.17.refs_1_, f32[256,1024]{1,0:T(8,128)} %reshape.67.refs_2_), custom_call_target="tpu_custom_call" | custom-call | tf_op jit(solution)/shard_map/pallas_call | solution.py:209
  272.6 0.8 slice.128
  273.4 0.9 slice.136
  274.3 1.0 slice.133
  275.3 1.1 slice.131
  276.4 1.3 slice.125
  277.6 1.2 reshape.68
  278.8 1.3 slice_reduce_fusion.7
  280.1 1.6 slice_reduce_fusion
  281.7 0.6 slice.129
  282.3 0.7 slice.137
  283.0 0.8 slice.134
  283.8 0.9 slice.132
  284.7 0.9 fusion.21
  285.6 9.1 %copy.33 = f32[768,3072]{1,0:T(8,128)} copy(f32[768,3072]{1,0:T(8,128)} %get-tuple-element.81) | data formatting | bytes 18874368
  294.7 2.2 copy.34
  (95 shorter events, 0.8 us)
Async XLA Ops:
  0.6 18.8 %copy-start = (f32[1536,80]{0,1:T(8,128)S(1)}, f32[1536,80]{0,1:T(8,128)}, u32[]{:S(2)}) copy-start(f32[1536,80]{0,1:T(8,128)} %param.18) | copy-start | bytes 1474564
  0.7 13.9 %slice-start.3 = ((s8[4718592]{0:T(1024)(128)(4,1)}), s8[4194304]{0:T(1024)(128)(4,1)S(1)}, s32[]{:S(2)}) async-start(s8[4718592]{0:T(1024)(128)(4,1)} %bitcast.58), calls=%async_computation.3 | async-start | bytes 8388608
  2.5 0.5 copy-start.22
  3.0 10.6 %copy-start.26 = (s32[1536]{0:T(1024)S(1)}, s32[1536]{0:T(1024)}, u32[]{:S(2)}) copy-start(s32[1536]{0:T(1024)} %param.21) | copy-start | bytes 18436
  3.0 10.6 %copy-start.16 = (f32[1536,16]{0,1:T(8,128)S(1)}, f32[1536,16]{0,1:T(8,128)}, u32[]{:S(2)}) copy-start(f32[1536,16]{0,1:T(8,128)} %param.22) | copy-start | bytes 294916
  3.0 11.3 %copy-start.20 = (f32[4,1536]{1,0:T(4,128)S(1)}, f32[4,1536]{1,0:T(4,128)}, u32[]{:S(2)}) copy-start(f32[4,1536]{1,0:T(4,128)} %param.16) | copy-start | bytes 73732
  3.0 11.5 %slice-start.4 = ((s8[4718592]{0:T(1024)(128)(4,1)}), s8[524288]{0:T(1024)(128)(4,1)S(1)}, s32[]{:S(2)}) async-start(s8[4718592]{0:T(1024)(128)(4,1)} %bitcast.58), calls=%async_computation.4 | async-start | bytes 1048576
  3.0 11.5 %copy-start.9 = (f32[1,128,768]{2,1,0:T(8,128)S(1)}, f32[1,128,768]{2,1,0:T(8,128)}, u32[]{:S(2)}) copy-start(f32[1,128,768]{2,1,0:T(8,128)} %param.25) | copy-start | bytes 1179652
  3.0 11.5 %copy-start.28 = (f32[1536]{0:T(1024)S(1)}, f32[1536]{0:T(1024)}, u32[]{:S(2)}) copy-start(f32[1536]{0:T(1024)} %param.17) | copy-start | bytes 18436
  9.6 4.9 %collective-permute-start = (f32[3,1536]{1,0:T(4,128)S(1)}, f32[3,1536]{1,0:T(4,128)S(1)}, u32[]{:S(2)}, u32[]{:S(2)}) collective-permute-start(f32[3,1536]{1,0:T(4,128)S(1)} %slice.139), channel_id=1, source_target_pairs={{0,4},{4,8},{8,12},{12,16},{16,20},{20,24},{24,28},{1,5},{5,9},{9,... | collective-permute-start | bytes 55304 | tf_op jit(solution)/shard_map/ppermute | solution.py:359
  14.4 5.0 %copy-start.7 = (f32[128,1536]{1,0:T(8,128)}, f32[128,1536]{1,0:T(8,128)S(1)}, u32[]{:S(2)}) copy-start(f32[128,1536]{1,0:T(8,128)S(1)} %slice.140) | copy-start | bytes 2359300
  14.5 4.9 %copy-start.21 = (f32[3,1536]{1,0:T(4,128)}, f32[3,1536]{1,0:T(4,128)S(1)}, u32[]{:S(2)}) copy-start(f32[3,1536]{1,0:T(4,128)S(1)} %collective-permute-done) | copy-start | bytes 55300
  14.5 5.6 %copy-start.13 = (f32[48,1536]{1,0:T(8,128)S(1)}, f32[48,1536]{1,0:T(8,128)}, u32[]{:S(2)}) copy-start(f32[48,1536]{1,0:T(8,128)} %param.19) | copy-start | bytes 884740
  14.6 5.6 %copy-start.24 = (f32[1536]{0:T(1024)S(1)}, f32[1536]{0:T(1024)}, u32[]{:S(2)}) copy-start(f32[1536]{0:T(1024)} %param.20) | copy-start | bytes 18436
  19.4 5.6 %copy-start.2 = (f32[128,1536]{1,0:T(8,128)}, f32[128,1536]{1,0:T(8,128)S(1)}, u32[]{:S(2)}) copy-start(f32[128,1536]{1,0:T(8,128)S(1)} %get-tuple-element.49.m) | copy-start | bytes 2359300
  62.1 6.7 %copy-start.3 = (f32[128,1536]{1,0:T(8,128)S(1)}, f32[128,1536]{1,0:T(8,128)}, u32[]{:S(2)}) copy-start(f32[128,1536]{1,0:T(8,128)} %copy-done.2) | copy-start | bytes 2359300
  64.1 0.9 copy-start.5
  68.8 3.0 copy-start.8
  68.8 3.0 copy-start.14
  68.8 3.0 copy-start.15
  71.7 1.8 copy-start.4
  71.8 15.7 %slice-start = ((s8[9437184]{0:T(1024)(128)(4,1)}), s8[4194304]{0:T(1024)(128)(4,1)S(1)}, s32[]{:S(2)}) async-start(s8[9437184]{0:T(1024)(128)(4,1)} %bitcast.56), calls=%async_computation | async-start | bytes 8388608
  73.5 4.8 %copy-start.10 = (f32[1,128,768]{2,1,0:T(8,128)S(1)}, f32[1,128,768]{2,1,0:T(8,128)}, u32[]{:S(2)}) copy-start(f32[1,128,768]{2,1,0:T(8,128)} %param.25) | copy-start | bytes 1179652
  73.6 14.0 %slice-start.1 = ((s8[9437184]{0:T(1024)(128)(4,1)}), s8[4194304]{0:T(1024)(128)(4,1)S(1)}, s32[]{:S(2)}) async-start(s8[9437184]{0:T(1024)(128)(4,1)} %bitcast.56), calls=%async_computation.1 | async-start | bytes 8388608
  78.3 5.9 %copy-start.18 = (f32[16,1536]{1,0:T(8,128)S(1)}, f32[16,1536]{1,0:T(8,128)}, u32[]{:S(2)}) copy-start(f32[16,1536]{1,0:T(8,128)} %get-tuple-element.26) | copy-start | bytes 294916
  78.3 5.9 %copy-start.6 = (f32[128,1536]{1,0:T(8,128)S(1)}, f32[128,1536]{1,0:T(8,128)}, u32[]{:S(2)}) copy-start(f32[128,1536]{1,0:T(8,128)} %copy-done.5) | copy-start | bytes 2359300
  78.3 6.2 %copy-start.25 = (f32[1536]{0:T(1024)S(1)}, f32[1536]{0:T(1024)}, u32[]{:S(2)}) copy-start(f32[1536]{0:T(1024)} %get-tuple-element.47) | copy-start | bytes 18436
  78.3 6.2 %copy-start.19 = (f32[1536]{0:T(1024)S(1)}, f32[1536]{0:T(1024)}, u32[]{:S(2)}) copy-start(f32[1536]{0:T(1024)} %get-tuple-element.51) | copy-start | bytes 18436
  78.3 9.3 %slice-start.2 = ((s8[9437184]{0:T(1024)(128)(4,1)}), s8[1048576]{0:T(1024)(128)(4,1)S(1)}, s32[]{:S(2)}) async-start(s8[9437184]{0:T(1024)(128)(4,1)} %bitcast.56), calls=%async_computation.2 | async-start | bytes 2097152
  78.3 9.3 %copy-start.17 = (f32[768]{0:T(1024)S(1)}, f32[768]{0:T(1024)}, u32[]{:S(2)}) copy-start(f32[768]{0:T(1024)} %param.14) | copy-start | bytes 9220
  78.3 9.3 %copy-start.23 = (f32[128]{0:T(128)S(1)}, f32[128]{0:T(128)}, u32[]{:S(2)}) copy-start(f32[128]{0:T(128)} %copy-done.22) | copy-start | bytes 1540
  82.6 4.6 %collective-permute-start.1 = (f32[3,1536]{1,0:T(4,128)S(1)}, f32[3,1536]{1,0:T(4,128)S(1)}, u32[]{:S(2)}, u32[]{:S(2)}) collective-permute-start(f32[3,1536]{1,0:T(4,128)S(1)} %slice.149), channel_id=1, source_target_pairs={{4,0},{8,4},{12,8},{16,12},{20,16},{24,20},{28,24},{5,1},{9,5},{13... | collective-permute-start | bytes 55304 | tf_op jit(solution)/shard_map/ppermute | solution.py:359
  272.6 12.1 %copy-start.11 = (f32[1,128,768]{2,1,0:T(8,128)S(1)}, f32[1,128,768]{2,1,0:T(8,128)}, u32[]{:S(2)}) copy-start(f32[1,128,768]{2,1,0:T(8,128)} %param.25) | copy-start | bytes 1179652
  272.6 12.1 %copy-start.12 = (f32[128,768]{1,0:T(8,128)S(1)}, f32[128,768]{1,0:T(8,128)}, u32[]{:S(2)}) copy-start(f32[128,768]{1,0:T(8,128)} %get-tuple-element.65) | copy-start | bytes 1179652
  272.6 12.1 %copy-start.27 = (f32[128]{0:T(128)S(1)}, f32[128]{0:T(128)}, u32[]{:S(2)}) copy-start(f32[128]{0:T(128)} %get-tuple-element.61) | copy-start | bytes 1540
  284.7 10.0 %slice-start.5 = ((s8[4718592]{0:T(1024)(128)(4,1)}), s8[4194304]{0:T(1024)(128)(4,1)S(1)}, s32[]{:S(2)}) async-start(s8[4718592]{0:T(1024)(128)(4,1)} %bitcast.60), calls=%async_computation.5 | async-start | bytes 8388608
  285.6 9.1 %slice-start.6 = ((s8[4718592]{0:T(1024)(128)(4,1)}), s8[524288]{0:T(1024)(128)(4,1)S(1)}, s32[]{:S(2)}) async-start(s8[4718592]{0:T(1024)(128)(4,1)} %bitcast.60), calls=%async_computation.6 | async-start | bytes 1048576
  285.6 11.3 %copy-start.1 = (f32[1536,80]{0,1:T(8,128)S(1)}, f32[1536,80]{0,1:T(8,128)}, u32[]{:S(2)}) copy-start(f32[1536,80]{0,1:T(8,128)} %param.18) | copy-start | bytes 1474564

commit v3 on v0

v3 whole, which is shorter than its diff:
```python
import functools

import jax
import jax.numpy as jnp
from jax import lax
from jax.experimental import pallas as pl
from jax.experimental.pallas import tpu as pltpu
from jax.sharding import PartitionSpec as P

f32 = jnp.float32
bf16 = jnp.bfloat16
MESH = pl.DeviceIdType.MESH
EPSILON = 1e-05
LOG2E = 1.4426950408889634
LN2 = 0.6931471805599453
LANES = 128
SCAN = 512
WBLOCK = 256
SLOTS = 4
SMALL = (256, 1024)


def mult(value, by):
    return value if isinstance(value, int) else pl.multiple_of(value, by)


def split(value):
    high = value.astype(bf16)
    return high, (value - high.astype(f32)).astype(bf16)


def dot(a, b, dims):
    return lax.dot_general(a, b, (dims, ((), ())), preferred_element_type=f32)


def matmul(a, b, dims=((1,), (0,))):
    (ah, al), (bh, bl) = split(a), split(b)
    return dot(ah, bh, dims) + dot(al, bh, dims) + dot(ah, bl, dims)


def stacked(value):
    return jnp.concatenate(split(value), axis=0)


def rows_matmul(both, b, dims):
    rows = both.shape[0] // 2
    bh, bl = split(b)
    wide = dot(both, bh, dims)
    return wide[:rows] + wide[rows:] + dot(both[:rows], bl, dims)


def sigmoid(v):
    return 1.0 / (1.0 + jnp.exp(-v))


def loop(count, body):
    def step(i, _):
        body(i)
        return 0

    lax.fori_loop(0, count, step, 0)


class Place:
    def __init__(self, sizes):
        self.sizes = sizes
        self.s, self.b = lax.axis_index("seq"), lax.axis_index("batch")
        self.at = {"seq": self.s, "batch": self.b}
        self.x, self.c, self.y = self.s % 2, self.b % 2, self.b // 2
        self.odd = self.c
        self.q = self.x + 2 * self.y

    def near(self, dx, dy, dc):
        seq = self.s + dx * (1 - 2 * self.x)
        batch = self.b + dc * (1 - 2 * self.c) + 2 * dy * (1 - 2 * self.y)
        return (seq, batch), self.q + dx * (1 - 2 * self.x) + 2 * dy * (1 - 2 * self.y)

    def bit(self, d):
        return self.at[d[0]] // (1 << d[1]) % 2

    def stage(self, pair):
        to = dict(self.at)
        first, second = pair
        if first == second:
            v = self.bit(first)
            to[first[0]] = to[first[0]] + (1 - 2 * v) * (1 << first[1])
        else:
            va, vb = self.bit(first), self.bit(second)
            to[first[0]] = to[first[0]] + (1 - self.odd) * (1 - 2 * va) * (1 << first[1])
            to[second[0]] = to[second[0]] + self.odd * (1 - 2 * vb) * (1 << second[1])
            v = (1 - self.odd) * va + self.odd * vb
        return (to["seq"], to["batch"]), v


class Links:
    def __init__(self, send, recv):
        self.send, self.recv, self.used, self.open = send, recv, 0, []

    def copy(self, src, dst, to, start=True):
        i = self.used
        self.used += 1
        c = pltpu.make_async_remote_copy(
            src_ref=src, dst_ref=dst, send_sem=self.send.at[i], recv_sem=self.recv.at[i], device_id=to, device_id_type=MESH
        )
        if start:
            c.start()
            self.open.append(c)
        return c

    def sent(self, copy):
        copy.wait_send()
        self.open = [c for c in self.open if c is not copy]

    def drain(self):
        for c in self.open:
            c.wait_send()
        self.open = []


GROUP = [(dx, dy, dc) for dx in (0, 1) for dy in (0, 1) for dc in (0, 1) if dx + dy + dc]


def log2(size):
    return size.bit_length() - 1


def all_bits(sizes):
    s = [("seq", k) for k in range(log2(sizes["seq"]))]
    b = [("batch", k) for k in range(log2(sizes["batch"]))]
    return s, b


def small_plan(sizes):
    s, b = all_bits(sizes)
    return [(b[0], b[0]), (s[0], b[1]), (b[1], s[0])] + [(q, q) for q in s[1:] + b[2:]]


def halvings(rows, stages):
    out = []
    for _ in range(stages):
        ok = rows % 16 == 0
        out.append(ok)
        rows = rows // 2 if ok else rows
    return out


def landing_rows(rows, stages):
    total = 0
    for ok in halvings(rows, stages):
        rows = rows // 2 if ok else rows
        total += rows
    return total


def reduce_rows(place, links, plan, acc, land, whole):
    rows = acc.shape[0]
    half = halvings(rows, len(plan))
    off, base, kept = 0, 0, []
    for pair, ok in zip(plan, half):
        to, v = place.stage(pair)
        if ok:
            rows //= 2
            keep, give = off + v * rows, off + (1 - v) * rows
        else:
            keep = give = off
        copy = links.copy(acc.at[pl.ds(mult(give, 8), rows)], land.at[pl.ds(base, rows)], to)
        yield
        copy.wait_recv()
        if not ok:
            links.sent(copy)

        def add(i, keep=keep, base=base):
            at = pl.ds(mult(keep + i * 8, 8), 8)
            acc[at] = acc[at] + land[pl.ds(mult(base + i * 8, 8), 8)]

        loop(rows // 8, add)
        base += rows
        if ok:
            kept.append((to, keep, rows))
        off = keep

    def place_row(i):
        whole(off + i * 8, 8)[...] = acc[pl.ds(mult(off + i * 8, 8), 8)]

    loop(rows // 8, place_row)
    for to, keep, rows in reversed(kept):
        part = whole(keep, rows)
        copy = links.copy(part, part, to)
        yield
        copy.wait_recv()


def tiled(count):
    return count in (2, 4, 6, 8, 12, 24)


def carry_peers(count, s):
    if tiled(count):
        return [lax.rem(s + i, count) for i in range(1, count)]
    return [s + (1 - 2 * (s // (1 << k) % 2)) * (1 << k) for k in range(log2(count))]


def carry_scratch(count, n, inner):
    if tiled(count):
        w = inner // (count // 2)
        return [pltpu.VMEM((count, 3, 8, w), f32), pltpu.VMEM((count, 2, 8, w), f32)]
    return [pltpu.VMEM((log2(count), 3, n, inner), f32), pltpu.VMEM((2, n, inner), f32)]


def carry_doubling(place, links, ends, edges, got, decays):
    edges[...] = jnp.zeros_like(edges)
    decays[...] = jnp.ones_like(decays)
    for k, p in enumerate(carry_peers(place.sizes["seq"], place.s)):
        copy = links.copy(ends, got.at[k], (p, place.b))
        copy.wait_recv()
        links.sent(copy)
        later = place.bit(("seq", k))

        @pl.when(later == 1)
        def _():
            edges[0] += decays[0] * got[k, 0]
            decays[0] *= got[k, 2]
            ends[0] += ends[2] * got[k, 0]
            ends[1] = got[k, 1] + got[k, 2] * ends[1]

        @pl.when(later == 0)
        def _():
            edges[1] += decays[1] * got[k, 1]
            decays[1] *= got[k, 2]
            ends[1] += ends[2] * got[k, 1]
            ends[0] = got[k, 0] + got[k, 2] * ends[0]

        ends[2] *= got[k, 2]


def carry_tiles(place, links, ends, edges, got, back):
    count, s, b = place.sizes["seq"], place.s, place.b
    across = count // 2
    width = ends.shape[2] // across
    peers = carry_peers(count, s)

    def part(ref, p):
        return ref.at[:, pl.ds(mult(p // across * 8, 8), 8), pl.ds(mult(p % across * width, LANES), width)]

    first = [links.copy(part(ends, p), got.at[s], (p, b)) for p in peers]
    got[s] = part(ends, s)[...]
    for c in first:
        c.wait_recv()
    value = jnp.zeros((8, width), f32)
    for p in range(count):
        back[p, 0] = value
        value = got[p, 0] + got[p, 2] * value
    value = jnp.zeros((8, width), f32)
    for p in reversed(range(count)):
        back[p, 1] = value
        value = got[p, 1] + got[p, 2] * value
    second = [links.copy(back.at[p], part(edges, s), (p, b)) for p in peers]
    part(edges, s)[...] = back[s]
    for c in second:
        c.wait_recv()


def carry(place, links, *refs):
    (carry_tiles if tiled(place.sizes["seq"]) else carry_doubling)(place, links, *refs)


def wide(tile):
    return jnp.concatenate([tile] * (SCAN // LANES), axis=1)


def spread(row, n):
    return jnp.broadcast_to(row, (n, row.shape[1]))


def fold(value):
    return sum(value[:, k : k + LANES] for k in range(0, value.shape[1], LANES))


def scan_ends(m, lanes):
    a2 = m.a2[:, lanes]
    n = a2.shape[0]

    def chunk(i, held):
        h, dec, acc = held
        at = pl.ds(pl.multiple_of(i * 8, 8), 8)
        s8, u8, d8 = m.step[at, lanes], m.u[at, lanes], m.d_res[at, lanes]
        for j in range(8):
            t = pl.ds(pl.multiple_of((i * 8 + j) * n, 8), n)
            b, c = wide(m.bb[t]), wide(m.cc[t])
            a = jnp.exp2(spread(s8[j : j + 1], n) * a2)
            h = a * h + spread(u8[j : j + 1], n) * b
            dec = dec * a
            acc = acc + dec * (spread(d8[j : j + 1], n) * c)
        return h, dec, acc

    zero = jnp.zeros_like(a2)
    h, dec, acc = lax.fori_loop(0, m.step.shape[0] // 8, chunk, (zero, zero + 1.0, zero))
    m.ends[0, :, lanes], m.ends[1, :, lanes], m.ends[2, :, lanes] = h, acc, dec


def scan_out(m, lanes):
    a2 = m.a2[:, lanes]
    n = a2.shape[0]

    def chunk(i, h):
        at = pl.ds(pl.multiple_of(i * 8, 8), 8)
        s8, u8 = m.step[at, lanes], m.u[at, lanes]
        ys = []
        for j in range(8):
            t = pl.ds(pl.multiple_of((i * 8 + j) * n, 8), n)
            b, c = wide(m.bb[t]), wide(m.cc[t])
            h = jnp.exp2(spread(s8[j : j + 1], n) * a2) * h + spread(u8[j : j + 1], n) * b
            ys.append(jnp.sum(c * h, axis=0, keepdims=True))
        m.y[at, lanes] = jnp.concatenate(ys, axis=0)
        return h

    lax.fori_loop(0, m.step.shape[0] // 8, chunk, m.edges[0, :, lanes])


def scan_back(m, lanes, first):
    a2 = m.a2[:, lanes]
    n = a2.shape[0]
    tokens = m.step.shape[0]

    def ahead(i, h):
        at = pl.ds(pl.multiple_of(i * 8, 8), 8)
        s8, u8, d8 = m.step[at, lanes], m.u[at, lanes], m.d_res[at, lanes]
        for j in range(8):
            t = pl.ds(pl.multiple_of((i * 8 + j) * n, 8), n)
            m.h[i * 8 + j] = h
            h = jnp.exp2(spread(s8[j : j + 1], n) * a2) * h + spread(u8[j : j + 1], n) * wide(m.bb[t])
            part = fold(spread(d8[j : j + 1], n) * h)
            m.cg[t] = part if first else m.cg[t] + part
        return h

    lax.fori_loop(0, tokens // 8, ahead, m.edges[0, :, lanes])

    def behind(i, held):
        q, rate = held
        r = tokens // 8 - 1 - i
        at = pl.ds(pl.multiple_of(r * 8, 8), 8)
        s8, u8, d8 = m.step[at, lanes], m.u[at, lanes], m.d_res[at, lanes]
        sg, lb = [None] * 8, [None] * 8
        for j in reversed(range(8)):
            t = pl.ds(pl.multiple_of((r * 8 + j) * n, 8), n)
            st = spread(s8[j : j + 1], n)
            lam = spread(d8[j : j + 1], n) * wide(m.cc[t]) + q
            q = jnp.exp2(st * a2) * lam
            dec = q * m.h[r * 8 + j]
            lb[j] = jnp.sum(lam * wide(m.bb[t]), axis=0, keepdims=True)
            sg[j] = jnp.sum(dec * a2, axis=0, keepdims=True)
            rate = rate + dec * st
            part = fold(lam * spread(u8[j : j + 1], n))
            m.bg[t] = part if first else m.bg[t] + part
        lb8, sg8 = jnp.concatenate(lb, axis=0), jnp.concatenate(sg, axis=0)
        m.sg[at, lanes] = LN2 * sg8 + m.mixed[at, lanes] * lb8
        m.ms[at, lanes] = s8 * lb8
        return q, rate

    _, rate = lax.fori_loop(0, tokens // 8, behind, (m.edges[1, :, lanes], jnp.zeros_like(a2)))
    m.rate[:, lanes] = rate


class Refs:
    pass


ARGS = ["x", "g", "gain", "w_in", "conv_w", "conv_b", "x_proj", "step_proj", "step_b", "code", "a2", "skip", "w_out"]
OUTS = ["block_out", "input_grad", "in_sum", "out_sum", "small_sum"]


def scratch(sizes, tokens, width, inner, n, rank):
    full = (tokens, inner)
    quarter, part = inner // 4, width // 2
    zs = log2(sizes["seq"]) - 1 + log2(sizes["batch"]) - 2
    v = lambda *shape: pltpu.VMEM(shape, f32)
    sh = {name: v(*full) for name in ("gate", "d_res", "conv", "mixed", "pre", "step", "u", "y", "gated", "d_gate", "sg", "ms", "x_grad")}
    sh.update(
        normed=v(tokens, width), hid=v(8 + tokens, inner), cgr=v(tokens + 8, inner), proj=v(tokens, LANES),
        wbuf=v(SLOTS, width, WBLOCK), w_out_v=v(inner, width), acc=v(tokens, width),
        bb=v(tokens * n, LANES), cc=v(tokens * n, LANES), bg=v(tokens * n, LANES), cg=v(tokens * n, LANES),
        h=v(tokens, n, SCAN), rate=v(n, inner), ends=v(3, n, inner), edges=v(2, n, inner),
        ng=v(8, tokens, part), gg=v(8, tokens, part),
        late0=v(8, tokens, quarter), late1=v(8, tokens, quarter), late2=v(8, tokens, quarter),
        tile0=v(quarter, part), tile1=v(part, quarter), tile2=v(part, quarter),
        land0=v(landing_rows(quarter, zs), part), land1=v(landing_rows(part, zs), quarter), land2=v(landing_rows(part, zs), quarter),
        small=v(*SMALL), small_land=v(landing_rows(SMALL[0], len(small_plan(sizes))), SMALL[1]),
    )
    sh["got"], sh["back"] = carry_scratch(sizes["seq"], n, inner)
    sh["send"], sh["recv"] = [pltpu.SemaphoreType.DMA((160,))] * 2
    sh["wsem"] = pltpu.SemaphoreType.DMA((SLOTS,))
    sh["osem"] = pltpu.SemaphoreType.DMA
    return sh


def stream(m, blocks, use):
    def fetch(i, slot):
        cols = pl.ds(mult(i * WBLOCK, WBLOCK), WBLOCK)
        return pltpu.make_async_copy(m.w_in.at[:, cols], m.wbuf.at[slot], m.wsem.at[slot])

    first, last = blocks
    for k in range(SLOTS - 1):
        fetch(first + k, k).start()

    def body(i):
        slot = lax.rem(i, SLOTS)
        fetch(first + i, slot).wait()

        @pl.when(i + SLOTS - 1 < last - first)
        def _():
            fetch(first + i + SLOTS - 1, lax.rem(i + SLOTS - 1, SLOTS)).start()

        use(i, m.wbuf[slot])

    loop(last - first, body)


def tile_chain(place, links, m, k, value, left, right, zplan, out, region):
    late, tile, land = getattr(m, f"late{k}"), getattr(m, f"tile{k}"), getattr(m, f"land{k}")
    quarter = late.shape[2]
    c, q = place.c, place.q
    core, _ = place.near(0, 0, 1)

    def cut(quart):
        return value.at[:, pl.ds(mult(quart * quarter, LANES), quarter)]

    def pass_on(quart):
        slot = late.at[quart * 2 + c]
        return links.copy(slot, slot, core)

    sent = []
    for dx, dy in ((1, 0), (0, 1), (1, 1)):
        to, quart = place.near(dx, dy, 0)
        sent.append((links.copy(cut(quart), late.at[q * 2 + c], to), quart))
    late[q * 2 + c] = cut(q)[...]
    passed = [pass_on(q)]
    yield
    for copy, quart in sent:
        copy.wait_recv()
        passed.append(pass_on(quart))
    yield
    for copy in passed:
        copy.wait_recv()
    for i in range(4):
        part = matmul(left(i), right(i), ((0,), (0,)))
        tile[...] = part if i == 0 else tile[...] + part
    yield from reduce_rows(place, links, zplan, tile, land, lambda row, rows: region(q, c, row, rows))

    def mine(quart):
        return region(quart, c, 0, tile.shape[0])

    def give(quart, to):
        part = mine(quart)
        return links.copy(part, part, to)

    first, q1 = place.near(1 - c, c, 0)
    second, q2 = place.near(c, 1 - c, 0)
    _, q3 = place.near(1, 1, 0)
    a, b, across = give(q, first), give(q, second), [give(q, core)]
    yield
    a.wait_recv()
    d = give(q1, second)
    across.append(give(q1, core))
    yield
    b.wait_recv()
    across.append(give(q2, core))
    yield
    d.wait_recv()
    across.append(give(q3, core))
    yield
    for copy in across:
        copy.wait_recv()


def block_kernel(sizes, names, *refs):
    m = Refs()
    for name, ref in zip(ARGS + OUTS + names, refs):
        setattr(m, name, ref)
    place = Place(sizes)
    links = Links(m.send, m.recv)
    s, b, c, q = place.s, place.b, place.c, place.q
    count = sizes["seq"]
    tokens, width = m.x.shape
    inner, n = m.a2.shape[1], m.a2.shape[0]
    rank = m.step_proj.shape[0]
    taps = m.conv_w.shape[0]
    part = width // 2
    last = s == count - 1

    bar = pltpu.get_barrier_semaphore()
    greet = [place.near(*d)[0] for d in GROUP] + [(p, b) for p in carry_peers(count, s)]
    greet += [(lax.rem(s + 1, count), b), (lax.rem(s + count - 1, count), b)]
    for to in greet:
        pl.semaphore_signal(bar, inc=1, device_id=to, device_id_type=MESH)
    fetch_out = pltpu.make_async_copy(m.w_out, m.w_out_v, m.osem)
    fetch_out.start()

    x = m.x[...]
    rms = lax.rsqrt(jnp.mean(x * x, axis=1, keepdims=True) + EPSILON)
    m.normed[...] = x * rms * m.gain[...]
    pl.semaphore_wait(bar, len(greet))
    slot = q * 2 + c
    early = []
    for d in GROUP:
        to, _ = place.near(*d)
        half = pl.ds(mult((c + d[2] * (1 - 2 * c)) * part, LANES), part)
        early.append(links.copy(m.normed.at[:, half], m.ng.at[slot], to))
        early.append(links.copy(m.g.at[:, half], m.gg.at[slot], to))
    own = pl.ds(mult(c * part, LANES), part)
    m.ng[slot] = m.normed[:, own]
    m.gg[slot] = m.g[:, own]

    left = stacked(m.normed[...])
    half_blocks = inner // WBLOCK

    def to_hidden(i, w):
        m.hid[pl.ds(8, tokens), pl.ds(mult(i * WBLOCK, WBLOCK), WBLOCK)] = rows_matmul(left, w, ((1,), (0,)))

    stream(m, (0, half_blocks), to_hidden)
    halo = links.copy(m.hid.at[pl.ds(tokens, 8)], m.hid.at[pl.ds(0, 8)], (lax.rem(s + 1, count), b), start=False)

    @pl.when(jnp.logical_not(last))
    def _():
        halo.start()

    def to_gate(i, w):
        m.gate[:, pl.ds(mult(i * WBLOCK, WBLOCK), WBLOCK)] = rows_matmul(left, w, ((1,), (0,)))

    stream(m, (half_blocks, 2 * half_blocks), to_gate)

    fetch_out.wait()
    g_left = stacked(m.g[...])

    def to_d_res(i):
        cols = pl.ds(mult(i * WBLOCK, WBLOCK), WBLOCK)
        d = rows_matmul(g_left, m.w_out_v[cols], ((1,), (1,)))
        z = m.gate[:, cols]
        sg = sigmoid(z)
        m.d_res[:, cols] = d * (z * sg)
        m.d_gate[:, cols] = d * (sg * (1.0 + z * (1.0 - sg)))

    loop(half_blocks, to_d_res)

    @pl.when(s > 0)
    def _():
        halo.wait_recv()

    @pl.when(s == 0)
    def _():
        m.hid[pl.ds(0, 8)] = jnp.zeros((8, inner), f32)

    def convolve(i):
        at = pl.ds(mult(i * 8, 8), 8)
        window = m.hid[pl.ds(mult(i * 8, 8), 16)]
        v = m.conv_b[...]
        for k in range(taps):
            o = 8 - taps + 1 + k
            v = v + m.conv_w[k : k + 1] * window[o : o + 8]
        m.conv[at] = v
        m.mixed[at] = v * sigmoid(v)

    loop(tokens // 8, convolve)

    proj = matmul(m.mixed[...], m.x_proj[...], ((1,), (1,)))
    m.proj[:, : proj.shape[1]] = proj
    low_rank = proj[:, :rank]
    for j in range(n):
        at = pl.ds(j, tokens, stride=n)
        m.bb[at] = jnp.broadcast_to(proj[:, rank + j : rank + j + 1], (tokens, LANES))
        m.cc[at] = jnp.broadcast_to(proj[:, rank + n + j : rank + n + j + 1], (tokens, LANES))
    low_left = stacked(low_rank)

    def to_step(i):
        cols = pl.ds(mult(i * WBLOCK, WBLOCK), WBLOCK)
        pre = rows_matmul(low_left, m.step_proj[:, cols], ((1,), (0,))) + (m.step_b[:, cols] - 0.5 * m.code[:, cols].astype(f32))
        step = jnp.maximum(pre, 0.0) + jnp.log1p(jnp.exp(-jnp.abs(pre)))
        m.pre[:, cols] = pre
        m.step[:, cols] = step
        m.u[:, cols] = step * m.mixed[:, cols]

    loop(half_blocks, to_step)

    blocks = [slice(k, k + SCAN) for k in range(0, inner, SCAN)]
    for lanes in blocks:
        scan_ends(m, lanes)
    carry(place, links, m.ends, m.edges, m.got, m.back)
    for lanes in blocks:
        scan_out(m, lanes)

    def to_gated(i):
        at = pl.ds(mult(i * 8, 8), 8)
        result = m.y[at] + m.skip[...] * m.mixed[at]
        z = m.gate[at]
        m.gated[at] = result * (z * sigmoid(z))
        m.d_gate[at] = m.d_gate[at] * result

    loop(tokens // 8, to_gated)

    s_bits, b_bits = all_bits(sizes)
    zplan = [(k, k) for k in s_bits[1:] + b_bits[2:]]
    quarter = inner // 4

    def pair(ref):
        return lambda i: ref[pl.ds(2 * i, 2)].reshape(2 * tokens, ref.shape[2])

    def out_region(quart, half, row, rows):
        return m.out_sum.at[pl.ds(mult(quart * quarter + row, 8), rows), pl.ds(mult(half * part, LANES), part)]

    def in_region(base):
        return lambda quart, half, row, rows: m.in_sum.at[
            pl.ds(mult(half * part + row, 8), rows), pl.ds(mult(base + quart * quarter, LANES), quarter)]

    def chain(k, value, left, right, region):
        return tile_chain(place, links, m, k, value, pair(left), pair(right), zplan, None, region)

    chains = []

    def go(*which):
        for w in which:
            if w < len(chains) and chains[w] is not None:
                try:
                    next(chains[w])
                except StopIteration:
                    chains[w] = None

    chains.append(chain(0, m.gated, m.late0, m.gg, out_region))
    go(0)
    chains.append(chain(1, m.d_gate, m.ng, m.late1, in_region(inner)))
    go(1)

    scan_back(m, blocks[0], True)
    go(0, 1)
    for e in early:
        e.wait_recv()
    scan_back(m, blocks[1], False)
    go(0)
    scan_back(m, blocks[2], False)
    go(1)

    column = lax.broadcasted_iota(jnp.int32, (tokens, LANES), 1)

    def collect(ref, base, total):
        for j in range(n):
            rows = jnp.sum(ref[pl.ds(j, tokens, stride=n)], axis=1, keepdims=True)
            total = total + jnp.where(column == base + j, rows, 0.0)
        return total

    bc_grad = collect(m.cg, rank + n, collect(m.bg, rank, jnp.zeros((tokens, LANES), f32)))

    def to_pre_grad(i, total):
        at = pl.ds(pl.multiple_of(i * 8, 8), 8)
        v = m.sg[at] * sigmoid(m.pre[at])
        m.sg[at] = v
        return total[0] + v, total[1] + m.d_res[at] * m.mixed[at]

    zero = jnp.zeros((8, inner), f32)
    total = lax.fori_loop(0, tokens // 8, to_pre_grad, (zero, zero))
    bias_grad, skip_grad = (jnp.sum(v, axis=0, keepdims=True) for v in total)
    pre_grad = m.sg[...]
    low_grad = matmul(pre_grad, m.step_proj[...], ((1,), (1,)))
    proj_grad = jnp.concatenate([low_grad, bc_grad[:, rank : rank + 2 * n]], axis=1)

    def put_small(row, value):
        rows = value.shape[0]
        cut, top = SMALL[1], 80
        m.small[row : row + rows] = value[:, :cut]
        over = inner - cut
        if row < top:
            m.small[2 * top + row : 2 * top + row + rows, :over] = value[:, cut:]
        else:
            m.small[top + row : top + row + rows, over:] = value[:, cut:]

    go(0)
    put_small(0, matmul(proj_grad, m.mixed[...], ((0,), (0,))))
    put_small(rank + 2 * n, matmul(m.proj[:, :rank], pre_grad, ((0,), (0,))))
    put_small(2 * rank + 2 * n, m.rate[...] * m.a2[...] * LN2)
    go(1)

    pg_left = stacked(proj_grad)

    def to_mixed_grad(i):
        cols = pl.ds(mult(i * WBLOCK, WBLOCK), WBLOCK)
        d = rows_matmul(pg_left, m.x_proj[:, cols], ((1,), (0,)))
        v = m.conv[:, cols]
        sg = sigmoid(v)
        d = d + m.ms[:, cols] + m.d_res[:, cols] * m.skip[:, cols]
        m.cgr[pl.ds(0, tokens), cols] = d * (sg * (1.0 + v * (1.0 - sg)))

    loop(half_blocks, to_mixed_grad)
    halo_back = links.copy(m.cgr.at[pl.ds(0, 8)], m.cgr.at[pl.ds(tokens, 8)], (lax.rem(s + count - 1, count), b), start=False)

    @pl.when(s > 0)
    def _():
        halo_back.start()

    def to_taps(i, total):
        at = pl.ds(pl.multiple_of(i * 8, 8), 8)
        window = m.hid[pl.ds(pl.multiple_of(i * 8, 8), 16)]
        v = m.cgr[at]
        o = 8 - taps + 1
        return tuple(t + v * window[o + k : o + k + 8] for k, t in enumerate(total[:-1])) + (total[-1] + v,)

    total = lax.fori_loop(0, tokens // 8, to_taps, (zero,) * (taps + 1))
    tap_rows = [jnp.sum(v, axis=0, keepdims=True) for v in total]
    go(0)

    @pl.when(jnp.logical_not(last))
    def _():
        halo_back.wait_recv()

    @pl.when(last)
    def _():
        m.cgr[pl.ds(tokens, 8)] = jnp.zeros((8, inner), f32)

    def to_x_grad(i):
        window = m.cgr[pl.ds(mult(i * 8, 8), 16)]
        v = m.conv_w[0:1] * window[taps - 1 : taps + 7]
        for k in range(1, taps):
            o = taps - 1 - k
            v = v + m.conv_w[k : k + 1] * window[o : o + 8]
        m.x_grad[pl.ds(mult(i * 8, 8), 8)] = v

    loop(tokens // 8, to_x_grad)
    chains.append(chain(2, m.x_grad, m.ng, m.late2, in_region(0)))
    go(2, 1)

    m.acc[...] = jnp.zeros_like(m.acc)

    def to_normed(ref):
        def use(i, w):
            d = stacked(ref[:, pl.ds(mult(i * WBLOCK, WBLOCK), WBLOCK)])
            m.acc[...] = m.acc[...] + rows_matmul(d, w, ((1,), (1,)))

        return use

    stream(m, (0, half_blocks), to_normed(m.x_grad))
    go(0, 2, 1)
    stream(m, (half_blocks, 2 * half_blocks), to_normed(m.d_gate))
    x = m.x[...]
    rms = lax.rsqrt(jnp.mean(x * x, axis=1, keepdims=True) + EPSILON)
    normed_grad = m.acc[...]
    gain_grad = jnp.sum(normed_grad * x * rms, axis=0, keepdims=True)
    weighted = normed_grad * m.gain[...]
    m.input_grad[...] = rms * weighted - rms * rms * rms * x * jnp.mean(weighted * x, axis=1, keepdims=True) + m.g[...]
    rows = tap_rows + [bias_grad, skip_grad, jnp.concatenate([gain_grad, jnp.zeros((1, inner - width), f32)], axis=1)]
    put_small(2 * rank + 3 * n, jnp.concatenate(rows, axis=0))
    end = 2 * rank + 3 * n + 8
    m.small[end:160] = jnp.zeros((160 - end, SMALL[1]), f32)
    m.small[240:256] = jnp.zeros((16, SMALL[1]), f32)
    m.small[80 + end : 240, SMALL[1] // 2 :] = jnp.zeros((160 - end, SMALL[1] // 2), f32)
    chains.append(reduce_rows(place, links, small_plan(sizes), m.small, m.small_land, lambda row, rows: m.small_sum.at[pl.ds(mult(row, 8), rows)]))
    go(3, 0, 2, 1)

    gl = stacked(m.gated[...])

    def to_out(i):
        cols = pl.ds(mult(i * WBLOCK, WBLOCK), WBLOCK)
        m.block_out[:, cols] = m.x[:, cols] + rows_matmul(gl, m.w_out_v[:, cols], ((1,), (0,)))

    loop(width // WBLOCK, to_out)
    while any(v is not None for v in chains):
        go(0, 1, 3, 2)

    @pl.when(jnp.logical_not(last))
    def _():
        halo.wait_send()

    @pl.when(s > 0)
    def _():
        halo_back.wait_send()

    links.drain()


def unpack_kernel(rank, n, a_v, b_v, c_v, d_v, small, a_o, b_o, c_o, d_o, x_proj_o, step_proj_o, decay_o, rows_o, sems):
    copies = [pltpu.make_async_copy(v, o, sems.at[i]) for i, (v, o) in enumerate(((a_v, a_o), (b_v, b_o), (c_v, c_o), (d_v, d_o)))]
    for c in copies:
        c.start()

    def take(row, rows):
        over = SMALL[1] // 2
        if row < 80:
            tail = small[160 + row : 160 + row + rows, :over]
        else:
            tail = small[80 + row : 80 + row + rows, over:]
        return jnp.concatenate([small[row : row + rows], tail], axis=1)

    x_proj_o[...] = take(0, rank + 2 * n)
    step_proj_o[...] = take(rank + 2 * n, rank)
    decay_o[...] = take(2 * rank + 2 * n, n)
    rows_o[...] = take(2 * rank + 3 * n, 8)
    for c in copies:
        c.wait()


VMEM = pl.BlockSpec(memory_space=pltpu.VMEM)
ANY = pl.BlockSpec(memory_space=pl.ANY)


def shards(sizes, inputs, norm_gain, w_in, conv_weight, conv_bias, x_proj, step_proj, step_bias, decay_code, decay_log,
           skip_gain, w_out, cotangent):
    seqs, tokens, width = inputs.shape
    assert seqs == 1 and sizes["batch"] == 4 and sizes["seq"] % 2 == 0
    inner = w_in.shape[1] // 2
    rank, n, taps = step_proj.shape[0], decay_log.shape[1], conv_weight.shape[0]
    row = lambda v: v.reshape(1, -1)
    sh = scratch(sizes, tokens, width, inner, n, rank)
    args = dict(
        x=inputs[0], g=cotangent[0], gain=row(norm_gain), w_in=w_in, conv_w=conv_weight, conv_b=row(conv_bias), x_proj=x_proj.T,
        step_proj=step_proj, step_b=row(step_bias), code=row(decay_code), a2=(-LOG2E * jnp.exp(decay_log)).T, skip=row(skip_gain),
        w_out=w_out)
    held = [pltpu.VMEM(v, f32) for v in ((tokens, width), (tokens, width), (width, 2 * inner), (inner, width), SMALL)]
    sums = pl.pallas_call(
        functools.partial(block_kernel, sizes, list(sh)),
        in_specs=[ANY if a in ("w_in", "w_out") else VMEM for a in ARGS],
        out_specs=[VMEM] * 5,
        out_shape=held,
        scratch_shapes=list(sh.values()),
        compiler_params=pltpu.CompilerParams(collective_id=1, has_side_effects=True, vmem_limit_bytes=VLIMIT << 20),
        name="block",
    )(*(args[a] for a in ARGS))
    wanted = [v.shape for v in sums[:4]] + [(rank + 2 * n, inner), (rank, inner), (n, inner), (8, inner)]
    block_out, input_grad, in_sum, out_sum, x_proj_sum, step_proj_sum, decay_sum, rows = pl.pallas_call(
        functools.partial(unpack_kernel, rank, n),
        in_specs=[VMEM] * 5,
        out_specs=[ANY] * 4 + [VMEM] * 4,
        out_shape=[jax.ShapeDtypeStruct(v, f32) for v in wanted],
        scratch_shapes=[pltpu.SemaphoreType.DMA((4,))],
        compiler_params=pltpu.CompilerParams(vmem_limit_bytes=VLIMIT2 << 20),
        name="unpack",
    )(*sums)
    return (block_out[None], input_grad[None], rows[7, :width], in_sum, rows[:taps], rows[taps], x_proj_sum.T, step_proj_sum,
            rows[taps + 1], decay_sum.T, rows[taps + 2], out_sum)


VLIMIT, VLIMIT2 = 47, 8


def solution(mesh):
    rows = P("batch", "seq", None)
    return jax.shard_map(
        functools.partial(shards, dict(mesh.shape)),
        mesh=mesh,
        in_specs=(rows,) + (P(),) * 11 + (rows,),
        out_specs=(rows, rows) + (P(),) * 10,
        check_vma=False,
    )
```

time: 2130 us -> 240 us (0.11); the launches traced: 2100 us -> 236 us
  local copies, waits for them, and re-layouts: 1010 us -> 8.31 us
  waiting for transfers between devices: 482 us -> 0 us
  other arithmetic: 379 us -> 1.55 us
  Pallas kernels: 0 us -> 225 us
  blocking collectives: 144 us -> 0 us
  matrix products: 65.3 us -> 0 us
    pad x192 -> x0, local copies, waits for them, and re-layouts: 811 us -> none  [block_states(): lax.associative_scan(pair_combine, (factor, source), axis=0)]
    psum x1 -> x0, waiting for transfers between devices: 481 us -> none  [shards(): lax.psum((gain_grad, in_grad, tap_grads, conv_bias_grad, x_proj_grad, ste...]
    pallas_call x0 -> x2, Pallas kernels: none -> 225 us  [the longest x1 219 us: shards(): pl.pallas_call(functools.partial(block_kernel, sizes, list(sh)), in_specs...]
    add x215 -> x0, other arithmetic: 223 us -> none  [the longest x96 105 us: pair_combine(): return (first[0] * second[0], first[1] * second[0] + second[1])]
    all_gather x3 -> x0, blocking collectives: 81.3 us -> none  [prefix(): pieces = jax.tree.map(lambda part: lax.all_gather(part, axis), value)]
    reduce_sum x24 -> x0, other arithmetic: 72.2 us -> none  [the longest x4 27 us: local_block(): output = jnp.sum(held * c_blk[:, :, :, None], axis=2)]
    dot_general x12 -> x0, matrix products: 65.3 us -> none  [matmul(): jnp.dot(left, right, precision=MATMUL_ACCURACY, preferred_element_type=jn...]
    psum x1 -> x0, blocking collectives: 62.5 us -> none  [shards(): lax.psum((gain_grad, in_grad, tap_grads, conv_bias_grad, x_proj_grad, ste...]
  transfers between devices with their start and end apart: 3 -> 0, of which waited for: 2 -> 0; matrix products, arithmetic and copies ran while one was open for 1% -> 0% of each run, Pallas kernels for 0% -> 0%
where the time goes in v3:
time: 240 us; the launch traced here: 236 us
  Pallas kernels  225 us (94%)
  local copies, waits for them, and re-layouts  8.31 us (3%)
    pallas_call x1, Pallas kernels, shards(): pl.pallas_call(functools.partial(block_kernel, sizes, list(sh)), in_specs...  219 us
    pallas_call x1, Pallas kernels, shards(): pl.pallas_call(functools.partial(unpack_kernel, rank, n), in_specs=[VMEM]...  6.49 us
    reshape x5, local copies, waits for them, and re-layouts, shards(): row = lambda v: v.reshape(1, -1)  6.44 us

profile of v3, /device:TPU:1, one launch (start us, length us, event | category | flops | bytes accessed | tf_op | source)
XLA Modules:
  0.0 235.6 jit_solution(7479636445527902794)
XLA Ops:
  0.6 1.3 reshape.39.refs_2_
  1.9 1.3 reshape.40.refs_5_
  3.2 1.3 reshape.41.refs_8_
  4.5 1.3 reshape.42.refs_9_
  5.8 1.3 reshape.43.refs_11_
  7.1 1.6 multiply_bitcast_fusion.refs_10_
  8.6 218.6 %block.1 = (f32[128,768]{1,0:T(8,128)S(1)}, f32[128,768]{1,0:T(8,128)S(1)}, f32[768,3072]{1,0:T(8,128)S(1)}, f32[1536,768]{1,0:T(8,128)S(1)}, f32[256,1024]{1,0:T(8,128)S(1)}) custom-call(f32[128,768]{1,0:T(8,128)} %bitcast.10, f32[128,768]{1,0:T(8,128)} %bitcast.11, f32[1,768]{1,0:T(1,128)} %reshape.39.refs_2_, f32[768,3072]{1,0:T(8,128)} %refs_3_.1, ...), custom_call_target="tpu_custom_call" | custom-call | tf_op jit(solution)/shard_map/block/pallas_call | solution.py:813
  227.3 6.5 %unpack.1 = (f32[128,768]{1,0:T(8,128)}, f32[128,768]{1,0:T(8,128)}, f32[768,3072]{1,0:T(8,128)}, f32[1536,768]{1,0:T(8,128)}, f32[80,1536]{1,0:T(8,128)}, /*ind...) custom-call(f32[128,768]{1,0:T(8,128)S(1)} %get-tuple-element.25.a_v, ...), custom_call_target="tpu_custom_call" | custom-call | tf_op jit(solution)/shard_map/unpack/pallas_call | solution.py:823
  233.8 0.6 slice_reduce_fusion.3
  234.4 0.6 slice.16
  235.0 0.7 slice_reduce_fusion

commit v4 on v3

v4 whole, which is shorter than its diff:
```python
import functools

import jax
import jax.numpy as jnp
from jax import lax
from jax.experimental import pallas as pl
from jax.experimental.pallas import tpu as pltpu
from jax.sharding import PartitionSpec as P

f32 = jnp.float32
bf16 = jnp.bfloat16
MESH = pl.DeviceIdType.MESH
EPSILON = 1e-05
LOG2E = 1.4426950408889634
LN2 = 0.6931471805599453
LANES = 128
SCAN = 512
WBLOCK = 256
SLOTS = 4
SMALL = (256, 1024)
PARTS = {"o": 2, "i": 4, "x": 4}
SPREAD = {"o0": "T3", "x0": "T3"}
COPIES = 250
ORDER = [
    "gated", "back0", "back1", "back2", "i", "o", "pre", "i", "i3", "i2", "o", "i0", "o0", "i1", "o1", "mixg",
    "xg", "taps", "mid", "ng0", "i3", "i2", "i0", "i1", "ng1", "inp", "bo", "i3", "o0", "o1", "i2", "i0",
    "i1", "s", "x", "x", "i3", "x1", "x2", "x3", "s", "x0", "i2", "i0", "i1", "o0", "o1", "i3",
    "i2", "i0", "i1", "i3", "s", "x1", "x2", "o0", "x3", "o1", "x0", "i2", "i0", "i1", "i3", "i3",
    "s", "x1", "x2", "x3", "o0", "x0", "o1", "i2", "i2", "s", "i0", "i0", "i3", "i1", "i1", "i3",
    "x1", "o0", "x2", "o0", "x3", "o1", "s", "i2", "x0", "i0", "i1", "x1", "i2", "i0", "i1", "o0",
    "x2", "x3", "s", "x0", "o1", "o1", "x1", "x0", "x0", "x2", "x3", "s", "x0", "x1", "x1", "o0",
    "x2", "x2", "x3", "x3", "o1", "o0", "x0", "o1", "x1", "s", "x0", "x1", "x2", "x3", "s", "x2",
    "x3",
]


def mult(value, by):
    return value if isinstance(value, int) else pl.multiple_of(value, by)


def split(value):
    high = value.astype(bf16)
    return high, (value - high.astype(f32)).astype(bf16)


def dot(a, b, dims):
    return lax.dot_general(a, b, (dims, ((), ())), preferred_element_type=f32)


def matmul(a, b, dims=((1,), (0,))):
    (ah, al), (bh, bl) = split(a), split(b)
    return dot(ah, bh, dims) + dot(al, bh, dims) + dot(ah, bl, dims)


def stacked(value):
    return jnp.concatenate(split(value), axis=0)


def rows_matmul(both, b, dims):
    rows = both.shape[0] // 2
    bh, bl = split(b)
    wide = dot(both, bh, dims)
    return wide[:rows] + wide[rows:] + dot(both[:rows], bl, dims)


def sigmoid(v):
    return 1.0 / (1.0 + jnp.exp(-v))


def loop(count, body):
    def step(i, _):
        body(i)
        return 0

    lax.fori_loop(0, count, step, 0)


class Place:
    def __init__(self, sizes):
        self.sizes = sizes
        self.s, self.b = lax.axis_index("seq"), lax.axis_index("batch")
        self.at = {"seq": self.s, "batch": self.b}
        self.x, self.c, self.y = self.s % 2, self.b % 2, self.b // 2
        self.odd = self.c

    def near(self, dx, dy, dc):
        dx, dy = dx * (1 - 2 * self.x), dy * (1 - 2 * self.y)
        return (self.s + dx, self.b + dc * (1 - 2 * self.c) + 2 * dy), (self.x + dx, self.y + dy)

    def bit(self, d):
        return self.at[d[0]] // (1 << d[1]) % 2

    def stage(self, pair):
        to = dict(self.at)
        first, second = pair
        if first == second:
            v = self.bit(first)
            to[first[0]] = to[first[0]] + (1 - 2 * v) * (1 << first[1])
        else:
            va, vb = self.bit(first), self.bit(second)
            to[first[0]] = to[first[0]] + (1 - self.odd) * (1 - 2 * va) * (1 << first[1])
            to[second[0]] = to[second[0]] + self.odd * (1 - 2 * vb) * (1 << second[1])
            v = (1 - self.odd) * va + self.odd * vb
        return (to["seq"], to["batch"]), v


class Links:
    def __init__(self, send, recv):
        self.send, self.recv, self.used, self.open = send, recv, 0, []

    def copy(self, src, dst, to, start=True):
        i = self.used
        self.used += 1
        c = pltpu.make_async_remote_copy(
            src_ref=src, dst_ref=dst, send_sem=self.send.at[i], recv_sem=self.recv.at[i], device_id=to, device_id_type=MESH
        )
        if start:
            c.start()
            self.open.append(c)
        return c

    def sent(self, copy):
        copy.wait_send()
        self.open = [c for c in self.open if c is not copy]

    def drain(self):
        for c in self.open:
            c.wait_send()
        self.open = []


GROUP = [(1, 0, 0), (1, 0, 1), (0, 1, 0), (0, 1, 1), (0, 0, 1)]


def log2(size):
    return size.bit_length() - 1


def all_bits(sizes):
    s = [("seq", k) for k in range(log2(sizes["seq"]))]
    b = [("batch", k) for k in range(log2(sizes["batch"]))]
    return s, b


def small_plan(sizes):
    s, b = all_bits(sizes)
    return [(b[0], b[0]), (s[0], b[1]), (b[1], s[0])] + [(q, q) for q in s[1:] + b[2:]]


def halvings(rows, stages):
    out = []
    for _ in range(stages):
        ok = rows % 16 == 0
        out.append(ok)
        rows = rows // 2 if ok else rows
    return out


def landing_rows(rows, stages):
    total = 0
    for ok in halvings(rows, stages):
        rows = rows // 2 if ok else rows
        total += rows
    return total


def reduce_rows(place, links, plan, acc, land, kept):
    rows = acc.shape[0]
    off, base = 0, 0
    for pair, ok in zip(plan, halvings(rows, len(plan))):
        to, v = place.stage(pair)
        parent = off
        if ok:
            rows //= 2
            off, give = off + v * rows, off + (1 - v) * rows
        else:
            give = off
        copy = links.copy(acc.at[pl.ds(mult(give, 8), rows)], land.at[pl.ds(base, rows)], to)
        yield
        copy.wait_recv()
        if not ok:
            links.sent(copy)

        def add(i, off=off, base=base):
            at = pl.ds(mult(off + i * 8, 8), 8)
            acc[at] = acc[at] + land[pl.ds(mult(base + i * 8, 8), 8)]

        loop(rows // 8, add)
        base += rows
        if ok:
            kept.append((to, parent, off, rows))
    return off, rows


def place_rows(acc, off, rows, whole):
    def one(i):
        whole(off + i * 8, 8)[...] = acc[pl.ds(mult(off + i * 8, 8), 8)]

    loop(rows // 8, one)


def small_chain(place, links, plan, acc, land, out):
    whole = lambda row, rows: out.at[pl.ds(mult(row, 8), rows)]
    kept = []
    off, rows = yield from reduce_rows(place, links, plan, acc, land, kept)
    place_rows(acc, off, rows, whole)
    for to, _, off, rows in reversed(kept):
        copy = links.copy(whole(off, rows), whole(off, rows), to)
        yield
        copy.wait_recv()


def tiled(count):
    return count in (2, 4, 6, 8, 12, 24)


def carry_peers(count, s):
    if tiled(count):
        return [lax.rem(s + i, count) for i in range(1, count)]
    return [s + (1 - 2 * (s // (1 << k) % 2)) * (1 << k) for k in range(log2(count))]


def carry_scratch(count, n, inner):
    v = lambda *shape: pltpu.VMEM(shape, f32)
    if tiled(count):
        w = inner // (count // 2)
        return dict(got=v(count, 2, 8, w), back=v(count, 2, 8, w), got_sum=v(count, 1, w), tile_dec=v(count, 8, w))
    return dict(got=v(2 * log2(count), 2, n, inner), back=v(2, n, inner), tot=v(2, n, inner))


def carry(place, links, m, way):
    return (carry_tiles if tiled(place.sizes["seq"]) else carry_doubling)(place, links, m, way)


def carry_doubling(place, links, m, way):
    bits = log2(place.sizes["seq"])
    m.edges[way] = jnp.zeros_like(m.edges[way])
    m.back[way] = jnp.ones_like(m.back[way])
    m.tot[0] = m.ends[way]
    m.tot[1] = jnp.exp2(m.a2[...] * m.sums[...])
    for k, p in enumerate(carry_peers(place.sizes["seq"], place.s)):
        got = m.got.at[way * bits + k]
        copy = links.copy(m.tot, got, (p, place.b))
        copy.wait_recv()
        links.sent(copy)
        later = place.bit(("seq", k))

        @pl.when(later == 1 - way)
        def _():
            m.edges[way] += m.back[way] * got[0]
            m.back[way] *= got[1]
            m.tot[0] += m.tot[1] * got[0]

        @pl.when(later == way)
        def _():
            m.tot[0] = got[0] + got[1] * m.tot[0]

        m.tot[1] *= got[1]
    yield
    yield


def carry_tiles(place, links, m, way):
    count, s, b = place.sizes["seq"], place.s, place.b
    across = count // 2
    width = m.ends.shape[2] // across
    peers = carry_peers(count, s)

    def cut(ref, p):
        return ref.at[pl.ds(mult(p // across * 8, 8), 8), pl.ds(mult(p % across * width, LANES), width)]

    def cut_sum(p):
        return m.sums.at[:, pl.ds(mult(p % across * width, LANES), width)]

    first = [links.copy(cut(m.ends.at[way], p), m.got.at[s, way], (p, b)) for p in peers]
    m.got[s, way] = cut(m.ends.at[way], s)[...]
    if way == 0:
        first += [links.copy(cut_sum(p), m.got_sum.at[s], (p, b)) for p in peers]
        m.got_sum[s] = cut_sum(s)[...]
    yield
    for c in first:
        c.wait_recv()
    if way == 0:
        a2 = cut(m.a2, s)[...]
        for p in range(count):
            m.tile_dec[p] = jnp.exp2(a2 * m.got_sum[p])
    value = jnp.zeros((8, width), f32)
    for p in reversed(range(count)) if way else range(count):
        m.back[p, way] = value
        value = m.got[p, way] + m.tile_dec[p] * value
    second = [links.copy(m.back.at[p, way], cut(m.edges.at[way], s), (p, b)) for p in peers]
    cut(m.edges.at[way], s)[...] = m.back[s, way]
    yield
    for c in second:
        c.wait_recv()


def wide(tile):
    return jnp.concatenate([tile] * (SCAN // LANES), axis=1)


def spread(row, n):
    return jnp.broadcast_to(row, (n, row.shape[1]))


def fold(value):
    return sum(value[:, k : k + LANES] for k in range(0, value.shape[1], LANES))


def scan_ends(m, lanes):
    a2 = m.a2[:, lanes]
    n = a2.shape[0]

    def chunk(i, h):
        at = pl.ds(pl.multiple_of(i * 8, 8), 8)
        s8, u8 = m.step[at, lanes], m.u[at, lanes]
        for j in range(8):
            b = wide(m.bb[pl.ds(pl.multiple_of((i * 8 + j) * n, 8), n)])
            h = jnp.exp2(spread(s8[j : j + 1], n) * a2) * h + spread(u8[j : j + 1], n) * b
        return h

    m.ends[0, :, lanes] = lax.fori_loop(0, m.step.shape[0] // 8, chunk, jnp.zeros_like(a2))


def scan_lams(m, lanes):
    a2 = m.a2[:, lanes]
    n = a2.shape[0]

    def chunk(i, held):
        dec, acc = held
        at = pl.ds(pl.multiple_of(i * 8, 8), 8)
        s8, d8 = m.step[at, lanes], m.d_res[at, lanes]
        for j in range(8):
            c = wide(m.cc[pl.ds(pl.multiple_of((i * 8 + j) * n, 8), n)])
            dec = dec * jnp.exp2(spread(s8[j : j + 1], n) * a2)
            acc = acc + dec * (spread(d8[j : j + 1], n) * c)
        return dec, acc

    zero = jnp.zeros_like(a2)
    m.ends[1, :, lanes] = lax.fori_loop(0, m.step.shape[0] // 8, chunk, (zero + 1.0, zero))[1]


def scan_out(m, lanes):
    a2 = m.a2[:, lanes]
    n = a2.shape[0]

    def chunk(i, h):
        at = pl.ds(pl.multiple_of(i * 8, 8), 8)
        s8, u8 = m.step[at, lanes], m.u[at, lanes]
        ys = []
        for j in range(8):
            t = pl.ds(pl.multiple_of((i * 8 + j) * n, 8), n)
            b, c = wide(m.bb[t]), wide(m.cc[t])
            h = jnp.exp2(spread(s8[j : j + 1], n) * a2) * h + spread(u8[j : j + 1], n) * b
            ys.append(jnp.sum(c * h, axis=0, keepdims=True))
        m.y[at, lanes] = jnp.concatenate(ys, axis=0)
        return h

    lax.fori_loop(0, m.step.shape[0] // 8, chunk, m.edges[0, :, lanes])


def scan_back(m, lanes, first):
    a2 = m.a2[:, lanes]
    n = a2.shape[0]
    tokens = m.step.shape[0]

    def ahead(i, h):
        at = pl.ds(pl.multiple_of(i * 8, 8), 8)
        s8, u8, d8 = m.step[at, lanes], m.u[at, lanes], m.d_res[at, lanes]
        for j in range(8):
            t = pl.ds(pl.multiple_of((i * 8 + j) * n, 8), n)
            m.h[i * 8 + j] = h
            h = jnp.exp2(spread(s8[j : j + 1], n) * a2) * h + spread(u8[j : j + 1], n) * wide(m.bb[t])
            part = fold(spread(d8[j : j + 1], n) * h)
            m.cg[t] = part if first else m.cg[t] + part
        return h

    lax.fori_loop(0, tokens // 8, ahead, m.edges[0, :, lanes])

    def behind(i, held):
        q, rate = held
        r = tokens // 8 - 1 - i
        at = pl.ds(pl.multiple_of(r * 8, 8), 8)
        s8, u8, d8 = m.step[at, lanes], m.u[at, lanes], m.d_res[at, lanes]
        sg, lb = [None] * 8, [None] * 8
        for j in reversed(range(8)):
            t = pl.ds(pl.multiple_of((r * 8 + j) * n, 8), n)
            st = spread(s8[j : j + 1], n)
            lam = spread(d8[j : j + 1], n) * wide(m.cc[t]) + q
            q = jnp.exp2(st * a2) * lam
            dec = q * m.h[r * 8 + j]
            lb[j] = jnp.sum(lam * wide(m.bb[t]), axis=0, keepdims=True)
            sg[j] = jnp.sum(dec * a2, axis=0, keepdims=True)
            rate = rate + dec * st
            part = fold(lam * spread(u8[j : j + 1], n))
            m.bg[t] = part if first else m.bg[t] + part
        lb8, sg8 = jnp.concatenate(lb, axis=0), jnp.concatenate(sg, axis=0)
        m.sg[at, lanes] = LN2 * sg8 + m.mixed[at, lanes] * lb8
        m.gate[at, lanes] = s8 * lb8
        return q, rate

    _, rate = lax.fori_loop(0, tokens // 8, behind, (m.edges[1, :, lanes], jnp.zeros_like(a2)))
    m.rate[:, lanes] = rate


class Refs:
    pass


FETCH = ["x", "gain", "g", "w_out", "conv_w", "conv_b", "x_proj", "step_proj", "step_b", "code", "a2", "skip"]
ARGS = [v + "_h" for v in FETCH] + ["w_in"]
OUTS = ["block_out", "input_grad", "in_sum", "out_sum", "small_sum"]


def pieces(key):
    return (PARTS[key], 1) if key == "o" else {1: (1, 1), 2: (1, 2), 4: (2, 2)}[PARTS[key]]


def scratch(sizes, tokens, width, inner, n, rank, taps):
    full = (tokens, inner)
    half, part = inner // 2, width // 2
    stages = log2(sizes["seq"])
    v = lambda *shape: pltpu.VMEM(shape, f32)
    sh = {name: v(*full) for name in ("gate", "d_res", "conv", "mixed", "pre", "step", "u", "y", "d_gate", "sg")}
    sh.update(
        x=v(tokens, width), g=v(tokens, width), vec=v(4, inner), gain=v(width // LANES, LANES),
        conv_b=v(inner // LANES, LANES), step_b=v(inner // LANES, LANES), skip=v(inner // LANES, LANES),
        code=pltpu.VMEM((inner // LANES, LANES), jnp.int32), conv_w=v(taps, inner), x_proj=v(rank + 2 * n, inner),
        step_proj=v(rank, inner), a2=v(n, inner), w_out=v(inner, width),
        normed=v(tokens, width), hid=v(8 + tokens, inner), cgr=v(tokens + 8, inner), proj=v(tokens, LANES),
        wbuf=v(SLOTS, width, WBLOCK), acc=v(tokens, width),
        bb=v(tokens * n, LANES), cc=v(tokens * n, LANES), bg=v(tokens * n, LANES), cg=v(tokens * n, LANES),
        h=v(tokens, n, SCAN), rate=v(n, inner), ends=v(2, n, inner), edges=v(2, n, inner), sums=v(1, inner),
        ng=v(4, tokens, part), gg=v(4, tokens, part),
        small=v(*SMALL), small_land=v(landing_rows(SMALL[0], len(small_plan(sizes))), SMALL[1]),
    )
    for key in "oix":
        rows, cols = (half, part) if key == "o" else (part, half)
        down, over = pieces(key)
        sh["late_" + key] = v(4, tokens, half)
        for k in range(down * over):
            sh[f"tile_{key}{k}"] = v(rows // down, cols // over)
            sh[f"land_{key}{k}"] = v(landing_rows(rows // down, stages), cols // over)
    sh.update(carry_scratch(sizes["seq"], n, inner))
    sh["send"], sh["recv"] = [pltpu.SemaphoreType.DMA((COPIES,))] * 2
    sh["wsem"] = pltpu.SemaphoreType.DMA((SLOTS,))
    sh["isem"] = pltpu.SemaphoreType.DMA((len(FETCH),))
    return sh


def stream(m, first, last):
    def fetch(i, slot):
        cols = pl.ds(mult((first + i) * WBLOCK, WBLOCK), WBLOCK)
        return pltpu.make_async_copy(m.w_in.at[:, cols], m.wbuf.at[slot], m.wsem.at[slot])

    ahead = SLOTS - 1
    for k in range(ahead):
        fetch(k, k).start()

    def run(use):
        def body(i):
            slot = lax.rem(i, SLOTS)
            fetch(i, slot).wait()

            @pl.when(i + ahead < last - first)
            def _():
                fetch(i + ahead, lax.rem(i + ahead, SLOTS)).start()

            use(i, m.wbuf[slot])

        loop(last - first, body)

    return run


def late_chain(place, links, m, key, value, left, right):
    late = getattr(m, "late_" + key)
    half = late.shape[2]
    mine = place.y if key == "o" else place.x
    to, _ = place.near(0, 1, 0) if key == "o" else place.near(1, 0, 0)
    core, _ = place.near(0, 0, 1)

    def cut(which):
        return value.at[:, pl.ds(mult(which * half, LANES), half)]

    def pass_on(which):
        slot = late.at[which * 2 + place.c]
        return links.copy(slot, slot, core)

    sent = links.copy(cut(1 - mine), late.at[mine * 2 + place.c], to)
    late[mine * 2 + place.c] = cut(mine)[...]
    passed = [pass_on(mine)]
    yield
    sent.wait_recv()
    passed.append(pass_on(1 - mine))
    yield
    for copy in passed:
        copy.wait_recv()
    down, over = pieces(key)
    for i in range(2):
        part = matmul(left(i), right(i), ((0,), (0,)))
        rows, cols = part.shape[0] // down, part.shape[1] // over
        for k in range(down * over):
            tile = getattr(m, f"tile_{key}{k}")
            r, c = k // over * rows, k % over * cols
            cell = part[r : r + rows, c : c + cols]
            tile[...] = cell if i == 0 else tile[...] + cell


def piece_chain(place, links, m, key, k, zplan, out, base):
    acc, land = getattr(m, f"tile_{key}{k}"), getattr(m, f"land_{key}{k}")
    rows, cols = acc.shape
    over = pieces(key)[1]
    r0, c0 = k // over * rows, k % over * cols
    half, part = out.shape[0] // 2 if key == "o" else out.shape[1] // 4, m.x.shape[1] // 2
    bit = ("seq", 0) if key == "o" else ("batch", 1)
    x, y, c = place.x, place.y, place.c
    core, _ = place.near(0, 0, 1)

    def region(at, row, count):
        xx, yy = at
        if key == "o":
            top, side = yy * half + r0 + xx * (rows // 2) + row, c * part + c0
        else:
            top, side = c * part + r0 + yy * (rows // 2) + row, base + xx * half + c0
        return out.at[pl.ds(mult(top, 8), count), pl.ds(mult(side, LANES), cols)]

    kept = []
    off, count = yield from reduce_rows(place, links, [(bit, bit)] + zplan, acc, land, kept)
    edge = kept[0][2]
    place_rows(acc, off, count, lambda row, n: region((x, y), row - edge, n))
    row = off - edge
    held, across = [(x, y)], []

    def give(at, to):
        ref = region(at, row, count)
        return links.copy(ref, ref, to)

    steps = list(reversed(kept[1:]))
    kind = SPREAD.get(key + str(k), "T1")
    steps.insert({"T1": len(steps), "T2": 0, "T3": 1}[kind], None)
    for i, step in enumerate(steps):
        last = i == len(steps) - 1
        if step is not None:
            to, parent, _, size = step
            copies = [give(at, to) for at in held]
            yield
            for copy in copies:
                copy.wait_recv()
            row, count = parent - edge, 2 * size
            continue
        first, at_a = place.near(1 - c, c, 0)
        second, at_b = place.near(c, 1 - c, 0)
        _, at_d = place.near(1, 1, 0)
        a, b = give((x, y), first), give((x, y), second)
        held = [(x, y), at_a, at_b, at_d]

        def onward(at):
            if last:
                across.append(give(at, core))

        onward((x, y))
        yield
        a.wait_recv()
        d = give(at_a, second)
        onward(at_a)
        yield
        b.wait_recv()
        onward(at_b)
        yield
        d.wait_recv()
        onward(at_d)
    if not across:
        across = [give(at, core) for at in held]
    yield
    for copy in across:
        copy.wait_recv()


def block_kernel(sizes, names, *refs):
    m = Refs()
    for name, ref in zip(ARGS + OUTS + names, refs):
        setattr(m, name, ref)
    place = Place(sizes)
    links = Links(m.send, m.recv)
    s, b, c = place.s, place.b, place.c
    count = sizes["seq"]
    tokens, width = m.x.shape
    inner, n = m.a2.shape[1], m.a2.shape[0]
    rank = m.step_proj.shape[0]
    taps = m.conv_w.shape[0]
    half, part = inner // 2, width // 2
    blocks_of_half = inner // WBLOCK
    last = s == count - 1

    fetched = {}
    for i, name in enumerate(FETCH):
        fetched[name] = pltpu.make_async_copy(getattr(m, name + "_h"), getattr(m, name), m.isem.at[i])
    for name in FETCH[:3]:
        fetched[name].start()
    to_hidden = stream(m, 0, blocks_of_half)
    for name in FETCH[3:]:
        fetched[name].start()
    bar = pltpu.get_barrier_semaphore()
    greet = [place.near(*d)[0] for d in GROUP] + [(p, b) for p in carry_peers(count, s)]
    greet += [(lax.rem(s + 1, count), b), (lax.rem(s + count - 1, count), b)]
    for to in greet:
        pl.semaphore_signal(bar, inc=1, device_id=to, device_id_type=MESH)

    fetched["x"].wait()
    fetched["gain"].wait()

    def to_row(name, k):
        ref = getattr(m, name)
        for j in range(ref.shape[0]):
            m.vec[k : k + 1, j * LANES : (j + 1) * LANES] = ref[j : j + 1]

    to_row("gain", 3)
    x = m.x[...]
    rms = lax.rsqrt(jnp.mean(x * x, axis=1, keepdims=True) + EPSILON)
    m.normed[...] = x * rms * m.vec[3:4, :width]
    fetched["g"].wait()
    pl.semaphore_wait(bar, len(greet))
    early = []
    for d in GROUP:
        to, _ = place.near(*d)
        cols = pl.ds(mult((c + d[2] * (1 - 2 * c)) * part, LANES), part)
        if not d[1]:
            early.append(links.copy(m.normed.at[:, cols], m.ng.at[place.x * 2 + c], to))
        if not d[0]:
            early.append(links.copy(m.g.at[:, cols], m.gg.at[place.y * 2 + c], to))
    own = pl.ds(mult(c * part, LANES), part)
    m.ng[place.x * 2 + c] = m.normed[:, own]
    m.gg[place.y * 2 + c] = m.g[:, own]

    left = stacked(m.normed[...])

    def hidden_block(i, w):
        m.hid[pl.ds(8, tokens), pl.ds(mult(i * WBLOCK, WBLOCK), WBLOCK)] = rows_matmul(left, w, ((1,), (0,)))

    to_hidden(hidden_block)
    to_gate = stream(m, blocks_of_half, 2 * blocks_of_half)
    halo = links.copy(m.hid.at[pl.ds(tokens, 8)], m.hid.at[pl.ds(0, 8)], (lax.rem(s + 1, count), b), start=False)

    @pl.when(jnp.logical_not(last))
    def _():
        halo.start()

    for name in FETCH[3:]:
        fetched[name].wait()
    m.step_b[...] = m.step_b[...] - 0.5 * m.code[...].astype(f32)
    for k, name in enumerate(("conv_b", "step_b", "skip")):
        to_row(name, k)
    m.a2[...] = -LOG2E * jnp.exp(m.a2[...])
    g_left = stacked(m.g[...])

    def d_gated_block(i):
        cols = pl.ds(mult(i * WBLOCK, WBLOCK), WBLOCK)
        m.d_res[:, cols] = rows_matmul(g_left, m.w_out[cols], ((1,), (1,)))

    loop(blocks_of_half, d_gated_block)

    @pl.when(s > 0)
    def _():
        halo.wait_recv()

    @pl.when(s == 0)
    def _():
        m.hid[pl.ds(0, 8)] = jnp.zeros((8, inner), f32)

    def convolve(i):
        window = m.hid[pl.ds(mult(i * 8, 8), 16)]
        v = m.vec[0:1]
        for k in range(taps):
            o = 8 - taps + 1 + k
            v = v + m.conv_w[k : k + 1] * window[o : o + 8]
        at = pl.ds(mult(i * 8, 8), 8)
        m.conv[at] = v
        m.mixed[at] = v * sigmoid(v)

    loop(tokens // 8, convolve)

    proj = matmul(m.mixed[...], m.x_proj[...], ((1,), (1,)))
    m.proj[:, : proj.shape[1]] = proj
    for j in range(n):
        at = pl.ds(j, tokens, stride=n)
        m.bb[at] = jnp.broadcast_to(proj[:, rank + j : rank + j + 1], (tokens, LANES))
        m.cc[at] = jnp.broadcast_to(proj[:, rank + n + j : rank + n + j + 1], (tokens, LANES))
    low_left = stacked(proj[:, :rank])

    def step_block(i):
        cols = pl.ds(mult(i * WBLOCK, WBLOCK), WBLOCK)
        pre = rows_matmul(low_left, m.step_proj[:, cols], ((1,), (0,))) + m.vec[1:2, cols]
        step = jnp.maximum(pre, 0.0) + jnp.log1p(jnp.exp(-jnp.abs(pre)))
        m.pre[:, cols] = pre
        m.step[:, cols] = step
        m.u[:, cols] = step * m.mixed[:, cols]
        m.sums[:, cols] = jnp.sum(step, axis=0, keepdims=True)

    loop(blocks_of_half, step_block)

    blocks = [slice(k, k + SCAN) for k in range(0, inner, SCAN)]
    for lanes in blocks:
        scan_ends(m, lanes)
    ahead = carry(place, links, m, 0)
    next(ahead)

    def gate_block(i, w):
        cols = pl.ds(mult(i * WBLOCK, WBLOCK), WBLOCK)
        z = rows_matmul(left, w, ((1,), (0,)))
        sg = sigmoid(z)
        act = z * sg
        d = m.d_res[:, cols]
        m.gate[:, cols] = act
        m.d_res[:, cols] = d * act
        m.d_gate[:, cols] = d * (sg * (1.0 + z * (1.0 - sg)))

    to_gate(gate_block)
    next(ahead)
    for lanes in blocks:
        scan_lams(m, lanes)
    behind = carry(place, links, m, 1)
    next(behind)
    for _ in ahead:
        pass
    for lanes in blocks:
        scan_out(m, lanes)
    next(behind)

    def gated_rows(i):
        at = pl.ds(mult(i * 8, 8), 8)
        result = m.y[at] + m.vec[2:3] * m.mixed[at]
        m.y[at] = result * m.gate[at]
        m.d_gate[at] = m.d_gate[at] * result

    loop(tokens // 8, gated_rows)

    s_bits, b_bits = all_bits(sizes)
    zplan = [(k, k) for k in s_bits[1:] + b_bits[2:]]
    chains, started, v = {}, set(), Refs()

    def pair(ref):
        return lambda i: ref[pl.ds(2 * i, 2)].reshape(2 * tokens, ref.shape[2])

    def go(name):
        started.add(name)
        try:
            next(chains[name])
        except StopIteration:
            del chains[name]
            if name in "oix":
                where = {"o": (m.out_sum, 0), "i": (m.in_sum, inner), "x": (m.in_sum, 0)}[name]
                for k in range(PARTS[name]):
                    chains[name + str(k)] = piece_chain(place, links, m, name, k, zplan, *where)

    def late(key, value, left, right):
        chains[key] = late_chain(place, links, m, key, value, pair(left), pair(right))
        go(key)

    column = lax.broadcasted_iota(jnp.int32, (tokens, LANES), 1)
    zero = jnp.zeros((8, inner), f32)

    def collect(ref, base, total):
        for j in range(n):
            rows = jnp.sum(ref[pl.ds(j, tokens, stride=n)], axis=1, keepdims=True)
            total = total + jnp.where(column == base + j, rows, 0.0)
        return total

    def put_small(row, value):
        rows = value.shape[0]
        cut, top = SMALL[1], 80
        m.small[row : row + rows] = value[:, :cut]
        over = inner - cut
        if row < top:
            m.small[2 * top + row : 2 * top + row + rows, :over] = value[:, cut:]
        else:
            m.small[top + row : top + row + rows, over:] = value[:, cut:]

    def gated():
        late("o", m.y, m.late_o, m.gg)
        late("i", m.d_gate, m.ng, m.late_i)
        for _ in behind:
            pass

    def back(k):
        scan_back(m, blocks[k], k == 0)
        if k == 0:
            for e in early:
                e.wait_recv()

    def pre():
        bc_grad = collect(m.cg, rank + n, collect(m.bg, rank, jnp.zeros((tokens, LANES), f32)))

        def rows(i, total):
            at = pl.ds(pl.multiple_of(i * 8, 8), 8)
            p = m.sg[at] * sigmoid(m.pre[at])
            m.sg[at] = p
            return total[0] + p, total[1] + m.d_res[at] * m.mixed[at]

        total = lax.fori_loop(0, tokens // 8, rows, (zero, zero))
        v.bias_grad, v.skip_grad = (jnp.sum(t, axis=0, keepdims=True) for t in total)
        low_grad = matmul(m.sg[...], m.step_proj[...], ((1,), (1,)))
        v.proj_grad = jnp.concatenate([low_grad, bc_grad[:, rank : rank + 2 * n]], axis=1)

    def mixg():
        pg_left = stacked(v.proj_grad)

        def block(i):
            cols = pl.ds(mult(i * WBLOCK, WBLOCK), WBLOCK)
            d = rows_matmul(pg_left, m.x_proj[:, cols], ((1,), (0,)))
            z = m.conv[:, cols]
            sg = sigmoid(z)
            d = d + m.gate[:, cols] + m.d_res[:, cols] * m.vec[2:3, cols]
            m.cgr[pl.ds(0, tokens), cols] = d * (sg * (1.0 + z * (1.0 - sg)))

        loop(blocks_of_half, block)
        v.halo_back = links.copy(
            m.cgr.at[pl.ds(0, 8)], m.cgr.at[pl.ds(tokens, 8)], (lax.rem(s + count - 1, count), b), start=False)

        @pl.when(s > 0)
        def _():
            v.halo_back.start()

    def xg():
        @pl.when(jnp.logical_not(last))
        def _():
            v.halo_back.wait_recv()

        @pl.when(last)
        def _():
            m.cgr[pl.ds(tokens, 8)] = jnp.zeros((8, inner), f32)

        def rows(i):
            window = m.cgr[pl.ds(mult(i * 8, 8), 16)]
            z = m.conv_w[0:1] * window[taps - 1 : taps + 7]
            for k in range(1, taps):
                o = taps - 1 - k
                z = z + m.conv_w[k : k + 1] * window[o : o + 8]
            m.gate[pl.ds(mult(i * 8, 8), 8)] = z

        loop(tokens // 8, rows)
        late("x", m.gate, m.ng, m.late_x)

    def taps_():
        def rows(i, total):
            at = pl.ds(pl.multiple_of(i * 8, 8), 8)
            window = m.hid[pl.ds(pl.multiple_of(i * 8, 8), 16)]
            z = m.cgr[at]
            o = 8 - taps + 1
            return tuple(t + z * window[o + k : o + k + 8] for k, t in enumerate(total[:-1])) + (total[-1] + z,)

        total = lax.fori_loop(0, tokens // 8, rows, (zero,) * (taps + 1))
        v.tap_rows = [jnp.sum(t, axis=0, keepdims=True) for t in total]

    def mid():
        put_small(0, matmul(v.proj_grad, m.mixed[...], ((0,), (0,))))
        put_small(rank + 2 * n, matmul(m.proj[:, :rank], m.sg[...], ((0,), (0,))))
        put_small(2 * rank + 2 * n, m.rate[...] * m.a2[...] * LN2)

    def normed_block(ref):
        def use(i, w):
            d = stacked(ref[:, pl.ds(mult(i * WBLOCK, WBLOCK), WBLOCK)])
            m.acc[...] = m.acc[...] + rows_matmul(d, w, ((1,), (1,)))

        return use

    def ng0():
        m.acc[...] = jnp.zeros_like(m.acc)
        stream(m, blocks_of_half, 2 * blocks_of_half)(normed_block(m.d_gate))

    def ng1():
        stream(m, 0, blocks_of_half)(normed_block(m.gate))

    def inp():
        x = m.x[...]
        rms = lax.rsqrt(jnp.mean(x * x, axis=1, keepdims=True) + EPSILON)
        normed_grad = m.acc[...]
        gain_grad = jnp.sum(normed_grad * x * rms, axis=0, keepdims=True)
        weighted = normed_grad * m.vec[3:4, :width]
        m.input_grad[...] = rms * weighted - rms * rms * rms * x * jnp.mean(weighted * x, axis=1, keepdims=True) + m.g[...]
        rows = v.tap_rows + [v.bias_grad, v.skip_grad, jnp.concatenate([gain_grad, jnp.zeros((1, inner - width), f32)], axis=1)]
        put_small(2 * rank + 3 * n, jnp.concatenate(rows, axis=0))
        end = 2 * rank + 3 * n + 8
        m.small[end:160] = jnp.zeros((160 - end, SMALL[1]), f32)
        m.small[240:256] = jnp.zeros((16, SMALL[1]), f32)
        m.small[80 + end : 240, SMALL[1] // 2 :] = jnp.zeros((160 - end, SMALL[1] // 2), f32)
        chains["s"] = small_chain(place, links, small_plan(sizes), m.small, m.small_land, m.small_sum)
        go("s")

    def bo():
        gl = stacked(m.y[...])

        def block(i):
            cols = pl.ds(mult(i * WBLOCK, WBLOCK), WBLOCK)
            m.block_out[:, cols] = m.x[:, cols] + rows_matmul(gl, m.w_out[:, cols], ((1,), (0,)))

        loop(width // WBLOCK, block)

    work = {
        "gated": gated, "back0": lambda: back(0), "back1": lambda: back(1), "back2": lambda: back(2), "pre": pre, "mixg": mixg,
        "xg": xg, "taps": taps_, "mid": mid, "ng0": ng0, "ng1": ng1, "inp": inp, "bo": bo,
    }
    for name in ORDER:
        if name in work:
            work.pop(name)()
        elif name in chains:
            go(name)
    assert not work
    while chains:
        for name in list(chains):
            go(name)

    @pl.when(jnp.logical_not(last))
    def _():
        halo.wait_send()

    @pl.when(s > 0)
    def _():
        v.halo_back.wait_send()

    links.drain()


def unpack_kernel(rank, n, a_v, b_v, c_v, d_v, small, a_o, b_o, c_o, d_o, x_proj_o, step_proj_o, decay_o, rows_o, sems):
    copies = []
    for v, o, cuts in ((c_v, c_o, 8), (d_v, d_o, 4), (a_v, a_o, 1), (b_v, b_o, 1)):
        rows = v.shape[0] // cuts
        for k in range(cuts):
            at = pl.ds(k * rows, rows)
            copies.append(pltpu.make_async_copy(v.at[at], o.at[at], sems.at[len(copies)]))
    for c in copies:
        c.start()

    def take(row, rows):
        over = SMALL[1] // 2
        if row < 80:
            tail = small[160 + row : 160 + row + rows, :over]
        else:
            tail = small[80 + row : 80 + row + rows, over:]
        return jnp.concatenate([small[row : row + rows], tail], axis=1)

    x_proj_o[...] = take(0, rank + 2 * n)
    step_proj_o[...] = take(rank + 2 * n, rank)
    decay_o[...] = take(2 * rank + 2 * n, n)
    rows_o[...] = take(2 * rank + 3 * n, 8)
    for c in copies:
        c.wait()


VMEM = pl.BlockSpec(memory_space=pltpu.VMEM)
ANY = pl.BlockSpec(memory_space=pl.ANY)


def shards(sizes, inputs, norm_gain, w_in, conv_weight, conv_bias, x_proj, step_proj, step_bias, decay_code, decay_log,
           skip_gain, w_out, cotangent):
    seqs, tokens, width = inputs.shape
    assert seqs == 1 and sizes["batch"] == 4 and sizes["seq"] % 2 == 0
    inner = w_in.shape[1] // 2
    rank, n, taps = step_proj.shape[0], decay_log.shape[1], conv_weight.shape[0]
    sh = scratch(sizes, tokens, width, inner, n, rank, taps)
    tall = lambda u: u.reshape(-1, LANES)
    args = dict(
        x=inputs[0], g=cotangent[0], gain=tall(norm_gain), conv_w=conv_weight, conv_b=tall(conv_bias), x_proj=x_proj.T,
        step_proj=step_proj, step_b=tall(step_bias), code=tall(decay_code), a2=decay_log.T, skip=tall(skip_gain), w_out=w_out)
    held = [pltpu.VMEM(v, f32) for v in ((tokens, width), (tokens, width), (width, 2 * inner), (inner, width), SMALL)]
    sums = pl.pallas_call(
        functools.partial(block_kernel, sizes, list(sh)),
        in_specs=[ANY] * len(ARGS),
        out_specs=[VMEM] * 5,
        out_shape=held,
        scratch_shapes=list(sh.values()),
        compiler_params=pltpu.CompilerParams(collective_id=1, has_side_effects=True, vmem_limit_bytes=VLIMIT << 19),
        name="block",
    )(*(args[a] for a in FETCH), w_in)
    wanted = [v.shape for v in sums[:4]] + [(rank + 2 * n, inner), (rank, inner), (n, inner), (8, inner)]
    block_out, input_grad, in_sum, out_sum, x_proj_sum, step_proj_sum, decay_sum, rows = pl.pallas_call(
        functools.partial(unpack_kernel, rank, n),
        in_specs=[VMEM] * 5,
        out_specs=[ANY] * 4 + [VMEM] * 4,
        out_shape=[jax.ShapeDtypeStruct(v, f32) for v in wanted],
        scratch_shapes=[pltpu.SemaphoreType.DMA((14,))],
        compiler_params=pltpu.CompilerParams(vmem_limit_bytes=VLIMIT2 << 19),
        name="unpack",
    )(*sums)
    return (block_out[None], input_grad[None], rows[7, :width], in_sum, rows[:taps], rows[taps], x_proj_sum.T, step_proj_sum,
            rows[taps + 1], decay_sum.T, rows[taps + 2], out_sum)


VLIMIT, VLIMIT2 = 97, 16


def solution(mesh):
    rows = P("batch", "seq", None)
    return jax.shard_map(
        functools.partial(shards, dict(mesh.shape)),
        mesh=mesh,
        in_specs=(rows,) + (P(),) * 11 + (rows,),
        out_specs=(rows, rows) + (P(),) * 10,
        check_vma=False,
    )
```

time: 240 us -> 186 us (0.78)
  Pallas kernels: 225 us -> 180 us
  local copies, waits for them, and re-layouts: 8.31 us -> 1.87 us
    pallas_call x1, Pallas kernels: 219 us -> 174 us  [shards(): pl.pallas_call(functools.partial(block_kernel, sizes, list(sh)), in_specs...]
    reshape x5 -> x0, local copies, waits for them, and re-layouts: 6.44 us -> none  [shards(): row = lambda v: v.reshape(1, -1)]
where the time goes in v4:
time: 186 us; the launch traced here: 183 us
  Pallas kernels  180 us (97%)
  local copies, waits for them, and re-layouts  1.87 us (1%)
    pallas_call x1, Pallas kernels, shards(): pl.pallas_call(functools.partial(block_kernel, sizes, list(sh)), in_specs...  174 us
    pallas_call x1, Pallas kernels, shards(): pl.pallas_call(functools.partial(unpack_kernel, rank, n), in_specs=[VMEM]...  6.28 us

profile of v4, /device:TPU:1, one launch (start us, length us, event | category | flops | bytes accessed | tf_op | source)
XLA Modules:
  0.0 182.8 jit_solution(1219972554490618983)
XLA Ops:
  0.6 174.0 %block.1 = (f32[128,768]{1,0:T(8,128)S(1)}, f32[128,768]{1,0:T(8,128)S(1)}, f32[768,3072]{1,0:T(8,128)S(1)}, f32[1536,768]{1,0:T(8,128)S(1)}, f32[256,1024]{1,0:T(8,128)S(1)}) custom-call(f32[128,768]{1,0:T(8,128)} %bitcast.14, f32[6,128]{1,0:T(8,128)} %bitcast.21, f32[128,768]{1,0:T(8,128)} %bitcast.15, f32[1536,768]{1,0:T(8,128)} %refs_3_.1, ...), custom_call_target="tpu_custom_call" | custom-call | tf_op jit(solution)/shard_map/block/pallas_call | solution.py:966
  174.7 6.3 %unpack.1 = (f32[128,768]{1,0:T(8,128)}, f32[128,768]{1,0:T(8,128)}, f32[768,3072]{1,0:T(8,128)}, f32[1536,768]{1,0:T(8,128)}, f32[80,1536]{1,0:T(8,128)}, /*ind...) custom-call(f32[128,768]{1,0:T(8,128)S(1)} %get-tuple-element.25.a_v, ...), custom_call_target="tpu_custom_call" | custom-call | tf_op jit(solution)/shard_map/unpack/pallas_call | solution.py:976
  181.0 0.6 slice_reduce_fusion.3
  181.6 0.6 slice.16
  182.2 0.7 slice_reduce_fusion

commit v5 on v4

--- a/solution.py
+++ b/solution.py
@@ -18,19 +18,20 @@
 WBLOCK = 256
 SLOTS = 4
 SMALL = (256, 1024)
-PARTS = {"o": 2, "i": 4, "x": 4}
-SPREAD = {"o0": "T3", "x0": "T3"}
-COPIES = 250
+PARTS = {"o0": 2, "o1": 2, "i1": 2, "x0": 2, "x1": 2}
+SPREAD = {"i1b": "T2", "o0a": "T3", "o1a": "T3", "x1b": "T3"}
+SENDS = 120
 ORDER = [
-    "gated", "back0", "back1", "back2", "i", "o", "pre", "i", "i3", "i2", "o", "i0", "o0", "i1", "o1", "mixg",
-    "xg", "taps", "mid", "ng0", "i3", "i2", "i0", "i1", "ng1", "inp", "bo", "i3", "o0", "o1", "i2", "i0",
-    "i1", "s", "x", "x", "i3", "x1", "x2", "x3", "s", "x0", "i2", "i0", "i1", "o0", "o1", "i3",
-    "i2", "i0", "i1", "i3", "s", "x1", "x2", "o0", "x3", "o1", "x0", "i2", "i0", "i1", "i3", "i3",
-    "s", "x1", "x2", "x3", "o0", "x0", "o1", "i2", "i2", "s", "i0", "i0", "i3", "i1", "i1", "i3",
-    "x1", "o0", "x2", "o0", "x3", "o1", "s", "i2", "x0", "i0", "i1", "x1", "i2", "i0", "i1", "o0",
-    "x2", "x3", "s", "x0", "o1", "o1", "x1", "x0", "x0", "x2", "x3", "s", "x0", "x1", "x1", "o0",
-    "x2", "x2", "x3", "x3", "o1", "o0", "x0", "o1", "x1", "s", "x0", "x1", "x2", "x3", "s", "x2",
-    "x3",
+    "gated", "i0", "i1", "o1", "a0", "b0", "o0", "a1", "b1", "o1", "a2", "o1", "i1", "o1b", "o0", "b2",
+    "i0", "o1a", "i1", "i1b", "o0", "i1a", "o0a", "pre", "o1b", "mixg", "o0b", "i1b", "i0", "o1a", "i0a", "o0a",
+    "xg", "x0", "taps", "o1b", "i1b", "i1a", "ng0", "o1a", "x1", "o0a", "o0b", "x0", "o1b", "i0a", "i1b", "i1a",
+    "x0", "x0a", "o1a", "x1", "o1b", "x0b", "o0a", "i1a", "x1", "x0a", "o0b", "x1a", "x0b", "i0a", "x1b", "ng1",
+    "x1a", "x0a", "i1b", "o1a", "o0a", "mid", "o0b", "x1b", "x0b", "i1b", "o1b", "i0a", "inp", "s", "i1a", "o1a",
+    "o0a", "s", "x1b", "o0b", "x1a", "i0a", "i1a", "x1b", "s", "o0a", "o0a", "o0b", "i1b", "x1a", "i1a", "x0b",
+    "x1b", "i0a", "o1b", "s", "x0a", "x1a", "o1a", "o0b", "s", "x0a", "x0b", "o0b", "x1a", "x1b", "x1b", "i1b",
+    "o0b", "i0a", "s", "x1a", "x1b", "i1a", "x1a", "i0a", "s", "x0b", "i0a", "x0a", "s", "x0b", "i1b", "o1b",
+    "o1b", "x0b", "i0a", "o1a", "x0a", "o0a", "s", "x1b", "o0b", "x1a", "o1b", "o0a", "x0b", "i1a", "x1a", "x0a",
+    "bo", "x0a", "x0b", "i1a", "s", "o1a", "x1b", "i1b", "s", "x0a", "o1a",
 ]
 
 
@@ -106,27 +107,33 @@
 
 class Links:
     def __init__(self, send, recv):
-        self.send, self.recv, self.used, self.open = send, recv, 0, []
+        self.send, self.recv, self.used, self.made, self.free, self.open = send, recv, 0, 0, [], []
 
     def copy(self, src, dst, to, start=True):
         i = self.used
         self.used += 1
+        if self.free:
+            k = self.free.pop()
+        else:
+            k = self.made
+            self.made += 1
+        assert self.used <= self.recv.shape[0] and self.made <= self.send.shape[0]
         c = pltpu.make_async_remote_copy(
-            src_ref=src, dst_ref=dst, send_sem=self.send.at[i], recv_sem=self.recv.at[i], device_id=to, device_id_type=MESH
+            src_ref=src, dst_ref=dst, send_sem=self.send.at[k], recv_sem=self.recv.at[i], device_id=to, device_id_type=MESH
         )
         if start:
             c.start()
-            self.open.append(c)
+            self.open.append((c, k))
         return c
 
-    def sent(self, copy):
-        copy.wait_send()
-        self.open = [c for c in self.open if c is not copy]
+    def sent(self, *copies):
+        for copy in copies:
+            copy.wait_send()
+            self.free += [k for c, k in self.open if c is copy]
+            self.open = [(c, k) for c, k in self.open if c is not copy]
 
     def drain(self):
-        for c in self.open:
-            c.wait_send()
-        self.open = []
+        self.sent(*(c for c, _ in self.open))
 
 
 GROUP = [(1, 0, 0), (1, 0, 1), (0, 1, 0), (0, 1, 1), (0, 0, 1)]
@@ -166,7 +173,7 @@
 
 def reduce_rows(place, links, plan, acc, land, kept):
     rows = acc.shape[0]
-    off, base = 0, 0
+    off, base, before = 0, 0, []
     for pair, ok in zip(plan, halvings(rows, len(plan))):
         to, v = place.stage(pair)
         parent = off
@@ -178,8 +185,11 @@
         copy = links.copy(acc.at[pl.ds(mult(give, 8), rows)], land.at[pl.ds(base, rows)], to)
         yield
         copy.wait_recv()
+        links.sent(*before)
+        before = [copy]
         if not ok:
             links.sent(copy)
+            before = []
 
         def add(i, off=off, base=base):
             at = pl.ds(mult(off + i * 8, 8), 8)
@@ -189,6 +199,7 @@
         base += rows
         if ok:
             kept.append((to, parent, off, rows))
+    links.sent(*before)
     return off, rows
 
 
@@ -290,9 +301,11 @@
         value = m.got[p, way] + m.tile_dec[p] * value
     second = [links.copy(m.back.at[p, way], cut(m.edges.at[way], s), (p, b)) for p in peers]
     cut(m.edges.at[way], s)[...] = m.back[s, way]
+    links.sent(*first)
     yield
     for c in second:
         c.wait_recv()
+    links.sent(*second)
 
 
 def wide(tile):
@@ -359,7 +372,7 @@
     lax.fori_loop(0, m.step.shape[0] // 8, chunk, m.edges[0, :, lanes])
 
 
-def scan_back(m, lanes, first):
+def scan_again(m, lanes, first):
     a2 = m.a2[:, lanes]
     n = a2.shape[0]
     tokens = m.step.shape[0]
@@ -376,6 +389,12 @@
         return h
 
     lax.fori_loop(0, tokens // 8, ahead, m.edges[0, :, lanes])
+
+
+def scan_back(m, lanes, first):
+    a2 = m.a2[:, lanes]
+    n = a2.shape[0]
+    tokens = m.step.shape[0]
 
     def behind(i, held):
         q, rate = held
@@ -412,8 +431,22 @@
 OUTS = ["block_out", "input_grad", "in_sum", "out_sum", "small_sum"]
 
 
-def pieces(key):
-    return (PARTS[key], 1) if key == "o" else {1: (1, 1), 2: (1, 2), 4: (2, 2)}[PARTS[key]]
+UNITS = ["o0", "o1", "i0", "i1", "x0", "x1"]
+
+
+def parts(unit):
+    return [unit + "ab"[k] for k in range(PARTS.get(unit, 1))]
+
+
+def recvs(sizes):
+    bits, count = log2(sizes["seq"]), sizes["seq"]
+    total = 6 + 2 + 3 * len(UNITS) + (5 * (count - 1) if tiled(count) else 2 * bits)
+    total += len(small_plan(sizes)) + sum(halvings(SMALL[0], len(small_plan(sizes))))
+    for unit in UNITS:
+        for p in parts(unit):
+            kept = sum(halvings(LANES * 3 // len(parts(unit)), bits)) - 1
+            total += bits + 7 + kept + 3 * {"T1": 0, "T2": kept, "T3": kept - 1}[SPREAD.get(p, "T1")]
+    return total
 
 
 def scratch(sizes, tokens, width, inner, n, rank, taps):
@@ -434,15 +467,15 @@
         ng=v(4, tokens, part), gg=v(4, tokens, part),
         small=v(*SMALL), small_land=v(landing_rows(SMALL[0], len(small_plan(sizes))), SMALL[1]),
     )
-    for key in "oix":
-        rows, cols = (half, part) if key == "o" else (part, half)
-        down, over = pieces(key)
-        sh["late_" + key] = v(4, tokens, half)
-        for k in range(down * over):
-            sh[f"tile_{key}{k}"] = v(rows // down, cols // over)
-            sh[f"land_{key}{k}"] = v(landing_rows(rows // down, stages), cols // over)
+    for unit in UNITS:
+        sh["late_" + unit] = v(4, tokens, part)
+        for p in parts(unit):
+            rows = part // len(parts(unit))
+            sh["tile_" + p] = v(rows, part)
+            sh["land_" + p] = v(landing_rows(rows, stages), part)
     sh.update(carry_scratch(sizes["seq"], n, inner))
-    sh["send"], sh["recv"] = [pltpu.SemaphoreType.DMA((COPIES,))] * 2
+    sh["send"] = pltpu.SemaphoreType.DMA((SENDS,))
+    sh["recv"] = pltpu.SemaphoreType.DMA((recvs(sizes),))
     sh["wsem"] = pltpu.SemaphoreType.DMA((SLOTS,))
     sh["isem"] = pltpu.SemaphoreType.DMA((len(FETCH),))
     return sh
@@ -473,15 +506,16 @@
     return run
 
 
-def late_chain(place, links, m, key, value, left, right):
-    late = getattr(m, "late_" + key)
-    half = late.shape[2]
-    mine = place.y if key == "o" else place.x
-    to, _ = place.near(0, 1, 0) if key == "o" else place.near(1, 0, 0)
+def late_chain(place, links, m, unit, value, left, right):
+    late = getattr(m, "late_" + unit)
+    width = late.shape[2]
+    shift = int(unit[1]) * width
+    mine = place.y if unit[0] == "o" else place.x
+    to, _ = place.near(0, 1, 0) if unit[0] == "o" else place.near(1, 0, 0)
     core, _ = place.near(0, 0, 1)
 
     def cut(which):
-        return value.at[:, pl.ds(mult(which * half, LANES), half)]
+        return value.at[:, pl.ds(mult(which * 2 * width + shift, LANES), width)]
 
     def pass_on(which):
         slot = late.at[which * 2 + place.c]
@@ -496,23 +530,22 @@
     yield
     for copy in passed:
         copy.wait_recv()
-    down, over = pieces(key)
+    links.sent(sent, *passed)
     for i in range(2):
-        part = matmul(left(i), right(i), ((0,), (0,)))
-        rows, cols = part.shape[0] // down, part.shape[1] // over
-        for k in range(down * over):
-            tile = getattr(m, f"tile_{key}{k}")
-            r, c = k // over * rows, k % over * cols
-            cell = part[r : r + rows, c : c + cols]
-            tile[...] = cell if i == 0 else tile[...] + cell
-
-
-def piece_chain(place, links, m, key, k, zplan, out, base):
-    acc, land = getattr(m, f"tile_{key}{k}"), getattr(m, f"land_{key}{k}")
+        cell = matmul(left(i), right(i), ((0,), (0,)))
+        rows = cell.shape[0] // len(parts(unit))
+        for k, p in enumerate(parts(unit)):
+            tile = getattr(m, "tile_" + p)
+            value = cell[k * rows : (k + 1) * rows]
+            tile[...] = value if i == 0 else tile[...] + value
+
+
+def piece_chain(place, links, m, p, zplan, out, base):
+    acc, land = getattr(m, "tile_" + p), getattr(m, "land_" + p)
     rows, cols = acc.shape
-    over = pieces(key)[1]
-    r0, c0 = k // over * rows, k % over * cols
-    half, part = out.shape[0] // 2 if key == "o" else out.shape[1] // 4, m.x.shape[1] // 2
+    key, shift, r0 = p[0], int(p[1]) * m.x.shape[1] // 2, "ab".index(p[2]) * rows
+    part = cols
+    half = 2 * part
     bit = ("seq", 0) if key == "o" else ("batch", 1)
     x, y, c = place.x, place.y, place.c
     core, _ = place.near(0, 0, 1)
@@ -520,9 +553,9 @@
     def region(at, row, count):
         xx, yy = at
         if key == "o":
-            top, side = yy * half + r0 + xx * (rows // 2) + row, c * part + c0
+            top, side = yy * half + shift + r0 + xx * (rows // 2) + row, c * part
         else:
-            top, side = c * part + r0 + yy * (rows // 2) + row, base + xx * half + c0
+            top, side = c * part + r0 + yy * (rows // 2) + row, base + xx * half + shift
         return out.at[pl.ds(mult(top, 8), count), pl.ds(mult(side, LANES), cols)]
 
     kept = []
@@ -537,7 +570,7 @@
         return links.copy(ref, ref, to)
 
     steps = list(reversed(kept[1:]))
-    kind = SPREAD.get(key + str(k), "T1")
+    kind = SPREAD.get(p, "T1")
     steps.insert({"T1": len(steps), "T2": 0, "T3": 1}[kind], None)
     for i, step in enumerate(steps):
         last = i == len(steps) - 1
@@ -547,6 +580,7 @@
             yield
             for copy in copies:
                 copy.wait_recv()
+            links.sent(*copies)
             row, count = parent - edge, 2 * size
             continue
         first, at_a = place.near(1 - c, c, 0)
@@ -569,6 +603,7 @@
         onward(at_b)
         yield
         d.wait_recv()
+        links.sent(a, b)
         onward(at_d)
     if not across:
         across = [give(at, core) for at in held]
@@ -602,8 +637,9 @@
     for name in FETCH[3:]:
         fetched[name].start()
     bar = pltpu.get_barrier_semaphore()
-    greet = [place.near(*d)[0] for d in GROUP] + [(p, b) for p in carry_peers(count, s)]
-    greet += [(lax.rem(s + 1, count), b), (lax.rem(s + count - 1, count), b)]
+    greet = [place.near(*d)[0] for d in GROUP[1:]] + [(p, b) for p in carry_peers(count, s)]
+    if not tiled(count):
+        greet += [(lax.rem(s + 1, count), b), (lax.rem(s + count - 1, count), b)]
     for to in greet:
         pl.semaphore_signal(bar, inc=1, device_id=to, device_id_type=MESH)
 
@@ -619,8 +655,21 @@
     x = m.x[...]
     rms = lax.rsqrt(jnp.mean(x * x, axis=1, keepdims=True) + EPSILON)
     m.normed[...] = x * rms * m.vec[3:4, :width]
+    left = stacked(m.normed[...])
+
+    def hidden_block(i, w):
+        m.hid[pl.ds(8, tokens), pl.ds(mult(i * WBLOCK, WBLOCK), WBLOCK)] = rows_matmul(left, w, ((1,), (0,)))
+
+    to_hidden(hidden_block)
+    to_gate = stream(m, blocks_of_half, 2 * blocks_of_half)
+    pl.semaphore_wait(bar, len(greet))
+    halo = links.copy(m.hid.at[pl.ds(tokens, 8)], m.hid.at[pl.ds(0, 8)], (lax.rem(s + 1, count), b), start=False)
+
+    @pl.when(jnp.logical_not(last))
+    def _():
+        halo.start()
+
     fetched["g"].wait()
-    pl.semaphore_wait(bar, len(greet))
     early = []
     for d in GROUP:
         to, _ = place.near(*d)
@@ -633,18 +682,6 @@
     m.ng[place.x * 2 + c] = m.normed[:, own]
     m.gg[place.y * 2 + c] = m.g[:, own]
 
-    left = stacked(m.normed[...])
-
-    def hidden_block(i, w):
-        m.hid[pl.ds(8, tokens), pl.ds(mult(i * WBLOCK, WBLOCK), WBLOCK)] = rows_matmul(left, w, ((1,), (0,)))
-
-    to_hidden(hidden_block)
-    to_gate = stream(m, blocks_of_half, 2 * blocks_of_half)
-    halo = links.copy(m.hid.at[pl.ds(tokens, 8)], m.hid.at[pl.ds(0, 8)], (lax.rem(s + 1, count), b), start=False)
-
-    @pl.when(jnp.logical_not(last))
-    def _():
-        halo.start()
 
     for name in FETCH[3:]:
         fetched[name].wait()
@@ -685,7 +722,6 @@
     for j in range(n):
         at = pl.ds(j, tokens, stride=n)
         m.bb[at] = jnp.broadcast_to(proj[:, rank + j : rank + j + 1], (tokens, LANES))
-        m.cc[at] = jnp.broadcast_to(proj[:, rank + n + j : rank + n + j + 1], (tokens, LANES))
     low_left = stacked(proj[:, :rank])
 
     def step_block(i):
@@ -704,6 +740,9 @@
         scan_ends(m, lanes)
     ahead = carry(place, links, m, 0)
     next(ahead)
+    for j in range(n):
+        at = pl.ds(j, tokens, stride=n)
+        m.cc[at] = jnp.broadcast_to(m.proj[:, rank + n + j : rank + n + j + 1], (tokens, LANES))
 
     def gate_block(i, w):
         cols = pl.ds(mult(i * WBLOCK, WBLOCK), WBLOCK)
@@ -737,25 +776,25 @@
 
     s_bits, b_bits = all_bits(sizes)
     zplan = [(k, k) for k in s_bits[1:] + b_bits[2:]]
-    chains, started, v = {}, set(), Refs()
+    chains, v = {}, Refs()
 
     def pair(ref):
         return lambda i: ref[pl.ds(2 * i, 2)].reshape(2 * tokens, ref.shape[2])
 
     def go(name):
-        started.add(name)
         try:
             next(chains[name])
         except StopIteration:
             del chains[name]
-            if name in "oix":
-                where = {"o": (m.out_sum, 0), "i": (m.in_sum, inner), "x": (m.in_sum, 0)}[name]
-                for k in range(PARTS[name]):
-                    chains[name + str(k)] = piece_chain(place, links, m, name, k, zplan, *where)
+            if name in UNITS:
+                where = {"o": (m.out_sum, 0), "i": (m.in_sum, inner), "x": (m.in_sum, 0)}[name[0]]
+                for p in parts(name):
+                    chains[p] = piece_chain(place, links, m, p, zplan, *where)
 
     def late(key, value, left, right):
-        chains[key] = late_chain(place, links, m, key, value, pair(left), pair(right))
-        go(key)
+        for unit in (key + "0", key + "1"):
+            ref = getattr(m, "late_" + unit)
+            chains[unit] = late_chain(place, links, m, unit, value, pair(ref if left is None else left), pair(ref if right is None else right))
 
     column = lax.broadcasted_iota(jnp.int32, (tokens, LANES), 1)
     zero = jnp.zeros((8, inner), f32)
@@ -777,16 +816,20 @@
             m.small[top + row : top + row + rows, over:] = value[:, cut:]
 
     def gated():
-        late("o", m.y, m.late_o, m.gg)
-        late("i", m.d_gate, m.ng, m.late_i)
-        for _ in behind:
-            pass
+        late("o", m.y, None, m.gg)
+        late("i", m.d_gate, m.ng, None)
+
+    def again(k):
+        scan_again(m, blocks[k], k == 0)
 
     def back(k):
-        scan_back(m, blocks[k], k == 0)
         if k == 0:
+            for _ in behind:
+                pass
             for e in early:
                 e.wait_recv()
+            links.sent(*early)
+        scan_back(m, blocks[k], k == 0)
 
     def pre():
         bc_grad = collect(m.cg, rank + n, collect(m.bg, rank, jnp.zeros((tokens, LANES), f32)))
@@ -839,7 +882,7 @@
             m.gate[pl.ds(mult(i * 8, 8), 8)] = z
 
         loop(tokens // 8, rows)
-        late("x", m.gate, m.ng, m.late_x)
+        late("x", m.gate, m.ng, None)
 
     def taps_():
         def rows(i, total):
@@ -885,7 +928,6 @@
         m.small[240:256] = jnp.zeros((16, SMALL[1]), f32)
         m.small[80 + end : 240, SMALL[1] // 2 :] = jnp.zeros((160 - end, SMALL[1] // 2), f32)
         chains["s"] = small_chain(place, links, small_plan(sizes), m.small, m.small_land, m.small_sum)
-        go("s")
 
     def bo():
         gl = stacked(m.y[...])
@@ -897,7 +939,8 @@
         loop(width // WBLOCK, block)
 
     work = {
-        "gated": gated, "back0": lambda: back(0), "back1": lambda: back(1), "back2": lambda: back(2), "pre": pre, "mixg": mixg,
+        "gated": gated, "a0": lambda: again(0), "b0": lambda: back(0), "a1": lambda: again(1), "b1": lambda: back(1),
+        "a2": lambda: again(2), "b2": lambda: back(2), "pre": pre, "mixg": mixg,
         "xg": xg, "taps": taps_, "mid": mid, "ng0": ng0, "ng1": ng1, "inp": inp, "bo": bo,
     }
     for name in ORDER:
@@ -921,7 +964,8 @@
     links.drain()
 
 
-def unpack_kernel(rank, n, a_v, b_v, c_v, d_v, small, a_o, b_o, c_o, d_o, x_proj_o, step_proj_o, decay_o, rows_o, sems):
+def unpack_kernel(rank, n, a_v, b_v, c_v, d_v, small, a_o, b_o, c_o, d_o, x_proj_o, step_proj_o, decay_o, taps_o, *rest):
+    row_os, sems = rest[:-1], rest[-1]
     copies = []
     for v, o, cuts in ((c_v, c_o, 8), (d_v, d_o, 4), (a_v, a_o, 1), (b_v, b_o, 1)):
         rows = v.shape[0] // cuts
@@ -942,7 +986,12 @@
     x_proj_o[...] = take(0, rank + 2 * n)
     step_proj_o[...] = take(rank + 2 * n, rank)
     decay_o[...] = take(2 * rank + 2 * n, n)
-    rows_o[...] = take(2 * rank + 3 * n, 8)
+    rows = take(2 * rank + 3 * n, 8)
+    taps = taps_o.shape[0]
+    taps_o[...] = rows[:taps]
+    for k, ref in enumerate(row_os):
+        for j in range(ref.shape[0]):
+            ref[j : j + 1] = rows[taps + k : taps + k + 1, j * LANES : (j + 1) * LANES]
     for c in copies:
         c.wait()
 
@@ -972,18 +1021,20 @@
         compiler_params=pltpu.CompilerParams(collective_id=1, has_side_effects=True, vmem_limit_bytes=VLIMIT << 19),
         name="block",
     )(*(args[a] for a in FETCH), w_in)
-    wanted = [v.shape for v in sums[:4]] + [(rank + 2 * n, inner), (rank, inner), (n, inner), (8, inner)]
-    block_out, input_grad, in_sum, out_sum, x_proj_sum, step_proj_sum, decay_sum, rows = pl.pallas_call(
+    wanted = [v.shape for v in sums[:4]] + [(rank + 2 * n, inner), (rank, inner), (n, inner), (taps, inner)]
+    wanted += [(inner // LANES, LANES)] * 3 + [(width // LANES, LANES)]
+    block_out, input_grad, in_sum, out_sum, x_proj_sum, step_proj_sum, decay_sum, taps_sum, *rows = pl.pallas_call(
         functools.partial(unpack_kernel, rank, n),
         in_specs=[VMEM] * 5,
-        out_specs=[ANY] * 4 + [VMEM] * 4,
+        out_specs=[ANY] * 4 + [VMEM] * 8,
         out_shape=[jax.ShapeDtypeStruct(v, f32) for v in wanted],
         scratch_shapes=[pltpu.SemaphoreType.DMA((14,))],
         compiler_params=pltpu.CompilerParams(vmem_limit_bytes=VLIMIT2 << 19),
         name="unpack",
     )(*sums)
-    return (block_out[None], input_grad[None], rows[7, :width], in_sum, rows[:taps], rows[taps], x_proj_sum.T, step_proj_sum,
-            rows[taps + 1], decay_sum.T, rows[taps + 2], out_sum)
+    conv_b_sum, step_b_sum, skip_sum, gain_sum = (v.reshape(-1) for v in rows)
+    return (block_out[None], input_grad[None], gain_sum, in_sum, taps_sum, conv_b_sum, x_proj_sum.T, step_proj_sum, step_b_sum,
+            decay_sum.T, skip_sum, out_sum)
 
 
 VLIMIT, VLIMIT2 = 97, 16

time: 186 us -> 157 us (0.84); the launches traced: 183 us -> 157 us
  Pallas kernels: 180 us -> 156 us
  local copies, waits for them, and re-layouts: 1.87 us -> 0 us
    pallas_call x1, Pallas kernels: 174 us -> 150 us  [shards(): pl.pallas_call(functools.partial(block_kernel, sizes, list(sh)), in_specs...]
    slice x3 -> x0, local copies, waits for them, and re-layouts: 1.87 us -> none  [the longest x1 0.65 us: shards(): rows[taps + 2]]
where the time goes in v5:
time: 157 us
  Pallas kernels  156 us (99%)
    pallas_call x1, Pallas kernels, shards(): pl.pallas_call(functools.partial(block_kernel, sizes, list(sh)), in_specs...  150 us
    pallas_call x1, Pallas kernels, shards(): pl.pallas_call(functools.partial(unpack_kernel, rank, n), in_specs=[VMEM]...  6.3 us

profile of v5, /device:TPU:1, one launch (start us, length us, event | category | flops | bytes accessed | tf_op | source)
XLA Modules:
  0.0 156.7 jit_solution(8044880509160582663)
XLA Ops:
  0.6 149.6 %block.1 = (f32[128,768]{1,0:T(8,128)S(1)}, f32[128,768]{1,0:T(8,128)S(1)}, f32[768,3072]{1,0:T(8,128)S(1)}, f32[1536,768]{1,0:T(8,128)S(1)}, f32[256,1024]{1,0:T(8,128)S(1)}) custom-call(f32[128,768]{1,0:T(8,128)} %bitcast.18, f32[6,128]{1,0:T(8,128)} %bitcast.25, f32[128,768]{1,0:T(8,128)} %bitcast.19, f32[1536,768]{1,0:T(8,128)} %refs_3_.1, ...), custom_call_target="tpu_custom_call" | custom-call | tf_op jit(solution)/shard_map/block/pallas_call | solution.py:1015
  150.2 6.3 %unpack.1 = (f32[128,768]{1,0:T(8,128)}, f32[128,768]{1,0:T(8,128)}, f32[768,3072]{1,0:T(8,128)}, f32[1536,768]{1,0:T(8,128)}, f32[80,1536]{1,0:T(8,128)}, /*ind...) custom-call(f32[128,768]{1,0:T(8,128)S(1)} %get-tuple-element.29.a_v, ...), custom_call_target="tpu_custom_call" | custom-call | tf_op jit(solution)/shard_map/unpack/pallas_call | solution.py:1026

commit v6 on v5

--- a/solution.py
+++ b/solution.py
@@ -18,20 +18,19 @@
 WBLOCK = 256
 SLOTS = 4
 SMALL = (256, 1024)
-PARTS = {"o0": 2, "o1": 2, "i1": 2, "x0": 2, "x1": 2}
-SPREAD = {"i1b": "T2", "o0a": "T3", "o1a": "T3", "x1b": "T3"}
-SENDS = 120
+PARTS = {"o1": 2, "x0": 2, "x1": 2}
+SPREAD = {"o0a": "T3", "o1a": "T3", "x0b": "T3"}
+SENDS = 64
 ORDER = [
-    "gated", "i0", "i1", "o1", "a0", "b0", "o0", "a1", "b1", "o1", "a2", "o1", "i1", "o1b", "o0", "b2",
-    "i0", "o1a", "i1", "i1b", "o0", "i1a", "o0a", "pre", "o1b", "mixg", "o0b", "i1b", "i0", "o1a", "i0a", "o0a",
-    "xg", "x0", "taps", "o1b", "i1b", "i1a", "ng0", "o1a", "x1", "o0a", "o0b", "x0", "o1b", "i0a", "i1b", "i1a",
-    "x0", "x0a", "o1a", "x1", "o1b", "x0b", "o0a", "i1a", "x1", "x0a", "o0b", "x1a", "x0b", "i0a", "x1b", "ng1",
-    "x1a", "x0a", "i1b", "o1a", "o0a", "mid", "o0b", "x1b", "x0b", "i1b", "o1b", "i0a", "inp", "s", "i1a", "o1a",
-    "o0a", "s", "x1b", "o0b", "x1a", "i0a", "i1a", "x1b", "s", "o0a", "o0a", "o0b", "i1b", "x1a", "i1a", "x0b",
-    "x1b", "i0a", "o1b", "s", "x0a", "x1a", "o1a", "o0b", "s", "x0a", "x0b", "o0b", "x1a", "x1b", "x1b", "i1b",
-    "o0b", "i0a", "s", "x1a", "x1b", "i1a", "x1a", "i0a", "s", "x0b", "i0a", "x0a", "s", "x0b", "i1b", "o1b",
-    "o1b", "x0b", "i0a", "o1a", "x0a", "o0a", "s", "x1b", "o0b", "x1a", "o1b", "o0a", "x0b", "i1a", "x1a", "x0a",
-    "bo", "x0a", "x0b", "i1a", "s", "o1a", "x1b", "i1b", "s", "x0a", "o1a",
+    "g0", "i0", "o0", "g1", "a0", "o1", "i1", "b0", "i0", "a1", "o0", "i0", "i0a", "o0", "o0a", "b1",
+    "a2", "o1", "b2", "o1", "o1b", "i0a", "pre", "i1", "mixg", "o1a", "o1b", "i0a", "i1", "i1a", "xg", "o0a",
+    "x0", "taps", "o1b", "i0a", "mid", "s", "o1a", "x1", "ng0", "x0", "i1a", "s", "o1b", "x0", "x0b", "o1a",
+    "i0a", "x0a", "o0a", "x1", "ng1", "o1a", "s", "o1b", "i1a", "x1", "x1b", "bo", "s", "o1a", "x1a", "x0a",
+    "o0a", "i0a", "s", "x1b", "inp", "i1a", "o0a", "x0b", "s", "x1b", "x0a", "i1a", "o1b", "o1a", "s", "x1b",
+    "x0a", "o1a", "x1a", "o0a", "n", "i0a", "o1a", "x0b", "x0a", "o0a", "i0a", "s", "i1a", "n", "x1a", "x0b",
+    "x0b", "o0a", "x1a", "n", "o1b", "s", "x1a", "x1b", "i1a", "x0b", "o1a", "x0a", "x1a", "o1b", "s", "x1b",
+    "i1a", "o1b", "o1b", "i0a", "x0b", "x0b", "o0a", "i0a", "x0a", "x1a", "x1b", "i1a", "x0a", "n", "x0a", "x1a",
+    "x1b", "x0b", "n", "i1a", "x1a", "x0a", "o1a", "x1b", "s", "o0a", "n", "x1a", "x0b", "x1b",
 ]
 
 
@@ -308,8 +307,8 @@
     links.sent(*second)
 
 
-def wide(tile):
-    return jnp.concatenate([tile] * (SCAN // LANES), axis=1)
+def wide(tile, width=SCAN):
+    return jnp.concatenate([tile] * (width // LANES), axis=1)
 
 
 def spread(row, n):
@@ -363,7 +362,7 @@
         ys = []
         for j in range(8):
             t = pl.ds(pl.multiple_of((i * 8 + j) * n, 8), n)
-            b, c = wide(m.bb[t]), wide(m.cc[t])
+            b, c = wide(m.bb[t], a2.shape[1]), wide(m.cc[t], a2.shape[1])
             h = jnp.exp2(spread(s8[j : j + 1], n) * a2) * h + spread(u8[j : j + 1], n) * b
             ys.append(jnp.sum(c * h, axis=0, keepdims=True))
         m.y[at, lanes] = jnp.concatenate(ys, axis=0)
@@ -428,7 +427,7 @@
 
 FETCH = ["x", "gain", "g", "w_out", "conv_w", "conv_b", "x_proj", "step_proj", "step_b", "code", "a2", "skip"]
 ARGS = [v + "_h" for v in FETCH] + ["w_in"]
-OUTS = ["block_out", "input_grad", "in_sum", "out_sum", "small_sum"]
+OUTS = ["block_out", "input_grad", "in_sum", "out_sum", "small_sum", "gain_sum"]
 
 
 UNITS = ["o0", "o1", "i0", "i1", "x0", "x1"]
@@ -441,7 +440,7 @@
 def recvs(sizes):
     bits, count = log2(sizes["seq"]), sizes["seq"]
     total = 6 + 2 + 3 * len(UNITS) + (5 * (count - 1) if tiled(count) else 2 * bits)
-    total += len(small_plan(sizes)) + sum(halvings(SMALL[0], len(small_plan(sizes))))
+    total += 2 * len(small_plan(sizes)) + sum(halvings(SMALL[0], len(small_plan(sizes))))
     for unit in UNITS:
         for p in parts(unit):
             kept = sum(halvings(LANES * 3 // len(parts(unit)), bits)) - 1
@@ -465,6 +464,7 @@
         bb=v(tokens * n, LANES), cc=v(tokens * n, LANES), bg=v(tokens * n, LANES), cg=v(tokens * n, LANES),
         h=v(tokens, n, SCAN), rate=v(n, inner), ends=v(2, n, inner), edges=v(2, n, inner), sums=v(1, inner),
         ng=v(4, tokens, part), gg=v(4, tokens, part),
+        gains=v(8, LANES), gains_land=v(landing_rows(8, len(small_plan(sizes))), LANES),
         small=v(*SMALL), small_land=v(landing_rows(SMALL[0], len(small_plan(sizes))), SMALL[1]),
     )
     for unit in UNITS:
@@ -689,22 +689,6 @@
     for k, name in enumerate(("conv_b", "step_b", "skip")):
         to_row(name, k)
     m.a2[...] = -LOG2E * jnp.exp(m.a2[...])
-    g_left = stacked(m.g[...])
-
-    def d_gated_block(i):
-        cols = pl.ds(mult(i * WBLOCK, WBLOCK), WBLOCK)
-        m.d_res[:, cols] = rows_matmul(g_left, m.w_out[cols], ((1,), (1,)))
-
-    loop(blocks_of_half, d_gated_block)
-
-    @pl.when(s > 0)
-    def _():
-        halo.wait_recv()
-
-    @pl.when(s == 0)
-    def _():
-        m.hid[pl.ds(0, 8)] = jnp.zeros((8, inner), f32)
-
     def convolve(i):
         window = m.hid[pl.ds(mult(i * 8, 8), 16)]
         v = m.vec[0:1]
@@ -715,7 +699,17 @@
         m.conv[at] = v
         m.mixed[at] = v * sigmoid(v)
 
-    loop(tokens // 8, convolve)
+    loop(tokens // 8 - 1, lambda i: convolve(i + 1))
+
+    @pl.when(s > 0)
+    def _():
+        halo.wait_recv()
+
+    @pl.when(s == 0)
+    def _():
+        m.hid[pl.ds(0, 8)] = jnp.zeros((8, inner), f32)
+
+    convolve(0)
 
     proj = matmul(m.mixed[...], m.x_proj[...], ((1,), (1,)))
     m.proj[:, : proj.shape[1]] = proj
@@ -740,6 +734,13 @@
         scan_ends(m, lanes)
     ahead = carry(place, links, m, 0)
     next(ahead)
+    g_left = stacked(m.g[...])
+
+    def d_gated_block(i):
+        cols = pl.ds(mult(i * WBLOCK, WBLOCK), WBLOCK)
+        m.d_res[:, cols] = rows_matmul(g_left, m.w_out[cols], ((1,), (1,)))
+
+    loop(blocks_of_half, d_gated_block)
     for j in range(n):
         at = pl.ds(j, tokens, stride=n)
         m.cc[at] = jnp.broadcast_to(m.proj[:, rank + n + j : rank + n + j + 1], (tokens, LANES))
@@ -762,17 +763,18 @@
     next(behind)
     for _ in ahead:
         pass
-    for lanes in blocks:
-        scan_out(m, lanes)
-    next(behind)
-
-    def gated_rows(i):
-        at = pl.ds(mult(i * 8, 8), 8)
-        result = m.y[at] + m.vec[2:3] * m.mixed[at]
-        m.y[at] = result * m.gate[at]
-        m.d_gate[at] = m.d_gate[at] * result
-
-    loop(tokens // 8, gated_rows)
+    def finish_quarters(k):
+        for first in (k * part, half + k * part):
+            cols = slice(first, first + part)
+            scan_out(m, cols)
+
+            def rows(i):
+                at = pl.ds(mult(i * 8, 8), 8)
+                result = m.y[at, cols] + m.vec[2:3, cols] * m.mixed[at, cols]
+                m.y[at, cols] = result * m.gate[at, cols]
+                m.d_gate[at, cols] = m.d_gate[at, cols] * result
+
+            loop(tokens // 8, rows)
 
     s_bits, b_bits = all_bits(sizes)
     zplan = [(k, k) for k in s_bits[1:] + b_bits[2:]]
@@ -791,8 +793,8 @@
                 for p in parts(name):
                     chains[p] = piece_chain(place, links, m, p, zplan, *where)
 
-    def late(key, value, left, right):
-        for unit in (key + "0", key + "1"):
+    def late(key, value, left, right, which=(0, 1)):
+        for unit in (key + str(k) for k in which):
             ref = getattr(m, "late_" + unit)
             chains[unit] = late_chain(place, links, m, unit, value, pair(ref if left is None else left), pair(ref if right is None else right))
 
@@ -815,9 +817,12 @@
         else:
             m.small[top + row : top + row + rows, over:] = value[:, cut:]
 
-    def gated():
-        late("o", m.y, None, m.gg)
-        late("i", m.d_gate, m.ng, None)
+    def quarters(k):
+        finish_quarters(k)
+        late("o", m.y, None, m.gg, (k,))
+        late("i", m.d_gate, m.ng, None, (k,))
+        if k == 0:
+            next(behind)
 
     def again(k):
         scan_again(m, blocks[k], k == 0)
@@ -899,6 +904,13 @@
         put_small(0, matmul(v.proj_grad, m.mixed[...], ((0,), (0,))))
         put_small(rank + 2 * n, matmul(m.proj[:, :rank], m.sg[...], ((0,), (0,))))
         put_small(2 * rank + 2 * n, m.rate[...] * m.a2[...] * LN2)
+        rows = v.tap_rows + [v.bias_grad, v.skip_grad, zero[:1]]
+        put_small(2 * rank + 3 * n, jnp.concatenate(rows, axis=0))
+        end = 2 * rank + 3 * n + 8
+        m.small[end:160] = jnp.zeros((160 - end, SMALL[1]), f32)
+        m.small[240:256] = jnp.zeros((16, SMALL[1]), f32)
+        m.small[80 + end : 240, SMALL[1] // 2 :] = jnp.zeros((160 - end, SMALL[1] // 2), f32)
+        chains["s"] = small_chain(place, links, small_plan(sizes), m.small, m.small_land, m.small_sum)
 
     def normed_block(ref):
         def use(i, w):
@@ -921,13 +933,10 @@
         gain_grad = jnp.sum(normed_grad * x * rms, axis=0, keepdims=True)
         weighted = normed_grad * m.vec[3:4, :width]
         m.input_grad[...] = rms * weighted - rms * rms * rms * x * jnp.mean(weighted * x, axis=1, keepdims=True) + m.g[...]
-        rows = v.tap_rows + [v.bias_grad, v.skip_grad, jnp.concatenate([gain_grad, jnp.zeros((1, inner - width), f32)], axis=1)]
-        put_small(2 * rank + 3 * n, jnp.concatenate(rows, axis=0))
-        end = 2 * rank + 3 * n + 8
-        m.small[end:160] = jnp.zeros((160 - end, SMALL[1]), f32)
-        m.small[240:256] = jnp.zeros((16, SMALL[1]), f32)
-        m.small[80 + end : 240, SMALL[1] // 2 :] = jnp.zeros((160 - end, SMALL[1] // 2), f32)
-        chains["s"] = small_chain(place, links, small_plan(sizes), m.small, m.small_land, m.small_sum)
+        for k in range(width // LANES):
+            m.gains[k : k + 1] = gain_grad[:, k * LANES : (k + 1) * LANES]
+        m.gains[width // LANES :] = jnp.zeros((8 - width // LANES, LANES), f32)
+        chains["n"] = small_chain(place, links, small_plan(sizes), m.gains, m.gains_land, m.gain_sum)
 
     def bo():
         gl = stacked(m.y[...])
@@ -939,7 +948,7 @@
         loop(width // WBLOCK, block)
 
     work = {
-        "gated": gated, "a0": lambda: again(0), "b0": lambda: back(0), "a1": lambda: again(1), "b1": lambda: back(1),
+        "g0": lambda: quarters(0), "g1": lambda: quarters(1), "a0": lambda: again(0), "b0": lambda: back(0), "a1": lambda: again(1), "b1": lambda: back(1),
         "a2": lambda: again(2), "b2": lambda: back(2), "pre": pre, "mixg": mixg,
         "xg": xg, "taps": taps_, "mid": mid, "ng0": ng0, "ng1": ng1, "inp": inp, "bo": bo,
     }
@@ -964,7 +973,7 @@
     links.drain()
 
 
-def unpack_kernel(rank, n, a_v, b_v, c_v, d_v, small, a_o, b_o, c_o, d_o, x_proj_o, step_proj_o, decay_o, taps_o, *rest):
+def unpack_kernel(rank, n, a_v, b_v, c_v, d_v, small, gains, a_o, b_o, c_o, d_o, x_proj_o, step_proj_o, decay_o, taps_o, *rest):
     row_os, sems = rest[:-1], rest[-1]
     copies = []
     for v, o, cuts in ((c_v, c_o, 8), (d_v, d_o, 4), (a_v, a_o, 1), (b_v, b_o, 1)):
@@ -989,7 +998,8 @@
     rows = take(2 * rank + 3 * n, 8)
     taps = taps_o.shape[0]
     taps_o[...] = rows[:taps]
-    for k, ref in enumerate(row_os):
+    row_os[3][...] = gains[: row_os[3].shape[0]]
+    for k, ref in enumerate(row_os[:3]):
         for j in range(ref.shape[0]):
             ref[j : j + 1] = rows[taps + k : taps + k + 1, j * LANES : (j + 1) * LANES]
     for c in copies:
@@ -1011,11 +1021,11 @@
     args = dict(
         x=inputs[0], g=cotangent[0], gain=tall(norm_gain), conv_w=conv_weight, conv_b=tall(conv_bias), x_proj=x_proj.T,
         step_proj=step_proj, step_b=tall(step_bias), code=tall(decay_code), a2=decay_log.T, skip=tall(skip_gain), w_out=w_out)
-    held = [pltpu.VMEM(v, f32) for v in ((tokens, width), (tokens, width), (width, 2 * inner), (inner, width), SMALL)]
+    held = [pltpu.VMEM(v, f32) for v in ((tokens, width), (tokens, width), (width, 2 * inner), (inner, width), SMALL, (8, LANES))]
     sums = pl.pallas_call(
         functools.partial(block_kernel, sizes, list(sh)),
         in_specs=[ANY] * len(ARGS),
-        out_specs=[VMEM] * 5,
+        out_specs=[VMEM] * 6,
         out_shape=held,
         scratch_shapes=list(sh.values()),
         compiler_params=pltpu.CompilerParams(collective_id=1, has_side_effects=True, vmem_limit_bytes=VLIMIT << 19),
@@ -1025,7 +1035,7 @@
     wanted += [(inner // LANES, LANES)] * 3 + [(width // LANES, LANES)]
     block_out, input_grad, in_sum, out_sum, x_proj_sum, step_proj_sum, decay_sum, taps_sum, *rows = pl.pallas_call(
         functools.partial(unpack_kernel, rank, n),
-        in_specs=[VMEM] * 5,
+        in_specs=[VMEM] * 6,
         out_specs=[ANY] * 4 + [VMEM] * 8,
         out_shape=[jax.ShapeDtypeStruct(v, f32) for v in wanted],
         scratch_shapes=[pltpu.SemaphoreType.DMA((14,))],

time: 157 us -> 153 us (0.975)
  Pallas kernels: 156 us -> 152 us
    pallas_call x1, Pallas kernels: 150 us -> 145 us  [shards(): pl.pallas_call(functools.partial(block_kernel, sizes, list(sh)), in_specs...]
where the time goes in v6:
time: 153 us
  Pallas kernels  152 us (99%)
    pallas_call x1, Pallas kernels, shards(): pl.pallas_call(functools.partial(block_kernel, sizes, list(sh)), in_specs...  145 us
    pallas_call x1, Pallas kernels, shards(): pl.pallas_call(functools.partial(unpack_kernel, rank, n), in_specs=[VMEM]...  6.3 us

profile of v6, /device:TPU:1, one launch (start us, length us, event | category | flops | bytes accessed | tf_op | source)
XLA Modules:
  0.0 152.5 jit_solution(2297144046322507788)
XLA Ops:
  0.6 145.4 %block.1 = (f32[128,768]{1,0:T(8,128)S(1)}, f32[128,768]{1,0:T(8,128)S(1)}, f32[768,3072]{1,0:T(8,128)S(1)}, f32[1536,768]{1,0:T(8,128)S(1)}, f32[256,1024]{1,0:T(8,128)S(1)}, /*index=5*/f32[8,128]{1,0:T(8,128)S(1)}) custom-call(f32[128,768]{1,0:T(8,128)} %bitcast.18, f32[6,128]{1,0:T(8,128)} %bitcast.25, f32[128,768]{1,0:T(8,128)} %bitcast.19, ...), custom_call_target="tpu_custom_call" | custom-call | tf_op jit(solution)/shard_map/block/pallas_call | solution.py:1025
  146.1 6.3 %unpack.1 = (f32[128,768]{1,0:T(8,128)}, f32[128,768]{1,0:T(8,128)}, f32[768,3072]{1,0:T(8,128)}, f32[1536,768]{1,0:T(8,128)}, f32[80,1536]{1,0:T(8,128)}, /*ind...) custom-call(f32[128,768]{1,0:T(8,128)S(1)} %get-tuple-element.30.a_v, ...), custom_call_target="tpu_custom_call" | custom-call | tf_op jit(solution)/shard_map/unpack/pallas_call | solution.py:1036

commit v7 on v6

--- a/solution.py
+++ b/solution.py
@@ -19,18 +19,18 @@
 SLOTS = 4
 SMALL = (256, 1024)
 PARTS = {"o1": 2, "x0": 2, "x1": 2}
-SPREAD = {"o0a": "T3", "o1a": "T3", "x0b": "T3"}
+SPREAD = {"i1a": "T3", "o1b": "T3", "x1a": "T3"}
 SENDS = 64
 ORDER = [
-    "g0", "i0", "o0", "g1", "a0", "o1", "i1", "b0", "i0", "a1", "o0", "i0", "i0a", "o0", "o0a", "b1",
-    "a2", "o1", "b2", "o1", "o1b", "i0a", "pre", "i1", "mixg", "o1a", "o1b", "i0a", "i1", "i1a", "xg", "o0a",
-    "x0", "taps", "o1b", "i0a", "mid", "s", "o1a", "x1", "ng0", "x0", "i1a", "s", "o1b", "x0", "x0b", "o1a",
-    "i0a", "x0a", "o0a", "x1", "ng1", "o1a", "s", "o1b", "i1a", "x1", "x1b", "bo", "s", "o1a", "x1a", "x0a",
-    "o0a", "i0a", "s", "x1b", "inp", "i1a", "o0a", "x0b", "s", "x1b", "x0a", "i1a", "o1b", "o1a", "s", "x1b",
-    "x0a", "o1a", "x1a", "o0a", "n", "i0a", "o1a", "x0b", "x0a", "o0a", "i0a", "s", "i1a", "n", "x1a", "x0b",
-    "x0b", "o0a", "x1a", "n", "o1b", "s", "x1a", "x1b", "i1a", "x0b", "o1a", "x0a", "x1a", "o1b", "s", "x1b",
-    "i1a", "o1b", "o1b", "i0a", "x0b", "x0b", "o0a", "i0a", "x0a", "x1a", "x1b", "i1a", "x0a", "n", "x0a", "x1a",
-    "x1b", "x0b", "n", "i1a", "x1a", "x0a", "o1a", "x1b", "s", "o0a", "n", "x1a", "x0b", "x1b",
+    "g0", "o0", "i0", "g1", "o1", "a0", "i1", "b0", "i0", "a1", "i0", "o0", "i0a", "o1", "b1", "o1",
+    "o1a", "i1", "a2", "o1b", "o0", "o0a", "b2", "i0a", "pre", "o1a", "mixg", "i0a", "i1", "i1a", "o1b", "xg",
+    "x0", "o1a", "taps", "o0a", "i0a", "mid", "s", "o1b", "x1", "s", "x0", "i1a", "o1a", "x0", "x0a", "o0a",
+    "o1a", "x0b", "o1b", "i0a", "x1", "x1", "x1b", "i1a", "ng0", "o0a", "o1b", "o1a", "x0b", "s", "x0a", "ng1",
+    "x1b", "x1a", "i1a", "o0a", "x0b", "x0a", "o1b", "i0a", "x1b", "i1a", "o1b", "s", "x0a", "x1a", "x0b", "inp",
+    "o0a", "o1a", "s", "o1b", "x0a", "x1b", "o1a", "s", "x0b", "n", "i1a", "o1a", "i0a", "x1a", "i1a", "i1a",
+    "o0a", "x1a", "x0b", "x1a", "s", "o0a", "x1b", "x0a", "n", "x1a", "i0a", "x0b", "o0a", "s", "x0b", "x0a",
+    "i0a", "x1a", "x0a", "x1a", "o1b", "x1b", "i1a", "n", "x0b", "bo", "s", "x0a", "i1a", "n", "x1b", "x0a",
+    "x1b", "x1a", "n", "o1b", "s", "i0a", "x1b", "o1a", "x1a", "o0a", "n", "s", "x0b", "x1b",
 ]
 
 
@@ -244,6 +244,9 @@
 
 def carry_doubling(place, links, m, way):
     bits = log2(place.sizes["seq"])
+    inner = m.a2.shape[1]
+    for k in range(0, inner, SCAN):
+        (scan_lams if way else scan_ends)(m, slice(k, k + SCAN))
     m.edges[way] = jnp.zeros_like(m.edges[way])
     m.back[way] = jnp.ones_like(m.back[way])
     m.tot[0] = m.ends[way]
@@ -282,10 +285,17 @@
     def cut_sum(p):
         return m.sums.at[:, pl.ds(mult(p % across * width, LANES), width)]
 
-    first = [links.copy(cut(m.ends.at[way], p), m.got.at[s, way], (p, b)) for p in peers]
+    first = []
+    for k in range(across):
+        (scan_lams if way else scan_ends)(m, pl.ds(mult(lax.rem(s + k, across) * width, LANES), width))
+        for i in (k, k + across):
+            if i:
+                p = peers[i - 1]
+                first.append(links.copy(cut(m.ends.at[way], p), m.got.at[s, way], (p, b)))
+                if way == 0:
+                    first.append(links.copy(cut_sum(p), m.got_sum.at[s], (p, b)))
     m.got[s, way] = cut(m.ends.at[way], s)[...]
     if way == 0:
-        first += [links.copy(cut_sum(p), m.got_sum.at[s], (p, b)) for p in peers]
         m.got_sum[s] = cut_sum(s)[...]
     yield
     for c in first:
@@ -327,7 +337,7 @@
         at = pl.ds(pl.multiple_of(i * 8, 8), 8)
         s8, u8 = m.step[at, lanes], m.u[at, lanes]
         for j in range(8):
-            b = wide(m.bb[pl.ds(pl.multiple_of((i * 8 + j) * n, 8), n)])
+            b = wide(m.bb[pl.ds(pl.multiple_of((i * 8 + j) * n, 8), n)], a2.shape[1])
             h = jnp.exp2(spread(s8[j : j + 1], n) * a2) * h + spread(u8[j : j + 1], n) * b
         return h
 
@@ -343,7 +353,7 @@
         at = pl.ds(pl.multiple_of(i * 8, 8), 8)
         s8, d8 = m.step[at, lanes], m.d_res[at, lanes]
         for j in range(8):
-            c = wide(m.cc[pl.ds(pl.multiple_of((i * 8 + j) * n, 8), n)])
+            c = wide(m.cc[pl.ds(pl.multiple_of((i * 8 + j) * n, 8), n)], a2.shape[1])
             dec = dec * jnp.exp2(spread(s8[j : j + 1], n) * a2)
             acc = acc + dec * (spread(d8[j : j + 1], n) * c)
         return dec, acc
@@ -654,11 +664,12 @@
     to_row("gain", 3)
     x = m.x[...]
     rms = lax.rsqrt(jnp.mean(x * x, axis=1, keepdims=True) + EPSILON)
-    m.normed[...] = x * rms * m.vec[3:4, :width]
-    left = stacked(m.normed[...])
+    scaled = x * m.vec[3:4, :width]
+    m.normed[...] = scaled * rms
+    left = stacked(scaled)
 
     def hidden_block(i, w):
-        m.hid[pl.ds(8, tokens), pl.ds(mult(i * WBLOCK, WBLOCK), WBLOCK)] = rows_matmul(left, w, ((1,), (0,)))
+        m.hid[pl.ds(8, tokens), pl.ds(mult(i * WBLOCK, WBLOCK), WBLOCK)] = rms * rows_matmul(left, w, ((1,), (0,)))
 
     to_hidden(hidden_block)
     to_gate = stream(m, blocks_of_half, 2 * blocks_of_half)
@@ -730,8 +741,6 @@
     loop(blocks_of_half, step_block)
 
     blocks = [slice(k, k + SCAN) for k in range(0, inner, SCAN)]
-    for lanes in blocks:
-        scan_ends(m, lanes)
     ahead = carry(place, links, m, 0)
     next(ahead)
     g_left = stacked(m.g[...])
@@ -747,7 +756,7 @@
 
     def gate_block(i, w):
         cols = pl.ds(mult(i * WBLOCK, WBLOCK), WBLOCK)
-        z = rows_matmul(left, w, ((1,), (0,)))
+        z = rms * rows_matmul(left, w, ((1,), (0,)))
         sg = sigmoid(z)
         act = z * sg
         d = m.d_res[:, cols]
@@ -757,8 +766,6 @@
 
     to_gate(gate_block)
     next(ahead)
-    for lanes in blocks:
-        scan_lams(m, lanes)
     behind = carry(place, links, m, 1)
     next(behind)
     for _ in ahead:

time: 153 us -> 158 us (1.033)
  Pallas kernels: 152 us -> 157 us
    pallas_call x1, Pallas kernels: 145 us -> 151 us  [shards(): pl.pallas_call(functools.partial(block_kernel, sizes, list(sh)), in_specs...]
where the time goes in v7:
time: 158 us
  Pallas kernels  157 us (99%)
    pallas_call x1, Pallas kernels, shards(): pl.pallas_call(functools.partial(block_kernel, sizes, list(sh)), in_specs...  151 us
    pallas_call x1, Pallas kernels, shards(): pl.pallas_call(functools.partial(unpack_kernel, rank, n), in_specs=[VMEM]...  6.3 us

profile of v7, /device:TPU:1, one launch (start us, length us, event | category | flops | bytes accessed | tf_op | source)
XLA Modules:
  0.0 158.1 jit_solution(17617549328488028766)
XLA Ops:
  0.6 151.0 %block.1 = (f32[128,768]{1,0:T(8,128)S(1)}, f32[128,768]{1,0:T(8,128)S(1)}, f32[768,3072]{1,0:T(8,128)S(1)}, f32[1536,768]{1,0:T(8,128)S(1)}, f32[256,1024]{1,0:T(8,128)S(1)}, /*index=5*/f32[8,128]{1,0:T(8,128)S(1)}) custom-call(f32[128,768]{1,0:T(8,128)} %bitcast.18, f32[6,128]{1,0:T(8,128)} %bitcast.25, f32[128,768]{1,0:T(8,128)} %bitcast.19, ...), custom_call_target="tpu_custom_call" | custom-call | tf_op jit(solution)/shard_map/block/pallas_call | solution.py:1032
  151.6 6.3 %unpack.1 = (f32[128,768]{1,0:T(8,128)}, f32[128,768]{1,0:T(8,128)}, f32[768,3072]{1,0:T(8,128)}, f32[1536,768]{1,0:T(8,128)}, f32[80,1536]{1,0:T(8,128)}, /*ind...) custom-call(f32[128,768]{1,0:T(8,128)S(1)} %get-tuple-element.30.a_v, ...), custom_call_target="tpu_custom_call" | custom-call | tf_op jit(solution)/shard_map/unpack/pallas_call | solution.py:1043

commit v8 on v6

--- a/solution.py
+++ b/solution.py
@@ -18,19 +18,21 @@
 WBLOCK = 256
 SLOTS = 4
 SMALL = (256, 1024)
-PARTS = {"o1": 2, "x0": 2, "x1": 2}
-SPREAD = {"o0a": "T3", "o1a": "T3", "x0b": "T3"}
-SENDS = 64
+PARTS = {"o0": 2, "o1": 2, "i0": 2, "x0": 2, "x1": 2}
+SPREAD = {"o1a": "T3", "x0b": "T3", "x1b": "T3"}
+SENDS = 72
 ORDER = [
-    "g0", "i0", "o0", "g1", "a0", "o1", "i1", "b0", "i0", "a1", "o0", "i0", "i0a", "o0", "o0a", "b1",
-    "a2", "o1", "b2", "o1", "o1b", "i0a", "pre", "i1", "mixg", "o1a", "o1b", "i0a", "i1", "i1a", "xg", "o0a",
-    "x0", "taps", "o1b", "i0a", "mid", "s", "o1a", "x1", "ng0", "x0", "i1a", "s", "o1b", "x0", "x0b", "o1a",
-    "i0a", "x0a", "o0a", "x1", "ng1", "o1a", "s", "o1b", "i1a", "x1", "x1b", "bo", "s", "o1a", "x1a", "x0a",
-    "o0a", "i0a", "s", "x1b", "inp", "i1a", "o0a", "x0b", "s", "x1b", "x0a", "i1a", "o1b", "o1a", "s", "x1b",
-    "x0a", "o1a", "x1a", "o0a", "n", "i0a", "o1a", "x0b", "x0a", "o0a", "i0a", "s", "i1a", "n", "x1a", "x0b",
-    "x0b", "o0a", "x1a", "n", "o1b", "s", "x1a", "x1b", "i1a", "x0b", "o1a", "x0a", "x1a", "o1b", "s", "x1b",
-    "i1a", "o1b", "o1b", "i0a", "x0b", "x0b", "o0a", "i0a", "x0a", "x1a", "x1b", "i1a", "x0a", "n", "x0a", "x1a",
-    "x1b", "x0b", "n", "i1a", "x1a", "x0a", "o1a", "x1b", "s", "o0a", "n", "x1a", "x0b", "x1b",
+    "g0", "o0", "i0", "g1", "a0", "i1", "o1", "b0", "a1", "o0", "i0", "b1", "o0", "i0", "i0a", "o0b",
+    "a2", "o0a", "i0b", "o1", "b2", "pre", "mixg", "i1", "o1", "o1a", "o0b", "i1", "i1a", "o0a", "xg", "x1",
+    "i0b", "taps", "o0b", "o1a", "mid", "o0a", "s", "i0a", "x0", "i0b", "x1", "s", "i1a", "o0b", "x1", "o0a",
+    "x1a", "o1b", "i0b", "o0b", "x0", "i0a", "x1b", "o0a", "o1a", "x0", "x0b", "x1a", "i0b", "o0b", "x1b", "i0a",
+    "x0a", "s", "o1a", "i1a", "ng0", "o1b", "i0a", "o0a", "x1a", "o1a", "i0b", "x1b", "x0b", "i1a", "ng1", "x0a",
+    "i0a", "s", "x1b", "x0b", "o1a", "inp", "i1a", "x1a", "o0a", "o1b", "o0b", "n", "i0b", "bo", "x0a", "o1a",
+    "x1b", "i0a", "n", "x0b", "x1a", "o1b", "o1a", "i1a", "x0a", "s", "o1b", "x0b", "x1b", "n", "s", "x1b",
+    "i0a", "o0b", "i0b", "x0a", "x1a", "s", "x0b", "x1b", "o1b", "x0b", "i0a", "x0a", "o0b", "s", "i0b", "x1a",
+    "o0b", "x0b", "i1a", "o1b", "o0a", "n", "o1a", "x1a", "o0a", "i1a", "n", "x1b", "o1b", "s", "o1b", "i0b",
+    "x1a", "x0b", "o1a", "x0a", "i0a", "i1a", "n", "o1b", "o0a", "x0a", "s", "i1a", "x0b", "x0a", "s", "x1a",
+    "x1b", "x0a",
 ]
 
 
@@ -654,11 +656,12 @@
     to_row("gain", 3)
     x = m.x[...]
     rms = lax.rsqrt(jnp.mean(x * x, axis=1, keepdims=True) + EPSILON)
-    m.normed[...] = x * rms * m.vec[3:4, :width]
-    left = stacked(m.normed[...])
+    scaled = x * m.vec[3:4, :width]
+    m.normed[...] = scaled * rms
+    left = stacked(scaled)
 
     def hidden_block(i, w):
-        m.hid[pl.ds(8, tokens), pl.ds(mult(i * WBLOCK, WBLOCK), WBLOCK)] = rows_matmul(left, w, ((1,), (0,)))
+        m.hid[pl.ds(8, tokens), pl.ds(mult(i * WBLOCK, WBLOCK), WBLOCK)] = rms * rows_matmul(left, w, ((1,), (0,)))
 
     to_hidden(hidden_block)
     to_gate = stream(m, blocks_of_half, 2 * blocks_of_half)
@@ -747,7 +750,7 @@
 
     def gate_block(i, w):
         cols = pl.ds(mult(i * WBLOCK, WBLOCK), WBLOCK)
-        z = rows_matmul(left, w, ((1,), (0,)))
+        z = rms * rows_matmul(left, w, ((1,), (0,)))
         sg = sigmoid(z)
         act = z * sg
         d = m.d_res[:, cols]

time: 153 us -> 149 us (0.974)
  Pallas kernels: 152 us -> 148 us
    pallas_call x1, Pallas kernels: 145 us -> 141 us  [shards(): pl.pallas_call(functools.partial(block_kernel, sizes, list(sh)), in_specs...]
where the time goes in v8:
time: 149 us; the launch traced here: 148 us
  Pallas kernels  148 us (99%)
    pallas_call x1, Pallas kernels, shards(): pl.pallas_call(functools.partial(block_kernel, sizes, list(sh)), in_specs...  141 us
    pallas_call x1, Pallas kernels, shards(): pl.pallas_call(functools.partial(unpack_kernel, rank, n), in_specs=[VMEM]...  6.3 us

profile of v8, /device:TPU:1, one launch (start us, length us, event | category | flops | bytes accessed | tf_op | source)
XLA Modules:
  0.0 148.5 jit_solution(10470377618470250976)
XLA Ops:
  0.6 141.3 %block.1 = (f32[128,768]{1,0:T(8,128)S(1)}, f32[128,768]{1,0:T(8,128)S(1)}, f32[768,3072]{1,0:T(8,128)S(1)}, f32[1536,768]{1,0:T(8,128)S(1)}, f32[256,1024]{1,0:T(8,128)S(1)}, /*index=5*/f32[8,128]{1,0:T(8,128)S(1)}) custom-call(f32[128,768]{1,0:T(8,128)} %bitcast.18, f32[6,128]{1,0:T(8,128)} %bitcast.25, f32[128,768]{1,0:T(8,128)} %bitcast.19, ...), custom_call_target="tpu_custom_call" | custom-call | tf_op jit(solution)/shard_map/block/pallas_call | solution.py:1028
  142.0 6.3 %unpack.1 = (f32[128,768]{1,0:T(8,128)}, f32[128,768]{1,0:T(8,128)}, f32[768,3072]{1,0:T(8,128)}, f32[1536,768]{1,0:T(8,128)}, f32[80,1536]{1,0:T(8,128)}, /*ind...) custom-call(f32[128,768]{1,0:T(8,128)S(1)} %get-tuple-element.30.a_v, ...), custom_call_target="tpu_custom_call" | custom-call | tf_op jit(solution)/shard_map/unpack/pallas_call | solution.py:1039

commit v9 on v8

--- a/solution.py
+++ b/solution.py
@@ -110,9 +110,12 @@
     def __init__(self, send, recv):
         self.send, self.recv, self.used, self.made, self.free, self.open = send, recv, 0, 0, [], []
 
-    def copy(self, src, dst, to, start=True):
-        i = self.used
+    def group(self):
         self.used += 1
+        return self.used - 1
+
+    def copy(self, src, dst, to, start=True, group=None):
+        i = self.group() if group is None else group
         if self.free:
             k = self.free.pop()
         else:
@@ -126,6 +129,9 @@
             c.start()
             self.open.append((c, k))
         return c
+
+    def take(self, like, group):
+        pltpu.make_async_copy(like, like, self.recv.at[group]).wait()
 
     def sent(self, *copies):
         for copy in copies:
@@ -284,15 +290,17 @@
     def cut_sum(p):
         return m.sums.at[:, pl.ds(mult(p % across * width, LANES), width)]
 
-    first = [links.copy(cut(m.ends.at[way], p), m.got.at[s, way], (p, b)) for p in peers]
+    one, two, three = links.group(), links.group(), links.group()
+    others = pl.ds(0, count - 1)
+    first = [links.copy(cut(m.ends.at[way], p), m.got.at[s, way], (p, b), group=one) for p in peers]
     m.got[s, way] = cut(m.ends.at[way], s)[...]
     if way == 0:
-        first += [links.copy(cut_sum(p), m.got_sum.at[s], (p, b)) for p in peers]
+        first += [links.copy(cut_sum(p), m.got_sum.at[s], (p, b), group=three) for p in peers]
         m.got_sum[s] = cut_sum(s)[...]
     yield
-    for c in first:
-        c.wait_recv()
+    links.take(m.got.at[others, way], one)
     if way == 0:
+        links.take(m.got_sum.at[others], three)
         a2 = cut(m.a2, s)[...]
         for p in range(count):
             m.tile_dec[p] = jnp.exp2(a2 * m.got_sum[p])
@@ -300,12 +308,11 @@
     for p in reversed(range(count)) if way else range(count):
         m.back[p, way] = value
         value = m.got[p, way] + m.tile_dec[p] * value
-    second = [links.copy(m.back.at[p, way], cut(m.edges.at[way], s), (p, b)) for p in peers]
+    second = [links.copy(m.back.at[p, way], cut(m.edges.at[way], s), (p, b), group=two) for p in peers]
     cut(m.edges.at[way], s)[...] = m.back[s, way]
     links.sent(*first)
     yield
-    for c in second:
-        c.wait_recv()
+    links.take(m.back.at[others, way], two)
     links.sent(*second)
 
 
@@ -441,12 +448,11 @@
 
 def recvs(sizes):
     bits, count = log2(sizes["seq"]), sizes["seq"]
-    total = 6 + 2 + 3 * len(UNITS) + (5 * (count - 1) if tiled(count) else 2 * bits)
+    total = 2 + 2 + 2 * len(UNITS) + (6 if tiled(count) else 2 * bits)
     total += 2 * len(small_plan(sizes)) + sum(halvings(SMALL[0], len(small_plan(sizes))))
     for unit in UNITS:
         for p in parts(unit):
-            kept = sum(halvings(LANES * 3 // len(parts(unit)), bits)) - 1
-            total += bits + 7 + kept + 3 * {"T1": 0, "T2": kept, "T3": kept - 1}[SPREAD.get(p, "T1")]
+            total += bits + 4 + sum(halvings(LANES * 3 // len(parts(unit)), bits)) - 1
     return total
 
 
@@ -515,13 +521,14 @@
     mine = place.y if unit[0] == "o" else place.x
     to, _ = place.near(0, 1, 0) if unit[0] == "o" else place.near(1, 0, 0)
     core, _ = place.near(0, 0, 1)
+    both = links.group()
 
     def cut(which):
         return value.at[:, pl.ds(mult(which * 2 * width + shift, LANES), width)]
 
     def pass_on(which):
         slot = late.at[which * 2 + place.c]
-        return links.copy(slot, slot, core)
+        return links.copy(slot, slot, core, group=both)
 
     sent = links.copy(cut(1 - mine), late.at[mine * 2 + place.c], to)
     late[mine * 2 + place.c] = cut(mine)[...]
@@ -530,8 +537,7 @@
     sent.wait_recv()
     passed.append(pass_on(1 - mine))
     yield
-    for copy in passed:
-        copy.wait_recv()
+    links.take(late.at[pl.ds(0, 2)], both)
     links.sent(sent, *passed)
     for i in range(2):
         cell = matmul(left(i), right(i), ((0,), (0,)))
@@ -565,11 +571,11 @@
     edge = kept[0][2]
     place_rows(acc, off, count, lambda row, n: region((x, y), row - edge, n))
     row = off - edge
-    held, across = [(x, y)], []
-
-    def give(at, to):
+    held, across, to_core = [(x, y)], [], links.group()
+
+    def give(at, to, group=None):
         ref = region(at, row, count)
-        return links.copy(ref, ref, to)
+        return links.copy(ref, ref, to, group=group)
 
     steps = list(reversed(kept[1:]))
     kind = SPREAD.get(p, "T1")
@@ -578,10 +584,10 @@
         last = i == len(steps) - 1
         if step is not None:
             to, parent, _, size = step
-            copies = [give(at, to) for at in held]
+            step_copies = links.group()
+            copies = [give(at, to, step_copies) for at in held]
             yield
-            for copy in copies:
-                copy.wait_recv()
+            links.take(out.at[pl.ds(0, len(held) * count), pl.ds(0, cols)], step_copies)
             links.sent(*copies)
             row, count = parent - edge, 2 * size
             continue
@@ -593,7 +599,7 @@
 
         def onward(at):
             if last:
-                across.append(give(at, core))
+                across.append(give(at, core, to_core))
 
         onward((x, y))
         yield
@@ -608,10 +614,9 @@
         links.sent(a, b)
         onward(at_d)
     if not across:
-        across = [give(at, core) for at in held]
+        across = [give(at, core, to_core) for at in held]
     yield
-    for copy in across:
-        copy.wait_recv()
+    links.take(out.at[pl.ds(0, 2 * rows), pl.ds(0, cols)], to_core)
 
 
 def block_kernel(sizes, names, *refs):
@@ -673,14 +678,14 @@
         halo.start()
 
     fetched["g"].wait()
-    early = []
+    early, early_n, early_g = [], links.group(), links.group()
     for d in GROUP:
         to, _ = place.near(*d)
         cols = pl.ds(mult((c + d[2] * (1 - 2 * c)) * part, LANES), part)
         if not d[1]:
-            early.append(links.copy(m.normed.at[:, cols], m.ng.at[place.x * 2 + c], to))
+            early.append(links.copy(m.normed.at[:, cols], m.ng.at[place.x * 2 + c], to, group=early_n))
         if not d[0]:
-            early.append(links.copy(m.g.at[:, cols], m.gg.at[place.y * 2 + c], to))
+            early.append(links.copy(m.g.at[:, cols], m.gg.at[place.y * 2 + c], to, group=early_g))
     own = pl.ds(mult(c * part, LANES), part)
     m.ng[place.x * 2 + c] = m.normed[:, own]
     m.gg[place.y * 2 + c] = m.g[:, own]
@@ -834,8 +839,8 @@
         if k == 0:
             for _ in behind:
                 pass
-            for e in early:
-                e.wait_recv()
+            links.take(m.ng.at[pl.ds(0, 3)], early_n)
+            links.take(m.gg.at[pl.ds(0, 3)], early_g)
             links.sent(*early)
         scan_back(m, blocks[k], k == 0)
 

time: 149 us -> 148 us (level)
  no operation moved by 1% of the time
where the time goes in v9:
time: 148 us
  Pallas kernels  147 us (99%)
    pallas_call x1, Pallas kernels, shards(): pl.pallas_call(functools.partial(block_kernel, sizes, list(sh)), in_specs...  141 us
    pallas_call x1, Pallas kernels, shards(): pl.pallas_call(functools.partial(unpack_kernel, rank, n), in_specs=[VMEM]...  6.3 us

profile of v9, /device:TPU:1, one launch (start us, length us, event | category | flops | bytes accessed | tf_op | source)
XLA Modules:
  0.0 147.7 jit_solution(15510400635002799463)
XLA Ops:
  0.6 140.6 %block.1 = (f32[128,768]{1,0:T(8,128)S(1)}, f32[128,768]{1,0:T(8,128)S(1)}, f32[768,3072]{1,0:T(8,128)S(1)}, f32[1536,768]{1,0:T(8,128)S(1)}, f32[256,1024]{1,0:T(8,128)S(1)}, /*index=5*/f32[8,128]{1,0:T(8,128)S(1)}) custom-call(f32[128,768]{1,0:T(8,128)} %bitcast.18, f32[6,128]{1,0:T(8,128)} %bitcast.25, f32[128,768]{1,0:T(8,128)} %bitcast.19, ...), custom_call_target="tpu_custom_call" | custom-call | tf_op jit(solution)/shard_map/block/pallas_call | solution.py:1033
  141.2 6.3 %unpack.1 = (f32[128,768]{1,0:T(8,128)}, f32[128,768]{1,0:T(8,128)}, f32[768,3072]{1,0:T(8,128)}, f32[1536,768]{1,0:T(8,128)}, f32[80,1536]{1,0:T(8,128)}, /*ind...) custom-call(f32[128,768]{1,0:T(8,128)S(1)} %get-tuple-element.30.a_v, ...), custom_call_target="tpu_custom_call" | custom-call | tf_op jit(solution)/shard_map/unpack/pallas_call | solution.py:1044

commit v10 on v9

--- a/solution.py
+++ b/solution.py
@@ -18,21 +18,21 @@
 WBLOCK = 256
 SLOTS = 4
 SMALL = (256, 1024)
-PARTS = {"o0": 2, "o1": 2, "i0": 2, "x0": 2, "x1": 2}
-SPREAD = {"o1a": "T3", "x0b": "T3", "x1b": "T3"}
+PARTS = {"o0": 2, "i0": 2, "i1": 2, "x0": 2, "x1": 2}
+SPREAD = {"i0a": "T3", "x0b": "T3", "x1b": "T2"}
 SENDS = 72
 ORDER = [
-    "g0", "o0", "i0", "g1", "a0", "i1", "o1", "b0", "a1", "o0", "i0", "b1", "o0", "i0", "i0a", "o0b",
-    "a2", "o0a", "i0b", "o1", "b2", "pre", "mixg", "i1", "o1", "o1a", "o0b", "i1", "i1a", "o0a", "xg", "x1",
-    "i0b", "taps", "o0b", "o1a", "mid", "o0a", "s", "i0a", "x0", "i0b", "x1", "s", "i1a", "o0b", "x1", "o0a",
-    "x1a", "o1b", "i0b", "o0b", "x0", "i0a", "x1b", "o0a", "o1a", "x0", "x0b", "x1a", "i0b", "o0b", "x1b", "i0a",
-    "x0a", "s", "o1a", "i1a", "ng0", "o1b", "i0a", "o0a", "x1a", "o1a", "i0b", "x1b", "x0b", "i1a", "ng1", "x0a",
-    "i0a", "s", "x1b", "x0b", "o1a", "inp", "i1a", "x1a", "o0a", "o1b", "o0b", "n", "i0b", "bo", "x0a", "o1a",
-    "x1b", "i0a", "n", "x0b", "x1a", "o1b", "o1a", "i1a", "x0a", "s", "o1b", "x0b", "x1b", "n", "s", "x1b",
-    "i0a", "o0b", "i0b", "x0a", "x1a", "s", "x0b", "x1b", "o1b", "x0b", "i0a", "x0a", "o0b", "s", "i0b", "x1a",
-    "o0b", "x0b", "i1a", "o1b", "o0a", "n", "o1a", "x1a", "o0a", "i1a", "n", "x1b", "o1b", "s", "o1b", "i0b",
-    "x1a", "x0b", "o1a", "x0a", "i0a", "i1a", "n", "o1b", "o0a", "x0a", "s", "i1a", "x0b", "x0a", "s", "x1a",
-    "x1b", "x0a",
+    "g0", "o0", "i0", "g1", "a0", "i1", "o1", "b0", "a1", "i0", "o0", "b1", "i0", "i0b", "o0", "a2",
+    "o0b", "i0a", "o1", "b2", "o1", "i1", "o1a", "i0b", "pre", "i0a", "mixg", "o0b", "i1", "o0a", "i1a", "i0b",
+    "taps", "o1a", "xg", "x0", "i0a", "i1b", "mid", "s", "o0b", "i0b", "i1a", "ng0", "s", "i0a", "x0", "o0a",
+    "o0b", "o1a", "x0", "x0b", "i0b", "x1", "s", "i1a", "i0a", "o0b", "x0a", "o0a", "i1b", "i0b", "o1a", "x0b",
+    "ng1", "i1a", "x1", "o0b", "s", "x1", "x0b", "o1a", "x1b", "i1a", "inp", "i0a", "s", "x1a", "x0b", "i0b",
+    "x1b", "o0a", "i1b", "i1a", "i0a", "s", "o1a", "x0a", "x1a", "x1b", "i1b", "s", "x0a", "o0a", "x1b", "i0a",
+    "i1a", "x1a", "o0b", "x0a", "s", "i1b", "x1b", "o1a", "o0a", "x1b", "x1a", "x0b", "x1b", "s", "o0b", "x0b",
+    "i0b", "x1a", "o0a", "o0a", "x0a", "i1a", "n", "n", "o0b", "x1b", "i0a", "i1b", "o1a", "x0a", "n", "bo",
+    "x0b", "o1a", "s", "x1a", "o0a", "x0b", "o0a", "x1b", "i1a", "i1b", "n", "x0a", "i1a", "i1b", "x0a", "s",
+    "x1a", "x1a", "n", "i0b", "x1b", "i1b", "x0b", "o1a", "o0b", "x0a", "n", "i1b", "i0a", "x1a", "i0b", "x0b",
+    "x0a", "x1a",
 ]
 
 

time: 148 us -> 148 us (level)
  no operation moved by 1% of the time
where the time goes in v10:
time: 148 us
  Pallas kernels  147 us (99%)
    pallas_call x1, Pallas kernels, shards(): pl.pallas_call(functools.partial(block_kernel, sizes, list(sh)), in_specs...  141 us
    pallas_call x1, Pallas kernels, shards(): pl.pallas_call(functools.partial(unpack_kernel, rank, n), in_specs=[VMEM]...  6.3 us

profile of v10, /device:TPU:1, one launch (start us, length us, event | category | flops | bytes accessed | tf_op | source)
XLA Modules:
  0.0 147.9 jit_solution(16793224630150177499)
XLA Ops:
  0.6 140.8 %block.1 = (f32[128,768]{1,0:T(8,128)S(1)}, f32[128,768]{1,0:T(8,128)S(1)}, f32[768,3072]{1,0:T(8,128)S(1)}, f32[1536,768]{1,0:T(8,128)S(1)}, f32[256,1024]{1,0:T(8,128)S(1)}, /*index=5*/f32[8,128]{1,0:T(8,128)S(1)}) custom-call(f32[128,768]{1,0:T(8,128)} %bitcast.18, f32[6,128]{1,0:T(8,128)} %bitcast.25, f32[128,768]{1,0:T(8,128)} %bitcast.19, ...), custom_call_target="tpu_custom_call" | custom-call | tf_op jit(solution)/shard_map/block/pallas_call | solution.py:1033
  141.4 6.3 %unpack.1 = (f32[128,768]{1,0:T(8,128)}, f32[128,768]{1,0:T(8,128)}, f32[768,3072]{1,0:T(8,128)}, f32[1536,768]{1,0:T(8,128)}, f32[80,1536]{1,0:T(8,128)}, /*ind...) custom-call(f32[128,768]{1,0:T(8,128)S(1)} %get-tuple-element.30.a_v, ...), custom_call_target="tpu_custom_call" | custom-call | tf_op jit(solution)/shard_map/unpack/pallas_call | solution.py:1044
